TPU v7x, 128 devices: a whole 4x4x4 slice. The times are simulated.
128 devices in a mesh: prow: 16 (over x, z), pcol: 8 (over y, core).
Axes of the slice: x: 4, y: 4, z: 4, core: 2. Of those that a mesh axis runs over, the one named last changes fastest.
Arguments:
- rhs: float32 [31, 64, 2048], P(None, None, 'prow'), may hold values from -6 to 6
- factor: bfloat16 [98, 2048, 2048], P(None, 'prow', 'pcol'), may hold values from -0.03125 to 0.03125
- inverse: bfloat16 [31, 2048, 2048], P(None, 'pcol', 'prow')
- pattern: int32 [98], replicated, may hold values 0 or 1
Outputs:
- solution: float32 [31, 64, 2048], P(None, None, 'prow')
- forward_solution: float32 [31, 64, 2048], P(None, None, 'pcol')
All inputs are finite; a program needn't handle non-finite values.
Results may differ from a plain program's by a relative error of at most 0.011.
Values sent between devices are 32-bit elements; how exact they have to be, the bound alone decides.
No kernel may reach another device: no remote copies, remote signals or barrier semaphores. Data moves between devices by JAX's collectives and lax.ppermute only.
A program may use at most 64 MiB of HBM per device.

v0:
```python
import jax
import jax.numpy as jnp
from jax import lax
from jax.experimental import pallas as pl
from jax.experimental.pallas import tpu as pltpu
from jax.sharding import PartitionSpec as P

LEV = 5
ROWS = 16
TOP = 3
TWIN = [(i, i ^ 1) for i in range(8)]
YRING = [[(i, (i + 2 * k) % 8) for i in range(8)] for k in (2, 1, 3)]
YGROUPS = [[0, 2, 4, 6], [1, 3, 5, 7]]
XRING = [[(i, (i + 4 * k) % 16) for i in range(16)] for k in (2, 1, 3)]
ZGROUPS = [[4 * x + z for z in range(4)] for x in range(4)]


def block_start(tree_depth):
    return (tree_depth - 2) * 2**tree_depth + 2


def blocks_of(array, tree_depth, upward):
    start = block_start(tree_depth)
    count = 2**tree_depth
    return array[start + upward - 1 : start + count * tree_depth : tree_depth]


def nodes_of(array, tree_depth):
    return array[2**tree_depth - 1 : 2 ** (tree_depth + 1) - 1]


def product(left, right, form):
    return jnp.einsum(form, left, right, preferred_element_type=jnp.float32)


def sum_ring(values, axis, ring):
    across, right, left = [lax.ppermute(values, axis, step) for step in ring]
    return (values + across) + (right + left)


def sum_y_ring(values):
    if values.size <= 32768:
        return sum_ring(values, "pcol", YRING)
    copies = jnp.broadcast_to(values[None], (4,) + values.shape)
    parts = lax.all_to_all(copies, "pcol", 0, 0, axis_index_groups=YGROUPS)
    return parts.sum(axis=0)


def sum_columns(values):
    shape = values.shape
    flat = values.reshape(-1, shape[-1])
    if flat.size <= 16384:
        flat = flat + lax.ppermute(flat, "pcol", TWIN)
        return sum_y_ring(flat).reshape(shape)
    halves = flat.reshape(2, -1, shape[-1])
    core = lax.axis_index("pcol") % 2
    mine = lax.dynamic_index_in_dim(halves, core, 0, keepdims=False)
    other = lax.dynamic_index_in_dim(halves, 1 - core, 0, keepdims=False)
    mine = mine + lax.ppermute(other, "pcol", TWIN)
    mine = sum_y_ring(mine)
    other = lax.ppermute(mine, "pcol", TWIN)
    both = jnp.where(core == 0, jnp.stack([mine, other]), jnp.stack([other, mine]))
    return both.reshape(shape)


def sum_x_ring(values):
    shape = values.shape
    return sum_ring(values.reshape(-1, shape[-1]), "prow", XRING).reshape(shape)


def scatter_rows(values):
    chunks = values.reshape(ROWS, -1, values.shape[-1])
    return lax.all_to_all(chunks, "prow", 0, 0).sum(axis=0)


def share_rows(part, shape):
    copies = jnp.broadcast_to(part[None], (ROWS,) + part.shape)
    return lax.all_to_all(copies, "prow", 0, 0).reshape(shape)


def sum_rows(values):
    return share_rows(scatter_rows(values), values.shape)


def round_inverses(whole, count):
    def kernel(blocks, out):
        for i in range(count):
            for z in range(4):
                out[i, :, 128 * z : 128 * z + 128] = blocks[z, i].astype(jnp.bfloat16)

    return pl.pallas_call(
        kernel,
        out_shape=jax.ShapeDtypeStruct((count, 256, 512), jnp.bfloat16),
        grid=(1,),
        in_specs=[pl.BlockSpec((4, count, 256, 128), lambda i: (0, 0, 0, 0))],
        out_specs=pl.BlockSpec((count, 256, 512), lambda i: (0, 0, 0)),
    )(whole)


def round_factors(whole, weights, first):
    count = whole.shape[1] - first

    def kernel(weights, blocks, out):
        weight = weights[pl.program_id(0)]
        for z in range(4):
            for h in range(2):
                values = blocks[z, 0, 128 * h : 128 * h + 128, :] * weight
                rows = slice(128 * z, 128 * z + 128)
                out[0, rows, 128 * h : 128 * h + 128] = values.astype(jnp.bfloat16)

    return pl.pallas_call(
        kernel,
        out_shape=jax.ShapeDtypeStruct((count, 512, 256), jnp.bfloat16),
        grid=(count,),
        in_specs=[
            pl.BlockSpec(memory_space=pltpu.SMEM),
            pl.BlockSpec((4, 1, 256, 128), lambda i: (0, i + first, 0, 0)),
        ],
        out_specs=pl.BlockSpec((1, 512, 256), lambda i: (i, 0, 0)),
    )(weights, whole)


def gather_blocks(inverses, factors, after):
    halves = factors.reshape(-1, 128, 2, 128).transpose(0, 2, 1, 3).reshape(-1, 256, 128)
    own = jnp.concatenate([inverses, halves]).astype(jnp.float32)
    own, after = lax.optimization_barrier((own, after))
    whole = lax.all_gather(own, "prow", axis_index_groups=ZGROUPS)
    return whole, after


def call(kernel, shapes, *operands):
    outs = [jax.ShapeDtypeStruct(shape, jnp.float32) for shape in shapes]
    return pl.pallas_call(kernel, out_shape=outs)(*operands)


def dot(left, right, contract):
    dims = (((1,), (contract,)), ((), ()))
    return lax.dot_general(left, right, dims, preferred_element_type=jnp.float32)


def enter_split(order, total, inverses, sums_1, sums_0, here):
    def kernel(here, order, total, inverses, sums_1, sums_0, out):
        for n in range(4):
            rounded = (order[3 + n] - total[n]).astype(jnp.bfloat16)
            piece = dot(rounded, inverses[n], 1)
            for z in range(4):
                out[z, :, 256 * n : 256 * n + 256] = piece[16 * z : 16 * z + 16]
        for i, value in enumerate((sums_1[0], sums_1[1], sums_0[0])):
            value = value - order[(i + 1) % 3] * here[0]
            for z in range(4):
                out[z, :, 1024 + 128 * i : 1152 + 128 * i] = value[16 * z : 16 * z + 16]

    specs = [pl.BlockSpec(memory_space=pltpu.SMEM)] + [pl.BlockSpec(memory_space=pltpu.VMEM)] * 5
    return pl.pallas_call(
        kernel,
        out_shape=jax.ShapeDtypeStruct((4, 16, 1408), jnp.float32),
        in_specs=specs,
    )(here.reshape(1), order, total, inverses, sums_1, sums_0)


def entered_split(got):
    def kernel(got, pieces, sums_1, sums_0):
        for n in range(4):
            at = slice(256 * n, 256 * n + 256)
            pieces[n] = (got[0, :, at] + got[1, :, at]) + (got[2, :, at] + got[3, :, at])
        for i, out in enumerate((sums_1.at[0], sums_1.at[1], sums_0.at[0])):
            for z in range(4):
                out[:, 128 * z : 128 * z + 128] = got[z, :, 1024 + 128 * i : 1152 + 128 * i]

    return call(kernel, [(4, 16, 256), (2, 16, 512), (1, 16, 512)], got)


def leave_split(target, forward_2, forward_1, forward_0, solution_1, solution_0):
    def kernel(target, forward_2, forward_1, forward_0, solution_1, solution_0, out):
        lane = 0
        for part in (target, forward_2, forward_1, forward_0):
            for n in range(part.shape[0]):
                for z in range(4):
                    out[z, :, lane : lane + 256] = part[n]
                lane += 256
        for part in (solution_0, solution_1):
            for n in range(part.shape[0]):
                for z in range(4):
                    out[z, :, lane : lane + 128] = part[n, :, 128 * z : 128 * z + 128]
                lane += 128

    operands = (target, forward_2, forward_1, forward_0, solution_1, solution_0)
    return call(kernel, [(4, 16, 3200)], *operands)[0]


def left_split(got, inverses):
    def kernel(got, inverses, pieces, forward, solved):
        for n in range(4):
            rounded = got[:, 256 * n : 256 * n + 256].astype(jnp.bfloat16)
            pieces[n] = dot(rounded, inverses[n], 0)
            forward[3 + n] = got[:, 1024 + 256 * n : 1280 + 256 * n]
        for n in range(2):
            forward[1 + n] = got[:, 2048 + 256 * n : 2304 + 256 * n]
        forward[0] = got[:, 2560:2816]
        for n in range(3):
            solved[n] = got[:, 2816 + 128 * n : 2944 + 128 * n]

    shapes = [(4, 64, 128), (7, 64, 256), (3, 64, 128)]
    return call(kernel, shapes, got.reshape(64, 3200), inverses)


def per_device(rhs, factor, inverse, pattern):
    live = pattern.astype(jnp.float32)
    bf16 = jnp.bfloat16
    forward_levels = [None] * LEV
    partial_value = [[] for _ in range(LEV)]

    def push_up(narrow, tree_depth, factors, weights, values):
        count = 2**tree_depth
        for upward in range(1, tree_depth + 1):
            blocks = factors[upward - 1 :: tree_depth]
            terms = product(narrow, blocks, "nrc,nwc->nrw")
            if weights is not None:
                terms = terms * weights[upward - 1 :: tree_depth][:, None, None]
            groups = count >> upward
            terms = terms.reshape((groups, 2**upward) + terms.shape[1:]).sum(axis=1)
            values[tree_depth - upward].append(terms)

    def own_blocks(array, tree_depth):
        start = block_start(tree_depth)
        return array[start : start + 2**tree_depth * tree_depth]

    for tree_depth in range(LEV - 1, TOP - 1, -1):
        residual = nodes_of(rhs, tree_depth)
        if tree_depth < LEV - 1:
            residual = residual - sum_columns(sum(partial_value[tree_depth]))
        pieces = product(residual.astype(bf16), nodes_of(inverse, tree_depth), "nrc,nwc->nrw")
        part = scatter_rows(pieces)
        if tree_depth == LEV - 1:
            whole, part = gather_blocks(inverse[0:3], factor[0:10], part)
        forward = share_rows(part, pieces.shape)
        forward_levels[tree_depth] = forward
        push_up(
            forward.astype(bf16),
            tree_depth,
            own_blocks(factor, tree_depth),
            own_blocks(live, tree_depth),
            partial_value,
        )

    here = (lax.axis_index("pcol") == 0).astype(jnp.float32)
    total = sum_columns(sum(partial_value[2]))
    sent = enter_split(
        rhs[0:7], total, inverse[3:7], sum(partial_value[1]), sum(partial_value[0]), here
    )
    got = lax.all_to_all(sent, "prow", 0, 0, axis_index_groups=ZGROUPS)
    pieces, sums_1, sums_0 = entered_split(got)
    pieces, whole = lax.optimization_barrier((pieces, whole))
    top_inverses = round_inverses(whole, 3)
    top_factors = round_factors(whole, live[0:10], 3)
    top_forward = [None] * TOP
    top_forward[2] = sum_x_ring(pieces)
    top_partial = [[sums_0], [sums_1]]
    inverse_at = [top_inverses[0:1], top_inverses[1:3]]
    factor_at = [None, top_factors[0:2], top_factors[2:10]]
    push_up(top_forward[2].astype(bf16), 2, factor_at[2], None, top_partial)
    for tree_depth in (1, 0):
        residual = -sum_columns(sum(top_partial[tree_depth]))
        pieces = product(residual.astype(bf16), inverse_at[tree_depth], "nrc,nwc->nrw")
        top_forward[tree_depth] = sum_x_ring(pieces)
        if tree_depth:
            push_up(top_forward[1].astype(bf16), 1, factor_at[1], None, top_partial)

    top_solved = []
    for tree_depth in range(TOP):
        target = top_forward[tree_depth]
        if tree_depth:
            terms = 0.0
            for upward in range(tree_depth, 0, -1):
                above = jnp.repeat(
                    top_solved[tree_depth - upward].astype(bf16), 2**upward, axis=0
                )
                blocks = factor_at[tree_depth][upward - 1 :: tree_depth]
                terms = terms + product(above, blocks, "nrw,nwc->nrc")
            target = target - sum_x_ring(terms)
        if tree_depth < TOP - 1:
            pieces = product(target.astype(bf16), inverse_at[tree_depth], "nrw,nwc->nrc")
            top_solved.append(sum_columns(pieces))

    sent = leave_split(target, *top_forward[::-1], top_solved[1], top_solved[0])
    got = lax.all_to_all(sent, "prow", 0, 0, axis_index_groups=ZGROUPS)
    pieces, top_forward, top_solved = left_split(got, inverse[3:7])

    gathered = [[] for _ in range(LEV)]

    def push_down(narrow, tree_depth):
        for lower in range(max(tree_depth + 1, TOP), LEV):
            upward = lower - tree_depth
            above = jnp.repeat(narrow, 2**upward, axis=0)
            terms = product(above, blocks_of(factor, lower, upward), "nrw,nwc->nrc")
            gathered[lower].append(terms * blocks_of(live, lower, upward)[:, None, None])

    for tree_depth in (0, 1):
        push_down(nodes_of(top_solved, tree_depth).astype(bf16), tree_depth)
    solved = [top_solved]
    for tree_depth in range(TOP - 1, LEV):
        if tree_depth >= TOP:
            target = forward_levels[tree_depth] - sum_rows(sum(gathered[tree_depth]))
            pieces = product(target.astype(bf16), nodes_of(inverse, tree_depth), "nrw,nwc->nrc")
        solution = sum_columns(pieces)
        solved.append(solution)
        push_down(solution.astype(bf16), tree_depth)
    forward_levels = [top_forward] + forward_levels[TOP:]
    return (jnp.concatenate(solved, axis=0), jnp.concatenate(forward_levels, axis=0))


def solution(mesh):
    in_specs = (P(None, None, "prow"), P(None, "prow", "pcol"), P(None, "pcol", "prow"), P())
    out_specs = (P(None, None, "prow"), P(None, None, "pcol"))
    return jax.shard_map(
        per_device, mesh=mesh, in_specs=in_specs, out_specs=out_specs, check_vma=False
    )
```

profile of v0, /device:TPU:1, one launch (start us, length us, event | category | flops | bytes accessed | tf_op | source)
XLA Modules:
  0.0 391.1 jit_solution(18198561641053516856)
XLA Ops:
  7.2 2.9 fusion.26
  10.0 8.6 %all-to-all-start = ((f32[16,64,256]{2,1,0:T(8,128)}), f32[16,64,256]{2,1,0:T(8,128)S(1)}, u32[]{:S(2)}, u32[]{:S(2)}) async-start(f32[16,64,256]{2,1,0:T(8,128)} %fusion.26), calls=%async_computation | async-start | bytes 2097152 | tf_op jit(solution)/shard_map/all_to_all | solution.py:73
  21.2 12.9 %all-to-all-done = f32[16,64,256]{2,1,0:T(8,128)S(1)} async-done(((f32[16,64,256]{2,1,0:T(8,128)}), f32[16,64,256]{2,1,0:T(8,128)S(1)}, u32[]{:S(2)}, u32[]{:S(2)}) %all-to-all-start) | async-done | bytes 1048608 | tf_op jit(solution)/shard_map/all_to_all | solution.py:73
  35.3 4.0 %all-to-all-start.1 = ((f32[16,64,256]{2,1,0:T(8,128)}), f32[16,64,256]{2,1,0:T(8,128)S(1)}, u32[]{:S(2)}, u32[]{:S(2)}) async-start(f32[16,64,256]{2,1,0:T(8,128)} %broadcast_in_dim.22), calls=%async_computation.1 | async-start | bytes 2097152 | tf_op jit(solution)/shard_map/all_to_all | solution.py:78
  39.3 4.8 %slice.160 = bf16[64,128,256]{2,1,0:T(8,128)(2,1)} slice(bf16[98,128,256]{2,1,0:T(8,128)(2,1)} %param.5), slice={[34:98], [0:128], [0:256]} | slice | bytes 8388608 | tf_op jit(solution)/shard_map/slice | solution.py:226
  44.2 9.4 %all-to-all-done.1 = f32[16,64,256]{2,1,0:T(8,128)S(1)} async-done(((f32[16,64,256]{2,1,0:T(8,128)}), f32[16,64,256]{2,1,0:T(8,128)S(1)}, u32[]{:S(2)}, u32[]{:S(2)}) %all-to-all-start.1) | async-done | bytes 1048608 | tf_op jit(solution)/shard_map/all_to_all | solution.py:78
  54.5 1.9 bitcast_reduce_fusion.1
  57.1 3.7 collective-permute-start
  68.3 3.8 collective-permute-done.1
  74.4 2.1 fusion.45
  76.5 4.9 %all-to-all-start.2 = ((f32[16,32,256]{2,1,0:T(8,128)}), f32[16,32,256]{2,1,0:T(8,128)}, u32[]{:S(2)}, u32[]{:S(2)}) async-start(f32[16,32,256]{2,1,0:T(8,128)} %bitcast.149), calls=%async_computation.2 | async-start | bytes 1048576 | tf_op jit(solution)/shard_map/all_to_all | solution.py:73
  83.2 2.8 slice.168
  87.2 4.6 %all-to-all-done.2 = f32[16,32,256]{2,1,0:T(8,128)} async-done(((f32[16,32,256]{2,1,0:T(8,128)}), f32[16,32,256]{2,1,0:T(8,128)}, u32[]{:S(2)}, u32[]{:S(2)}) %all-to-all-start.2) | async-done | bytes 524320 | tf_op jit(solution)/shard_map/all_to_all | solution.py:73
  93.7 5.4 %all-to-all-start.3 = ((f32[16,32,256]{2,1,0:T(8,128)}), f32[16,32,256]{2,1,0:T(8,128)S(1)}, u32[]{:S(2)}, u32[]{:S(2)}) async-start(f32[16,32,256]{2,1,0:T(8,128)} %broadcast_in_dim.23), calls=%async_computation.3 | async-start | bytes 1048576 | tf_op jit(solution)/shard_map/all_to_all | solution.py:78
  100.9 2.0 bitcast_reduce_fusion
  104.7 3.4 all-to-all-done.3
  108.5 3.6 collective-permute-start.5
  117.8 2.6 collective-permute-done.6
  120.4 2.1 collective-permute-start.9
  124.1 2.1 shard_map.59
  126.2 11.7 %all_to_all.55.got = f32[4,16,1408]{2,1,0:T(8,128)} all-to-all(f32[4,16,1408]{2,1,0:T(8,128)} %shard_map.59), channel_id=1, replica_groups={{0,8,16,24},{32,40,48,56},{64,72,80,88},{96,104,112,120},{1,9,17,25},{3..., dimensions={0} | all-to-all | bytes 720896 | tf_op jit(solution)/shard_map/all_to_all | solution.py:251
  139.6 2.6 collective-permute-start.12
  142.6 7.5 %shard_map.61 = bf16[10,512,256]{2,1,0:T(8,128)(2,1)} custom-call(f32[10]{0:T(128)} %bitcast.210, f32[4,13,256,128]{3,2,1,0:T(8,128)} %bitcast.140), custom_call_target="tpu_custom_call" | custom-call | tf_op jit(solution)/shard_map/pallas_call | solution.py:111
  152.3 2.0 collective-permute-start.13
  155.4 2.7 collective-permute-start.16
  158.1 2.4 shard_map.62
  160.5 2.2 collective-permute-done.14
  164.2 2.5 collective-permute-start.19
  168.1 2.8 collective-permute-done.17
  172.7 3.8 collective-permute-start.20
  177.3 2.7 collective-permute-start.23
  181.3 3.0 collective-permute-done.21
  184.4 2.7 collective-permute-start.26
  188.3 3.0 collective-permute-done.24
  191.4 3.8 collective-permute-start.27
  196.0 2.7 collective-permute-start.30
  200.0 3.0 collective-permute-done.28
  204.8 2.7 collective-permute-start.33
  208.8 3.0 collective-permute-done.31
  211.9 3.8 collective-permute-start.34
  216.7 2.7 collective-permute-start.37
  221.4 2.6 collective-permute-done.35
  224.6 2.7 collective-permute-start.40
  229.2 2.8 collective-permute-done.38
  232.7 1.9 shard_map.63
  234.6 3.5 all-to-all-start.5
  238.4 8.4 %all-to-all-done.5 = f32[4,16,3200]{2,1,0:T(8,128)S(1)} async-done(((f32[4,16,3200]{2,1,0:T(8,128)}), f32[4,16,3200]{2,1,0:T(8,128)S(1)}, u32[]{:S(2)}, u32[]{:S(2)}) %all-to-all-start.5) | async-done | bytes 819232 | tf_op jit(solution)/shard_map/all_to_all | solution.py:286
  247.6 2.1 shard_map.64
  251.5 4.9 %collective-permute-start.41 = (f32[128,128]{1,0:T(8,128)S(1)}, f32[128,128]{1,0:T(8,128)S(1)}, u32[]{:S(2)}, u32[]{:S(2)}) collective-permute-start(f32[128,128]{1,0:T(8,128)S(1)} %dynamic-slice_bitcast_fusion.3), channel_id=1, source_target_pairs={{0,1},{1,0},{2,3},{3,2},{4,5},{5,4},{6,7},{7,6},{8,9},{9,8},{10,11... | collective-permute-start | bytes 196616 | tf_op jit(solution)/shard_map/ppermute | solution.py:59
  258.2 2.7 collective-permute-start.44
  262.5 3.0 collective-permute-done.42
  265.5 2.1 collective-permute-start.45
  270.3 13.6 %all_to_all.56 = f32[16,32,256]{2,1,0:T(8,128)S(1)} all-to-all(f32[16,32,256]{2,1,0:T(8,128)S(1)} %bitcast.153), channel_id=1, replica_groups=mesh['prow'=16,'pcol'=8] {'prow'}, dimensions={0} | all-to-all | bytes 1048576 | tf_op jit(solution)/shard_map/all_to_all | solution.py:73
  284.9 3.6 all-to-all-start.7
  288.9 8.6 %all-to-all-done.7 = f32[16,32,256]{2,1,0:T(8,128)S(1)} async-done(((f32[16,32,256]{2,1,0:T(8,128)}), f32[16,32,256]{2,1,0:T(8,128)S(1)}, u32[]{:S(2)}, u32[]{:S(2)}) %all-to-all-start.7) | async-done | bytes 524320 | tf_op jit(solution)/shard_map/all_to_all | solution.py:78
  298.9 3.8 collective-permute-start.46
  304.3 2.7 collective-permute-start.49
  308.6 2.0 collective-permute-done.48
  317.7 18.8 %all_to_all.57 = f32[16,64,256]{2,1,0:T(8,128)S(1)} all-to-all(f32[16,64,256]{2,1,0:T(8,128)S(1)} %fusion), channel_id=1, replica_groups=mesh['prow'=16,'pcol'=8] {'prow'}, dimensions={0} | all-to-all | bytes 2097152 | tf_op jit(solution)/shard_map/all_to_all | solution.py:73
  336.7 18.9 %all_to_all.58 = f32[16,64,256]{2,1,0:T(8,128)S(1)} all-to-all(f32[16,64,256]{2,1,0:T(8,128)S(1)} %broadcast_in_dim.31), channel_id=1, replica_groups=mesh['prow'=16,'pcol'=8] {'prow'}, dimensions={0} | all-to-all | bytes 2097152 | tf_op jit(solution)/shard_map/all_to_all | solution.py:78
  356.0 3.5 collective-permute-start.51
  360.8 17.8 %all_to_all.59 = f32[4,512,128]{2,1,0:T(8,128)S(1)} all-to-all(f32[4,512,128]{2,1,0:T(8,128)S(1)} %broadcast_in_dim.32), channel_id=1, replica_groups={{0,2,4,6},{1,3,5,7},{8,10,12,14},{9,11,13,15},{16,18,20,22},{17,19,21,2..., dimensions={0} | all-to-all | bytes 2097152 | tf_op jit(solution)/shard_map/all_to_all | solution.py:45
  378.7 1.9 collective-permute-start.52
  380.6 2.6 pad_maximum_fusion
  (227 shorter events, 81.5 us)
Async XLA Ops:
  10.0 24.1 %all-to-all-start = ((f32[16,64,256]{2,1,0:T(8,128)}), f32[16,64,256]{2,1,0:T(8,128)S(1)}, u32[]{:S(2)}, u32[]{:S(2)}) async-start(f32[16,64,256]{2,1,0:T(8,128)} %fusion.26), calls=%async_computation | async-start | bytes 2097152 | tf_op jit(solution)/shard_map/all_to_all | solution.py:73
  18.6 121.0 %all-gather.3.cloned.1.call-start = ((), (), s32[]{:S(2)}) async-start(), calls=%async_computation.11 | async-start | bytes 8519680 | tf_op jit(solution)/shard_map/all_gather | solution.py:127
  35.3 18.4 %all-to-all-start.1 = ((f32[16,64,256]{2,1,0:T(8,128)}), f32[16,64,256]{2,1,0:T(8,128)S(1)}, u32[]{:S(2)}, u32[]{:S(2)}) async-start(f32[16,64,256]{2,1,0:T(8,128)} %broadcast_in_dim.22), calls=%async_computation.1 | async-start | bytes 2097152 | tf_op jit(solution)/shard_map/all_to_all | solution.py:78
  44.0 39.1 %copy-start.18 = (f32[98]{0:T(128)}, f32[98]{0:T(128)S(1)}, u32[]{:S(2)}) copy-start(f32[98]{0:T(128)S(1)} %convert_element_type.66) | copy-start | bytes 1180
  57.1 4.9 %collective-permute-start = (f32[256,128]{1,0:T(8,128)}, f32[256,128]{1,0:T(8,128)S(1)}, u32[]{:S(2)}, u32[]{:S(2)}) collective-permute-start(f32[256,128]{1,0:T(8,128)} %dynamic-slice_bitcast_fusion.2), channel_id=1, source_target_pairs={{0,1},{1,0},{2,3},{3,2},{4,5},{5,4},{6,7},{7,6},{8,9},{9,8},{10,11... | collective-permute-start | bytes 393224 | tf_op jit(solution)/shard_map/ppermute | solution.py:59
  62.0 6.2 %collective-permute-start.2 = (f32[256,128]{1,0:T(8,128)S(1)}, f32[256,128]{1,0:T(8,128)S(1)}, u32[]{:S(2)}, u32[]{:S(2)}) collective-permute-start(f32[256,128]{1,0:T(8,128)S(1)} %bitcast_add_fusion.2), channel_id=1, source_target_pairs={{0,2},{1,3},{2,4},{3,5},{4,6},{5,7},{6,0},{7,1},{8,10},{9,11},{10,... | collective-permute-start | bytes 393224 | tf_op jit(solution)/shard_map/ppermute | solution.py:37
  63.4 4.9 %collective-permute-start.3 = (f32[256,128]{1,0:T(8,128)S(1)}, f32[256,128]{1,0:T(8,128)S(1)}, u32[]{:S(2)}, u32[]{:S(2)}) collective-permute-start(f32[256,128]{1,0:T(8,128)S(1)} %bitcast_add_fusion.2), channel_id=1, source_target_pairs={{0,6},{1,7},{2,0},{3,1},{4,2},{5,3},{6,4},{7,5},{8,14},{9,15},{10,... | collective-permute-start | bytes 393224 | tf_op jit(solution)/shard_map/ppermute | solution.py:37
  64.9 7.2 %collective-permute-start.1 = (f32[256,128]{1,0:T(8,128)S(1)}, f32[256,128]{1,0:T(8,128)S(1)}, u32[]{:S(2)}, u32[]{:S(2)}) collective-permute-start(f32[256,128]{1,0:T(8,128)S(1)} %bitcast_add_fusion.2), channel_id=1, source_target_pairs={{0,4},{1,5},{2,6},{3,7},{4,0},{5,1},{6,2},{7,3},{8,12},{9,13},{10,... | collective-permute-start | bytes 393224 | tf_op jit(solution)/shard_map/ppermute | solution.py:37
  72.1 2.3 collective-permute-start.4
  76.5 15.3 %all-to-all-start.2 = ((f32[16,32,256]{2,1,0:T(8,128)}), f32[16,32,256]{2,1,0:T(8,128)}, u32[]{:S(2)}, u32[]{:S(2)}) async-start(f32[16,32,256]{2,1,0:T(8,128)} %bitcast.149), calls=%async_computation.2 | async-start | bytes 1048576 | tf_op jit(solution)/shard_map/all_to_all | solution.py:73
  93.7 14.4 %all-to-all-start.3 = ((f32[16,32,256]{2,1,0:T(8,128)}), f32[16,32,256]{2,1,0:T(8,128)S(1)}, u32[]{:S(2)}, u32[]{:S(2)}) async-start(f32[16,32,256]{2,1,0:T(8,128)} %broadcast_in_dim.23), calls=%async_computation.3 | async-start | bytes 1048576 | tf_op jit(solution)/shard_map/all_to_all | solution.py:78
  108.5 4.5 %collective-permute-start.5 = (f32[128,128]{1,0:T(8,128)S(1)}, f32[128,128]{1,0:T(8,128)S(1)}, u32[]{:S(2)}, u32[]{:S(2)}) collective-permute-start(f32[128,128]{1,0:T(8,128)S(1)} %dynamic-slice_bitcast_fusion.4), channel_id=1, source_target_pairs={{0,1},{1,0},{2,3},{3,2},{4,5},{5,4},{6,7},{7,6},{8,9},{9,8},{10,11... | collective-permute-start | bytes 196616 | tf_op jit(solution)/shard_map/ppermute | solution.py:59
  113.0 4.8 %collective-permute-start.7 = (f32[128,128]{1,0:T(8,128)S(1)}, f32[128,128]{1,0:T(8,128)S(1)}, u32[]{:S(2)}, u32[]{:S(2)}) collective-permute-start(f32[128,128]{1,0:T(8,128)S(1)} %bitcast_add_fusion.4), channel_id=1, source_target_pairs={{0,2},{1,3},{2,4},{3,5},{4,6},{5,7},{6,0},{7,1},{8,10},{9,11},{10,... | collective-permute-start | bytes 196616 | tf_op jit(solution)/shard_map/ppermute | solution.py:37
  113.9 3.9 collective-permute-start.8
  115.8 4.7 %collective-permute-start.6 = (f32[128,128]{1,0:T(8,128)S(1)}, f32[128,128]{1,0:T(8,128)S(1)}, u32[]{:S(2)}, u32[]{:S(2)}) collective-permute-start(f32[128,128]{1,0:T(8,128)S(1)} %bitcast_add_fusion.4), channel_id=1, source_target_pairs={{0,4},{1,5},{2,6},{3,7},{4,0},{5,1},{6,2},{7,3},{8,12},{9,13},{10,... | collective-permute-start | bytes 196616 | tf_op jit(solution)/shard_map/ppermute | solution.py:37
  120.4 3.0 collective-permute-start.9
  139.6 12.3 %collective-permute-start.11 = (f32[64,256]{1,0:T(8,128)}, f32[64,256]{1,0:T(8,128)S(1)}, u32[]{:S(2)}, u32[]{:S(2)}) collective-permute-start(f32[64,256]{1,0:T(8,128)} %bitcast.205), channel_id=1, source_target_pairs={{0,32},{8,40},{16,48},{24,56},{32,64},{40,72},{48,80},{56,88},{64,... | collective-permute-start | bytes 196616 | tf_op jit(solution)/shard_map/ppermute | solution.py:37
  139.6 12.2 %collective-permute-start.12 = (f32[64,256]{1,0:T(8,128)}, f32[64,256]{1,0:T(8,128)S(1)}, u32[]{:S(2)}, u32[]{:S(2)}) collective-permute-start(f32[64,256]{1,0:T(8,128)} %bitcast.206), channel_id=1, source_target_pairs={{0,96},{8,104},{16,112},{24,120},{32,0},{40,8},{48,16},{56,24},{64... | collective-permute-start | bytes 196616 | tf_op jit(solution)/shard_map/ppermute | solution.py:37
  142.3 9.6 %collective-permute-start.10 = (f32[64,256]{1,0:T(8,128)}, f32[64,256]{1,0:T(8,128)S(1)}, u32[]{:S(2)}, u32[]{:S(2)}) collective-permute-start(f32[64,256]{1,0:T(8,128)} %bitcast.207), channel_id=1, source_target_pairs={{0,64},{8,72},{16,80},{24,88},{32,96},{40,104},{48,112},{56,120},{... | collective-permute-start | bytes 196616 | tf_op jit(solution)/shard_map/ppermute | solution.py:37
  151.9 80.1 %copy-start.6 = (f32[64,256]{1,0:T(8,128)}, f32[64,256]{1,0:T(8,128)S(1)}, u32[]{:S(2)}) copy-start(f32[64,256]{1,0:T(8,128)S(1)} %add_add_fusion.5) | copy-start | bytes 196612
  152.3 3.0 collective-permute-start.13
  155.3 5.2 %collective-permute-start.15 = (f32[32,512]{1,0:T(8,128)S(1)}, f32[32,512]{1,0:T(8,128)S(1)}, u32[]{:S(2)}, u32[]{:S(2)}) collective-permute-start(f32[32,512]{1,0:T(8,128)S(1)} %bitcast_add_fusion.6), channel_id=1, source_target_pairs={{0,2},{1,3},{2,4},{3,5},{4,6},{5,7},{6,0},{7,1},{8,10},{9,11},{10,... | collective-permute-start | bytes 196616 | tf_op jit(solution)/shard_map/ppermute | solution.py:37
  155.4 5.1 %collective-permute-start.16 = (f32[32,512]{1,0:T(8,128)S(1)}, f32[32,512]{1,0:T(8,128)S(1)}, u32[]{:S(2)}, u32[]{:S(2)}) collective-permute-start(f32[32,512]{1,0:T(8,128)S(1)} %bitcast_add_fusion.6), channel_id=1, source_target_pairs={{0,6},{1,7},{2,0},{3,1},{4,2},{5,3},{6,4},{7,5},{8,14},{9,15},{10,... | collective-permute-start | bytes 196616 | tf_op jit(solution)/shard_map/ppermute | solution.py:37
  158.1 4.6 %collective-permute-start.14 = (f32[32,512]{1,0:T(8,128)S(1)}, f32[32,512]{1,0:T(8,128)S(1)}, u32[]{:S(2)}, u32[]{:S(2)}) collective-permute-start(f32[32,512]{1,0:T(8,128)S(1)} %bitcast_add_fusion.6), channel_id=1, source_target_pairs={{0,4},{1,5},{2,6},{3,7},{4,0},{5,1},{6,2},{7,3},{8,12},{9,13},{10,... | collective-permute-start | bytes 196616 | tf_op jit(solution)/shard_map/ppermute | solution.py:37
  164.0 4.1 %collective-permute-start.18 = (f32[32,256]{1,0:T(8,128)S(1)}, f32[32,256]{1,0:T(8,128)S(1)}, u32[]{:S(2)}, u32[]{:S(2)}) collective-permute-start(f32[32,256]{1,0:T(8,128)S(1)} %bitcast.194), channel_id=1, source_target_pairs={{0,32},{8,40},{16,48},{24,56},{32,64},{40,72},{48,80},{56,88},{64,... | collective-permute-start | bytes 98312 | tf_op jit(solution)/shard_map/ppermute | solution.py:37
  164.2 3.9 collective-permute-start.19
  166.7 4.3 %collective-permute-start.17 = (f32[32,256]{1,0:T(8,128)S(1)}, f32[32,256]{1,0:T(8,128)S(1)}, u32[]{:S(2)}, u32[]{:S(2)}) collective-permute-start(f32[32,256]{1,0:T(8,128)S(1)} %bitcast.196), channel_id=1, source_target_pairs={{0,64},{8,72},{16,80},{24,88},{32,96},{40,104},{48,112},{56,120},{... | collective-permute-start | bytes 98312 | tf_op jit(solution)/shard_map/ppermute | solution.py:37
  171.0 41.0 %copy-start.12 = (f32[32,256]{1,0:T(8,128)}, f32[32,256]{1,0:T(8,128)S(1)}, u32[]{:S(2)}) copy-start(f32[32,256]{1,0:T(8,128)S(1)} %add_add_fusion.9) | copy-start | bytes 98308
  172.7 4.7 %collective-permute-start.20 = (f32[16,512]{1,0:T(8,128)S(1)}, f32[16,512]{1,0:T(8,128)S(1)}, u32[]{:S(2)}, u32[]{:S(2)}) collective-permute-start(f32[16,512]{1,0:T(8,128)S(1)} %fusion.9), channel_id=1, source_target_pairs={{0,1},{1,0},{2,3},{3,2},{4,5},{5,4},{6,7},{7,6},{8,9},{9,8},{10,11... | collective-permute-start | bytes 98312 | tf_op jit(solution)/shard_map/ppermute | solution.py:53
  177.3 4.0 %collective-permute-start.22 = (f32[16,512]{1,0:T(8,128)S(1)}, f32[16,512]{1,0:T(8,128)S(1)}, u32[]{:S(2)}, u32[]{:S(2)}) collective-permute-start(f32[16,512]{1,0:T(8,128)S(1)} %add.241), channel_id=1, source_target_pairs={{0,2},{1,3},{2,4},{3,5},{4,6},{5,7},{6,0},{7,1},{8,10},{9,11},{10,... | collective-permute-start | bytes 98312 | tf_op jit(solution)/shard_map/ppermute | solution.py:37
  177.3 4.0 %collective-permute-start.23 = (f32[16,512]{1,0:T(8,128)S(1)}, f32[16,512]{1,0:T(8,128)S(1)}, u32[]{:S(2)}, u32[]{:S(2)}) collective-permute-start(f32[16,512]{1,0:T(8,128)S(1)} %add.241), channel_id=1, source_target_pairs={{0,6},{1,7},{2,0},{3,1},{4,2},{5,3},{6,4},{7,5},{8,14},{9,15},{10,... | collective-permute-start | bytes 98312 | tf_op jit(solution)/shard_map/ppermute | solution.py:37
  180.0 4.3 %collective-permute-start.21 = (f32[16,512]{1,0:T(8,128)S(1)}, f32[16,512]{1,0:T(8,128)S(1)}, u32[]{:S(2)}, u32[]{:S(2)}) collective-permute-start(f32[16,512]{1,0:T(8,128)S(1)} %add.241), channel_id=1, source_target_pairs={{0,4},{1,5},{2,6},{3,7},{4,0},{5,1},{6,2},{7,3},{8,12},{9,13},{10,... | collective-permute-start | bytes 98312 | tf_op jit(solution)/shard_map/ppermute | solution.py:37
  184.4 3.8 collective-permute-start.25
  184.4 3.8 collective-permute-start.26
  187.1 4.1 %collective-permute-start.24 = (f32[16,256]{1,0:T(8,128)S(1)}, f32[16,256]{1,0:T(8,128)S(1)}, u32[]{:S(2)}, u32[]{:S(2)}) collective-permute-start(f32[16,256]{1,0:T(8,128)S(1)} %fusion.54), channel_id=1, source_target_pairs={{0,64},{8,72},{16,80},{24,88},{32,96},{40,104},{48,112},{56,120},{... | collective-permute-start | bytes 49160 | tf_op jit(solution)/shard_map/ppermute | solution.py:37
  191.2 33.3 %copy-start.14 = (f32[16,256]{1,0:T(8,128)}, f32[16,256]{1,0:T(8,128)S(1)}, u32[]{:S(2)}) copy-start(f32[16,256]{1,0:T(8,128)S(1)} %add_add_fusion.10) | copy-start | bytes 49156
  191.4 4.6 %collective-permute-start.27 = (f32[16,512]{1,0:T(8,128)S(1)}, f32[16,512]{1,0:T(8,128)S(1)}, u32[]{:S(2)}, u32[]{:S(2)}) collective-permute-start(f32[16,512]{1,0:T(8,128)S(1)} %fusion.53), channel_id=1, source_target_pairs={{0,1},{1,0},{2,3},{3,2},{4,5},{5,4},{6,7},{7,6},{8,9},{9,8},{10,11... | collective-permute-start | bytes 98312 | tf_op jit(solution)/shard_map/ppermute | solution.py:53
  196.0 4.0 %collective-permute-start.29 = (f32[16,512]{1,0:T(8,128)S(1)}, f32[16,512]{1,0:T(8,128)S(1)}, u32[]{:S(2)}, u32[]{:S(2)}) collective-permute-start(f32[16,512]{1,0:T(8,128)S(1)} %add.248), channel_id=1, source_target_pairs={{0,2},{1,3},{2,4},{3,5},{4,6},{5,7},{6,0},{7,1},{8,10},{9,11},{10,... | collective-permute-start | bytes 98312 | tf_op jit(solution)/shard_map/ppermute | solution.py:37
  196.0 4.0 %collective-permute-start.30 = (f32[16,512]{1,0:T(8,128)S(1)}, f32[16,512]{1,0:T(8,128)S(1)}, u32[]{:S(2)}, u32[]{:S(2)}) collective-permute-start(f32[16,512]{1,0:T(8,128)S(1)} %add.248), channel_id=1, source_target_pairs={{0,6},{1,7},{2,0},{3,1},{4,2},{5,3},{6,4},{7,5},{8,14},{9,15},{10,... | collective-permute-start | bytes 98312 | tf_op jit(solution)/shard_map/ppermute | solution.py:37
  198.7 4.3 %collective-permute-start.28 = (f32[16,512]{1,0:T(8,128)S(1)}, f32[16,512]{1,0:T(8,128)S(1)}, u32[]{:S(2)}, u32[]{:S(2)}) collective-permute-start(f32[16,512]{1,0:T(8,128)S(1)} %add.248), channel_id=1, source_target_pairs={{0,4},{1,5},{2,6},{3,7},{4,0},{5,1},{6,2},{7,3},{8,12},{9,13},{10,... | collective-permute-start | bytes 98312 | tf_op jit(solution)/shard_map/ppermute | solution.py:37
  204.8 4.0 %collective-permute-start.32 = (f32[32,256]{1,0:T(8,128)S(1)}, f32[32,256]{1,0:T(8,128)S(1)}, u32[]{:S(2)}, u32[]{:S(2)}) collective-permute-start(f32[32,256]{1,0:T(8,128)S(1)} %bitcast.197), channel_id=1, source_target_pairs={{0,32},{8,40},{16,48},{24,56},{32,64},{40,72},{48,80},{56,88},{64,... | collective-permute-start | bytes 98312 | tf_op jit(solution)/shard_map/ppermute | solution.py:37
  204.8 4.0 %collective-permute-start.33 = (f32[32,256]{1,0:T(8,128)S(1)}, f32[32,256]{1,0:T(8,128)S(1)}, u32[]{:S(2)}, u32[]{:S(2)}) collective-permute-start(f32[32,256]{1,0:T(8,128)S(1)} %bitcast.198), channel_id=1, source_target_pairs={{0,96},{8,104},{16,112},{24,120},{32,0},{40,8},{48,16},{56,24},{64... | collective-permute-start | bytes 98312 | tf_op jit(solution)/shard_map/ppermute | solution.py:37
  207.5 4.3 %collective-permute-start.31 = (f32[32,256]{1,0:T(8,128)S(1)}, f32[32,256]{1,0:T(8,128)S(1)}, u32[]{:S(2)}, u32[]{:S(2)}) collective-permute-start(f32[32,256]{1,0:T(8,128)S(1)} %bitcast.199), channel_id=1, source_target_pairs={{0,64},{8,72},{16,80},{24,88},{32,96},{40,104},{48,112},{56,120},{... | collective-permute-start | bytes 98312 | tf_op jit(solution)/shard_map/ppermute | solution.py:37
  211.9 4.7 %collective-permute-start.34 = (f32[32,512]{1,0:T(8,128)S(1)}, f32[32,512]{1,0:T(8,128)S(1)}, u32[]{:S(2)}, u32[]{:S(2)}) collective-permute-start(f32[32,512]{1,0:T(8,128)S(1)} %bitcast.183), channel_id=1, source_target_pairs={{0,1},{1,0},{2,3},{3,2},{4,5},{5,4},{6,7},{7,6},{8,9},{9,8},{10,11... | collective-permute-start | bytes 196616 | tf_op jit(solution)/shard_map/ppermute | solution.py:53
  216.6 4.4 %collective-permute-start.36 = (f32[32,512]{1,0:T(8,128)S(1)}, f32[32,512]{1,0:T(8,128)S(1)}, u32[]{:S(2)}, u32[]{:S(2)}) collective-permute-start(f32[32,512]{1,0:T(8,128)S(1)} %bitcast_add_fusion.5), channel_id=1, source_target_pairs={{0,2},{1,3},{2,4},{3,5},{4,6},{5,7},{6,0},{7,1},{8,10},{9,11},{10,... | collective-permute-start | bytes 196616 | tf_op jit(solution)/shard_map/ppermute | solution.py:37
  216.7 4.7 %collective-permute-start.37 = (f32[32,512]{1,0:T(8,128)S(1)}, f32[32,512]{1,0:T(8,128)S(1)}, u32[]{:S(2)}, u32[]{:S(2)}) collective-permute-start(f32[32,512]{1,0:T(8,128)S(1)} %bitcast_add_fusion.5), channel_id=1, source_target_pairs={{0,6},{1,7},{2,0},{3,1},{4,2},{5,3},{6,4},{7,5},{8,14},{9,15},{10,... | collective-permute-start | bytes 196616 | tf_op jit(solution)/shard_map/ppermute | solution.py:37
  219.4 4.6 %collective-permute-start.35 = (f32[32,512]{1,0:T(8,128)S(1)}, f32[32,512]{1,0:T(8,128)S(1)}, u32[]{:S(2)}, u32[]{:S(2)}) collective-permute-start(f32[32,512]{1,0:T(8,128)S(1)} %bitcast_add_fusion.5), channel_id=1, source_target_pairs={{0,4},{1,5},{2,6},{3,7},{4,0},{5,1},{6,2},{7,3},{8,12},{9,13},{10,... | collective-permute-start | bytes 196616 | tf_op jit(solution)/shard_map/ppermute | solution.py:37
  224.6 4.3 %collective-permute-start.39 = (f32[64,256]{1,0:T(8,128)S(1)}, f32[64,256]{1,0:T(8,128)S(1)}, u32[]{:S(2)}, u32[]{:S(2)}) collective-permute-start(f32[64,256]{1,0:T(8,128)S(1)} %bitcast.179), channel_id=1, source_target_pairs={{0,32},{8,40},{16,48},{24,56},{32,64},{40,72},{48,80},{56,88},{64,... | collective-permute-start | bytes 196616 | tf_op jit(solution)/shard_map/ppermute | solution.py:37
  224.6 4.6 %collective-permute-start.40 = (f32[64,256]{1,0:T(8,128)S(1)}, f32[64,256]{1,0:T(8,128)S(1)}, u32[]{:S(2)}, u32[]{:S(2)}) collective-permute-start(f32[64,256]{1,0:T(8,128)S(1)} %bitcast.180), channel_id=1, source_target_pairs={{0,96},{8,104},{16,112},{24,120},{32,0},{40,8},{48,16},{56,24},{64... | collective-permute-start | bytes 196616 | tf_op jit(solution)/shard_map/ppermute | solution.py:37
  227.3 4.7 %collective-permute-start.38 = (f32[64,256]{1,0:T(8,128)S(1)}, f32[64,256]{1,0:T(8,128)S(1)}, u32[]{:S(2)}, u32[]{:S(2)}) collective-permute-start(f32[64,256]{1,0:T(8,128)S(1)} %bitcast.181), channel_id=1, source_target_pairs={{0,64},{8,72},{16,80},{24,88},{32,96},{40,104},{48,112},{56,120},{... | collective-permute-start | bytes 196616 | tf_op jit(solution)/shard_map/ppermute | solution.py:37
  234.6 12.2 %all-to-all-start.5 = ((f32[4,16,3200]{2,1,0:T(8,128)}), f32[4,16,3200]{2,1,0:T(8,128)S(1)}, u32[]{:S(2)}, u32[]{:S(2)}) async-start(f32[4,16,3200]{2,1,0:T(8,128)} %shard_map.63), calls=%async_computation.5 | async-start | bytes 1638400 | tf_op jit(solution)/shard_map/all_to_all | solution.py:286
  251.5 5.8 %collective-permute-start.41 = (f32[128,128]{1,0:T(8,128)S(1)}, f32[128,128]{1,0:T(8,128)S(1)}, u32[]{:S(2)}, u32[]{:S(2)}) collective-permute-start(f32[128,128]{1,0:T(8,128)S(1)} %dynamic-slice_bitcast_fusion.3), channel_id=1, source_target_pairs={{0,1},{1,0},{2,3},{3,2},{4,5},{5,4},{6,7},{7,6},{8,9},{9,8},{10,11... | collective-permute-start | bytes 196616 | tf_op jit(solution)/shard_map/ppermute | solution.py:59
  258.1 4.4 %collective-permute-start.43 = (f32[128,128]{1,0:T(8,128)S(1)}, f32[128,128]{1,0:T(8,128)S(1)}, u32[]{:S(2)}, u32[]{:S(2)}) collective-permute-start(f32[128,128]{1,0:T(8,128)S(1)} %bitcast_add_fusion.3), channel_id=1, source_target_pairs={{0,2},{1,3},{2,4},{3,5},{4,6},{5,7},{6,0},{7,1},{8,10},{9,11},{10,... | collective-permute-start | bytes 196616 | tf_op jit(solution)/shard_map/ppermute | solution.py:37
  258.2 4.3 %collective-permute-start.44 = (f32[128,128]{1,0:T(8,128)S(1)}, f32[128,128]{1,0:T(8,128)S(1)}, u32[]{:S(2)}, u32[]{:S(2)}) collective-permute-start(f32[128,128]{1,0:T(8,128)S(1)} %bitcast_add_fusion.3), channel_id=1, source_target_pairs={{0,6},{1,7},{2,0},{3,1},{4,2},{5,3},{6,4},{7,5},{8,14},{9,15},{10,... | collective-permute-start | bytes 196616 | tf_op jit(solution)/shard_map/ppermute | solution.py:37
  260.9 4.6 %collective-permute-start.42 = (f32[128,128]{1,0:T(8,128)S(1)}, f32[128,128]{1,0:T(8,128)S(1)}, u32[]{:S(2)}, u32[]{:S(2)}) collective-permute-start(f32[128,128]{1,0:T(8,128)S(1)} %bitcast_add_fusion.3), channel_id=1, source_target_pairs={{0,4},{1,5},{2,6},{3,7},{4,0},{5,1},{6,2},{7,3},{8,12},{9,13},{10,... | collective-permute-start | bytes 196616 | tf_op jit(solution)/shard_map/ppermute | solution.py:37
  265.5 3.4 collective-permute-start.45
  284.9 12.6 %all-to-all-start.7 = ((f32[16,32,256]{2,1,0:T(8,128)}), f32[16,32,256]{2,1,0:T(8,128)S(1)}, u32[]{:S(2)}, u32[]{:S(2)}) async-start(f32[16,32,256]{2,1,0:T(8,128)} %broadcast_in_dim.27), calls=%async_computation.7 | async-start | bytes 1048576 | tf_op jit(solution)/shard_map/all_to_all | solution.py:78
  298.9 5.3 %collective-permute-start.46 = (f32[256,128]{1,0:T(8,128)S(1)}, f32[256,128]{1,0:T(8,128)S(1)}, u32[]{:S(2)}, u32[]{:S(2)}) collective-permute-start(f32[256,128]{1,0:T(8,128)S(1)} %dynamic-slice_bitcast_fusion.1), channel_id=1, source_target_pairs={{0,1},{1,0},{2,3},{3,2},{4,5},{5,4},{6,7},{7,6},{8,9},{9,8},{10,11... | collective-permute-start | bytes 393224 | tf_op jit(solution)/shard_map/ppermute | solution.py:59
  304.2 6.4 %collective-permute-start.48 = (f32[256,128]{1,0:T(8,128)S(1)}, f32[256,128]{1,0:T(8,128)S(1)}, u32[]{:S(2)}, u32[]{:S(2)}) collective-permute-start(f32[256,128]{1,0:T(8,128)S(1)} %bitcast_add_fusion.1), channel_id=1, source_target_pairs={{0,2},{1,3},{2,4},{3,5},{4,6},{5,7},{6,0},{7,1},{8,10},{9,11},{10,... | collective-permute-start | bytes 393224 | tf_op jit(solution)/shard_map/ppermute | solution.py:37
  304.3 7.9 %collective-permute-start.49 = (f32[256,128]{1,0:T(8,128)S(1)}, f32[256,128]{1,0:T(8,128)S(1)}, u32[]{:S(2)}, u32[]{:S(2)}) collective-permute-start(f32[256,128]{1,0:T(8,128)S(1)} %bitcast_add_fusion.1), channel_id=1, source_target_pairs={{0,6},{1,7},{2,0},{3,1},{4,2},{5,3},{6,4},{7,5},{8,14},{9,15},{10,... | collective-permute-start | bytes 393224 | tf_op jit(solution)/shard_map/ppermute | solution.py:37
  307.0 6.0 %collective-permute-start.47 = (f32[256,128]{1,0:T(8,128)S(1)}, f32[256,128]{1,0:T(8,128)S(1)}, u32[]{:S(2)}, u32[]{:S(2)}) collective-permute-start(f32[256,128]{1,0:T(8,128)S(1)} %bitcast_add_fusion.1), channel_id=1, source_target_pairs={{0,4},{1,5},{2,6},{3,7},{4,0},{5,1},{6,2},{7,3},{8,12},{9,13},{10,... | collective-permute-start | bytes 393224 | tf_op jit(solution)/shard_map/ppermute | solution.py:37
  313.0 3.1 collective-permute-start.50
  356.0 4.7 %collective-permute-start.51 = (f32[512,128]{1,0:T(8,128)S(1)}, f32[512,128]{1,0:T(8,128)S(1)}, u32[]{:S(2)}, u32[]{:S(2)}) collective-permute-start(f32[512,128]{1,0:T(8,128)S(1)} %dynamic-slice_bitcast_fusion), channel_id=1, source_target_pairs={{0,1},{1,0},{2,3},{3,2},{4,5},{5,4},{6,7},{7,6},{8,9},{9,8},{10,11... | collective-permute-start | bytes 786440 | tf_op jit(solution)/shard_map/ppermute | solution.py:59
  378.7 4.5 %collective-permute-start.52 = (f32[512,128]{1,0:T(8,128)S(1)}, f32[512,128]{1,0:T(8,128)S(1)}, u32[]{:S(2)}, u32[]{:S(2)}) collective-permute-start(f32[512,128]{1,0:T(8,128)S(1)} %reduce_sum.143), channel_id=1, source_target_pairs={{0,1},{1,0},{2,3},{3,2},{4,5},{5,4},{6,7},{7,6},{8,9},{9,8},{10,11... | collective-permute-start | bytes 786440 | tf_op jit(solution)/shard_map/ppermute | solution.py:61
  (18 other events, 191.6 us)
Sparse Core Ops, SparseCore 0:
  34.3 87.7 all-gather.2
where the time goes:
time: 393 us; the launch traced here: 391 us
  starting transfers between devices  111 us (28%)
  waiting for transfers between devices  104 us (26%)
  blocking collectives  80.8 us (21%)
  matrix products  30.3 us (8%)
  local copies, waits for them, and re-layouts  20.9 us (5%)
  Pallas kernels  17.6 us (4%)
  between operations  14.8 us (4%)
  other arithmetic  11.8 us (3%)
    ppermute x39, waiting for transfers between devices, sum_ring(): across, right, left = [lax.ppermute(values, axis, step) for step in ring]  48.3 us
    ppermute x39, starting transfers between devices, sum_ring(): across, right, left = [lax.ppermute(values, axis, step) for step in ring]  39.1 us
    all_to_all x2, blocking collectives, scatter_rows(): return lax.all_to_all(chunks, 'prow', 0, 0).sum(axis=0)  32.4 us
    dot_general x28, matrix products, product(): return jnp.einsum(form, left, right, preferred_element_type=jnp.float32)  30.3 us
    all_to_all x3, waiting for transfers between devices, share_rows(): return lax.all_to_all(copies, 'prow', 0, 0).reshape(shape)  21.4 us
    ppermute x5, starting transfers between devices, sum_columns(): mine = mine + lax.ppermute(other, 'pcol', TWIN)  19.5 us
    all_to_all x1, blocking collectives, share_rows(): return lax.all_to_all(copies, 'prow', 0, 0).reshape(shape)  18.9 us
    all_to_all x1, blocking collectives, sum_y_ring(): parts = lax.all_to_all(copies, 'pcol', 0, 0, axis_index_groups=YGROUPS)  17.8 us
  transfers between devices with their start and end apart: 60, of which 40 were waited for; matrix products, arithmetic and copies ran while one was open for 11% of the time, Pallas kernels for 3%

commit v1 on v0

--- a/solution.py
+++ b/solution.py
@@ -10,7 +10,6 @@
 TOP = 3
 TWIN = [(i, i ^ 1) for i in range(8)]
 YRING = [[(i, (i + 2 * k) % 8) for i in range(8)] for k in (2, 1, 3)]
-YGROUPS = [[0, 2, 4, 6], [1, 3, 5, 7]]
 XRING = [[(i, (i + 4 * k) % 16) for i in range(16)] for k in (2, 1, 3)]
 ZGROUPS = [[4 * x + z for z in range(4)] for x in range(4)]
 
@@ -33,31 +32,35 @@
     return jnp.einsum(form, left, right, preferred_element_type=jnp.float32)
 
 
+def sum_children(terms, upward):
+    return terms.reshape((-1, 2**upward) + terms.shape[1:]).sum(axis=1)
+
+
+def top_order(array):
+    return jnp.concatenate([array[2:10:2], array[3:10:2], array[0:2]])
+
+
+def top_inverses(array):
+    return jnp.concatenate([array[1:3], array[0:1]])
+
+
 def sum_ring(values, axis, ring):
     across, right, left = [lax.ppermute(values, axis, step) for step in ring]
     return (values + across) + (right + left)
 
 
-def sum_y_ring(values):
-    if values.size <= 32768:
-        return sum_ring(values, "pcol", YRING)
-    copies = jnp.broadcast_to(values[None], (4,) + values.shape)
-    parts = lax.all_to_all(copies, "pcol", 0, 0, axis_index_groups=YGROUPS)
-    return parts.sum(axis=0)
-
-
 def sum_columns(values):
     shape = values.shape
     flat = values.reshape(-1, shape[-1])
-    if flat.size <= 16384:
+    if flat.size <= 32768:
         flat = flat + lax.ppermute(flat, "pcol", TWIN)
-        return sum_y_ring(flat).reshape(shape)
+        return sum_ring(flat, "pcol", YRING).reshape(shape)
     halves = flat.reshape(2, -1, shape[-1])
     core = lax.axis_index("pcol") % 2
     mine = lax.dynamic_index_in_dim(halves, core, 0, keepdims=False)
     other = lax.dynamic_index_in_dim(halves, 1 - core, 0, keepdims=False)
     mine = mine + lax.ppermute(other, "pcol", TWIN)
-    mine = sum_y_ring(mine)
+    mine = sum_ring(mine, "pcol", YRING)
     other = lax.ppermute(mine, "pcol", TWIN)
     both = jnp.where(core == 0, jnp.stack([mine, other]), jnp.stack([other, mine]))
     return both.reshape(shape)
@@ -82,7 +85,7 @@
     return share_rows(scatter_rows(values), values.shape)
 
 
-def round_inverses(whole, count):
+def round_inverses(whole, count, at):
     def kernel(blocks, out):
         for i in range(count):
             for z in range(4):
@@ -92,37 +95,35 @@
         kernel,
         out_shape=jax.ShapeDtypeStruct((count, 256, 512), jnp.bfloat16),
         grid=(1,),
-        in_specs=[pl.BlockSpec((4, count, 256, 128), lambda i: (0, 0, 0, 0))],
+        in_specs=[pl.BlockSpec((4, count, 256, 128), lambda i: (0, at, 0, 0))],
         out_specs=pl.BlockSpec((count, 256, 512), lambda i: (0, 0, 0)),
     )(whole)
 
 
-def round_factors(whole, weights, first):
-    count = whole.shape[1] - first
-
+def round_factors(whole, weights, count, at):
     def kernel(weights, blocks, out):
-        weight = weights[pl.program_id(0)]
-        for z in range(4):
-            for h in range(2):
-                values = blocks[z, 0, 128 * h : 128 * h + 128, :] * weight
-                rows = slice(128 * z, 128 * z + 128)
-                out[0, rows, 128 * h : 128 * h + 128] = values.astype(jnp.bfloat16)
+        for i in range(count):
+            for z in range(4):
+                for h in range(2):
+                    values = blocks[z, i, 128 * h : 128 * h + 128, :] * weights[i]
+                    rows = slice(128 * z, 128 * z + 128)
+                    out[i, rows, 128 * h : 128 * h + 128] = values.astype(jnp.bfloat16)
 
     return pl.pallas_call(
         kernel,
         out_shape=jax.ShapeDtypeStruct((count, 512, 256), jnp.bfloat16),
-        grid=(count,),
+        grid=(1,),
         in_specs=[
             pl.BlockSpec(memory_space=pltpu.SMEM),
-            pl.BlockSpec((4, 1, 256, 128), lambda i: (0, i + first, 0, 0)),
+            pl.BlockSpec((4, count, 256, 128), lambda i: (0, at, 0, 0)),
         ],
-        out_specs=pl.BlockSpec((1, 512, 256), lambda i: (i, 0, 0)),
+        out_specs=pl.BlockSpec((count, 512, 256), lambda i: (0, 0, 0)),
     )(weights, whole)
 
 
 def gather_blocks(inverses, factors, after):
     halves = factors.reshape(-1, 128, 2, 128).transpose(0, 2, 1, 3).reshape(-1, 256, 128)
-    own = jnp.concatenate([inverses, halves]).astype(jnp.float32)
+    own = jnp.concatenate([halves, inverses]).astype(jnp.float32)
     own, after = lax.optimization_barrier((own, after))
     whole = lax.all_gather(own, "prow", axis_index_groups=ZGROUPS)
     return whole, after
@@ -210,20 +211,11 @@
     forward_levels = [None] * LEV
     partial_value = [[] for _ in range(LEV)]
 
-    def push_up(narrow, tree_depth, factors, weights, values):
-        count = 2**tree_depth
+    def push_up(narrow, tree_depth):
         for upward in range(1, tree_depth + 1):
-            blocks = factors[upward - 1 :: tree_depth]
-            terms = product(narrow, blocks, "nrc,nwc->nrw")
-            if weights is not None:
-                terms = terms * weights[upward - 1 :: tree_depth][:, None, None]
-            groups = count >> upward
-            terms = terms.reshape((groups, 2**upward) + terms.shape[1:]).sum(axis=1)
-            values[tree_depth - upward].append(terms)
-
-    def own_blocks(array, tree_depth):
-        start = block_start(tree_depth)
-        return array[start : start + 2**tree_depth * tree_depth]
+            terms = product(narrow, blocks_of(factor, tree_depth, upward), "nrc,nwc->nrw")
+            terms = terms * blocks_of(live, tree_depth, upward)[:, None, None]
+            partial_value[tree_depth - upward].append(sum_children(terms, upward))
 
     for tree_depth in range(LEV - 1, TOP - 1, -1):
         residual = nodes_of(rhs, tree_depth)
@@ -232,16 +224,10 @@
         pieces = product(residual.astype(bf16), nodes_of(inverse, tree_depth), "nrc,nwc->nrw")
         part = scatter_rows(pieces)
         if tree_depth == LEV - 1:
-            whole, part = gather_blocks(inverse[0:3], factor[0:10], part)
+            whole, part = gather_blocks(top_inverses(inverse), top_order(factor), part)
         forward = share_rows(part, pieces.shape)
         forward_levels[tree_depth] = forward
-        push_up(
-            forward.astype(bf16),
-            tree_depth,
-            own_blocks(factor, tree_depth),
-            own_blocks(live, tree_depth),
-            partial_value,
-        )
+        push_up(forward.astype(bf16), tree_depth)
 
     here = (lax.axis_index("pcol") == 0).astype(jnp.float32)
     total = sum_columns(sum(partial_value[2]))
@@ -251,20 +237,28 @@
     got = lax.all_to_all(sent, "prow", 0, 0, axis_index_groups=ZGROUPS)
     pieces, sums_1, sums_0 = entered_split(got)
     pieces, whole = lax.optimization_barrier((pieces, whole))
-    top_inverses = round_inverses(whole, 3)
-    top_factors = round_factors(whole, live[0:10], 3)
+    weights = top_order(live)
+    parents = round_factors(whole, weights[0:4], 4, 0)
+    roots = round_factors(whole, weights[4:8], 4, 1)
+    children = round_factors(whole, weights[8:10], 2, 4)
+    inverse_at = [round_inverses(whole, 1, 12), round_inverses(whole, 2, 5)]
     top_forward = [None] * TOP
     top_forward[2] = sum_x_ring(pieces)
     top_partial = [[sums_0], [sums_1]]
-    inverse_at = [top_inverses[0:1], top_inverses[1:3]]
-    factor_at = [None, top_factors[0:2], top_factors[2:10]]
-    push_up(top_forward[2].astype(bf16), 2, factor_at[2], None, top_partial)
+
+    def split_up(narrow, tree_depth):
+        for upward in range(1, tree_depth + 1):
+            terms = product(narrow, factor_at[tree_depth][upward - 1], "nrc,nwc->nrw")
+            top_partial[tree_depth - upward].append(sum_children(terms, upward))
+
+    factor_at = [None, [children], [parents, roots]]
+    split_up(top_forward[2].astype(bf16), 2)
     for tree_depth in (1, 0):
         residual = -sum_columns(sum(top_partial[tree_depth]))
         pieces = product(residual.astype(bf16), inverse_at[tree_depth], "nrc,nwc->nrw")
         top_forward[tree_depth] = sum_x_ring(pieces)
         if tree_depth:
-            push_up(top_forward[1].astype(bf16), 1, factor_at[1], None, top_partial)
+            split_up(top_forward[1].astype(bf16), 1)
 
     top_solved = []
     for tree_depth in range(TOP):
@@ -275,7 +269,7 @@
                 above = jnp.repeat(
                     top_solved[tree_depth - upward].astype(bf16), 2**upward, axis=0
                 )
-                blocks = factor_at[tree_depth][upward - 1 :: tree_depth]
+                blocks = factor_at[tree_depth][upward - 1]
                 terms = terms + product(above, blocks, "nrw,nwc->nrc")
             target = target - sum_x_ring(terms)
         if tree_depth < TOP - 1:
@@ -301,12 +295,14 @@
     for tree_depth in range(TOP - 1, LEV):
         if tree_depth >= TOP:
             target = forward_levels[tree_depth] - sum_rows(sum(gathered[tree_depth]))
+            if tree_depth == LEV - 1:
+                forward_whole = jnp.concatenate([top_forward] + forward_levels[TOP:])
+                target, forward_whole = lax.optimization_barrier((target, forward_whole))
             pieces = product(target.astype(bf16), nodes_of(inverse, tree_depth), "nrw,nwc->nrc")
         solution = sum_columns(pieces)
         solved.append(solution)
         push_down(solution.astype(bf16), tree_depth)
-    forward_levels = [top_forward] + forward_levels[TOP:]
-    return (jnp.concatenate(solved, axis=0), jnp.concatenate(forward_levels, axis=0))
+    return jnp.concatenate(solved), forward_whole
 
 
 def solution(mesh):

time: 393 us -> 391 us (level)
  waiting for transfers between devices: 104 us -> 117 us
  blocking collectives: 80.8 us -> 68.7 us
  local copies, waits for them, and re-layouts: 20.9 us -> 10.5 us
  matrix products: 30.3 us -> 38.4 us
    all_to_all x1 -> x0, blocking collectives: 17.8 us -> none  [sum_y_ring(): parts = lax.all_to_all(copies, 'pcol', 0, 0, axis_index_groups=YGROUPS)]
    all_to_all x1 -> x2, blocking collectives: 11.7 us -> 24.9 us  [per_device(): got = lax.all_to_all(sent, 'prow', 0, 0, axis_index_groups=ZGROUPS)]
    all_to_all x3, waiting for transfers between devices: 21.4 us -> 31.3 us  [share_rows(): return lax.all_to_all(copies, 'prow', 0, 0).reshape(shape)]
    ppermute x5 -> x3, starting transfers between devices: 19.5 us -> 10.6 us  [sum_columns(): mine = mine + lax.ppermute(other, 'pcol', TWIN)]
    ppermute x39 -> x42, waiting for transfers between devices: 48.3 us -> 56.9 us  [sum_ring(): across, right, left = [lax.ppermute(values, axis, step) for step in ring]]
    all_to_all x1 -> x0, waiting for transfers between devices: 8.37 us -> none  [per_device(): got = lax.all_to_all(sent, 'prow', 0, 0, axis_index_groups=ZGROUPS)]
    ppermute x39 -> x42, starting transfers between devices: 39.1 us -> 47.3 us  [sum_ring(): across, right, left = [lax.ppermute(values, axis, step) for step in ring]]
    dot_general x28, matrix products: 30.3 us -> 38.4 us  [product(): return jnp.einsum(form, left, right, preferred_element_type=jnp.float32)]
  transfers between devices with their start and end apart: 60 -> 60, of which waited for: 40 -> 38; matrix products, arithmetic and copies ran while one was open for 11% -> 9% of each run, Pallas kernels for 3% -> 4%
where the time goes in v1:
time: 391 us; the launch traced here: 389 us
  waiting for transfers between devices  117 us (30%)
  starting transfers between devices  109 us (28%)
  blocking collectives  68.7 us (18%)
  matrix products  38.4 us (10%)
  Pallas kernels  19.5 us (5%)
  between operations  14.8 us (4%)
  other arithmetic  11.2 us (3%)
  local copies, waits for them, and re-layouts  10.5 us (3%)
    ppermute x42, waiting for transfers between devices, sum_ring(): across, right, left = [lax.ppermute(values, axis, step) for step in ring]  56.9 us
    ppermute x42, starting transfers between devices, sum_ring(): across, right, left = [lax.ppermute(values, axis, step) for step in ring]  47.3 us
    dot_general x28, matrix products, product(): return jnp.einsum(form, left, right, preferred_element_type=jnp.float32)  38.4 us
    all_to_all x3, waiting for transfers between devices, share_rows(): return lax.all_to_all(copies, 'prow', 0, 0).reshape(shape)  31.3 us
    all_to_all x2, blocking collectives, scatter_rows(): return lax.all_to_all(chunks, 'prow', 0, 0).sum(axis=0)  30.4 us
    all_to_all x2, blocking collectives, per_device(): got = lax.all_to_all(sent, 'prow', 0, 0, axis_index_groups=ZGROUPS)  24.9 us
    all_to_all x2, waiting for transfers between devices, scatter_rows(): return lax.all_to_all(chunks, 'prow', 0, 0).sum(axis=0)  20.3 us
    ppermute x6, starting transfers between devices, sum_columns(): flat = flat + lax.ppermute(flat, 'pcol', TWIN)  19.8 us
  transfers between devices with their start and end apart: 60, of which 38 were waited for; matrix products, arithmetic and copies ran while one was open for 9% of the time, Pallas kernels for 4%

profile of v1, /device:TPU:1, one launch (start us, length us, event | category | flops | bytes accessed | tf_op | source)
XLA Modules:
  0.0 388.8 jit_solution(12619696642782009377)
XLA Ops:
  7.2 2.9 fusion.20
  10.2 8.6 %all-to-all-start = ((f32[16,64,256]{2,1,0:T(8,128)}), f32[16,64,256]{2,1,0:T(8,128)S(1)}, u32[]{:S(2)}, u32[]{:S(2)}) async-start(f32[16,64,256]{2,1,0:T(8,128)} %fusion.20), calls=%async_computation | async-start | bytes 2097152 | tf_op jit(solution)/shard_map/all_to_all | solution.py:76
  21.4 12.9 %all-to-all-done = f32[16,64,256]{2,1,0:T(8,128)S(1)} async-done(((f32[16,64,256]{2,1,0:T(8,128)}), f32[16,64,256]{2,1,0:T(8,128)S(1)}, u32[]{:S(2)}, u32[]{:S(2)}) %all-to-all-start) | async-done | bytes 1048608 | tf_op jit(solution)/shard_map/all_to_all | solution.py:76
  35.5 4.0 %all-to-all-start.1 = ((f32[16,64,256]{2,1,0:T(8,128)}), f32[16,64,256]{2,1,0:T(8,128)S(1)}, u32[]{:S(2)}, u32[]{:S(2)}) async-start(f32[16,64,256]{2,1,0:T(8,128)} %broadcast_in_dim.20), calls=%async_computation.1 | async-start | bytes 2097152 | tf_op jit(solution)/shard_map/all_to_all | solution.py:81
  39.6 14.2 %all-to-all-done.1 = f32[16,64,256]{2,1,0:T(8,128)S(1)} async-done(((f32[16,64,256]{2,1,0:T(8,128)}), f32[16,64,256]{2,1,0:T(8,128)S(1)}, u32[]{:S(2)}, u32[]{:S(2)}) %all-to-all-start.1) | async-done | bytes 1048608 | tf_op jit(solution)/shard_map/all_to_all | solution.py:81
  54.7 1.7 bitcast_reduce_fusion.1
  57.1 3.7 collective-permute-start
  62.1 2.8 collective-permute-start.3
  67.4 6.2 %collective-permute-done.2 = f32[256,128]{1,0:T(8,128)S(1)} collective-permute-done((f32[256,128]{1,0:T(8,128)S(1)}, f32[256,128]{1,0:T(8,128)S(1)}, u32[]{:S(2)}, u32[]{:S(2)}) %collective-permute-start.2) | collective-permute-done | bytes 131104 | tf_op jit(solution)/shard_map/ppermute | solution.py:48
  75.9 2.1 fusion.33
  78.0 4.9 %all-to-all-start.2 = ((f32[16,32,256]{2,1,0:T(8,128)}), f32[16,32,256]{2,1,0:T(8,128)}, u32[]{:S(2)}, u32[]{:S(2)}) async-start(f32[16,32,256]{2,1,0:T(8,128)} %bitcast.154), calls=%async_computation.2 | async-start | bytes 1048576 | tf_op jit(solution)/shard_map/all_to_all | solution.py:76
  83.6 1.7 slice.110.order
  86.0 7.4 %all-to-all-done.2 = f32[16,32,256]{2,1,0:T(8,128)} async-done(((f32[16,32,256]{2,1,0:T(8,128)}), f32[16,32,256]{2,1,0:T(8,128)}, u32[]{:S(2)}, u32[]{:S(2)}) %all-to-all-start.2) | async-done | bytes 524320 | tf_op jit(solution)/shard_map/all_to_all | solution.py:76
  95.3 5.4 %all-to-all-start.3 = ((f32[16,32,256]{2,1,0:T(8,128)}), f32[16,32,256]{2,1,0:T(8,128)S(1)}, u32[]{:S(2)}, u32[]{:S(2)}) async-start(f32[16,32,256]{2,1,0:T(8,128)} %broadcast_in_dim.21), calls=%async_computation.3 | async-start | bytes 1048576 | tf_op jit(solution)/shard_map/all_to_all | solution.py:81
  100.7 1.9 fusion.5
  102.6 1.9 bitcast_reduce_fusion
  104.5 1.9 bitcast_reduce_fusion.2
  106.4 3.3 all-to-all-done.3
  111.3 3.6 collective-permute-start.5
  120.7 2.7 collective-permute-done.8
  123.4 3.9 collective-permute-done.7
  128.0 2.1 shard_map.59
  130.1 10.5 %all_to_all.50.got = f32[4,16,1408]{2,1,0:T(8,128)} all-to-all(f32[4,16,1408]{2,1,0:T(8,128)} %shard_map.59), channel_id=1, replica_groups={{0,8,16,24},{32,40,48,56},{64,72,80,88},{96,104,112,120},{1,9,17,25},{3..., dimensions={0} | all-to-all | bytes 720896 | tf_op jit(solution)/shard_map/all_to_all | solution.py:237
  142.3 2.7 collective-permute-start.11
  146.0 2.7 shard_map.62
  151.8 3.9 collective-permute-start.12
  159.7 2.1 shard_map.63
  164.5 2.7 collective-permute-start.18
  167.9 2.1 shard_map.64
  170.0 2.9 shard_map.61
  173.2 1.7 fusion.9
  174.9 2.5 collective-permute-start.19
  178.3 2.2 collective-permute-start.22
  181.7 1.8 shard_map.65
  187.4 3.2 collective-permute-start.23
  193.0 3.2 collective-permute-start.26
  197.1 2.9 collective-permute-start.29
  201.3 2.7 collective-permute-done.28
  208.9 1.9 collective-permute-start.30
  210.7 2.7 collective-permute-done.30
  214.7 3.2 collective-permute-start.33
  218.8 3.0 collective-permute-start.36
  223.1 5.0 %collective-permute-done.35 = f32[32,512]{1,0:T(8,128)S(1)} collective-permute-done((f32[32,512]{1,0:T(8,128)S(1)}, f32[32,512]{1,0:T(8,128)S(1)}, u32[]{:S(2)}, u32[]{:S(2)}) %collective-permute-start.35) | collective-permute-done | bytes 65568 | tf_op jit(solution)/shard_map/ppermute | solution.py:48
  228.7 2.7 collective-permute-start.39
  233.0 3.0 collective-permute-done.37
  236.6 1.9 shard_map.66
  238.6 14.4 %all_to_all.51 = f32[4,16,3200]{2,1,0:T(8,128)} all-to-all(f32[4,16,3200]{2,1,0:T(8,128)} %shard_map.66), channel_id=1, replica_groups={{0,8,16,24},{32,40,48,56},{64,72,80,88},{96,104,112,120},{1,9,17,25},{3..., dimensions={0} | all-to-all | bytes 1638400 | tf_op jit(solution)/shard_map/all_to_all | solution.py:280
  253.0 2.1 shard_map.67
  256.0 3.5 collective-permute-start.40
  266.6 4.9 %collective-permute-done.42 = f32[256,128]{1,0:T(8,128)S(1)} collective-permute-done((f32[256,128]{1,0:T(8,128)S(1)}, f32[256,128]{1,0:T(8,128)S(1)}, u32[]{:S(2)}, u32[]{:S(2)}) %collective-permute-start.42) | collective-permute-done | bytes 131104 | tf_op jit(solution)/shard_map/ppermute | solution.py:48
  272.9 11.7 %all_to_all.52 = f32[16,32,256]{2,1,0:T(8,128)S(1)} all-to-all(f32[16,32,256]{2,1,0:T(8,128)S(1)} %bitcast.155), channel_id=1, replica_groups=mesh['prow'=16,'pcol'=8] {'prow'}, dimensions={0} | all-to-all | bytes 1048576 | tf_op jit(solution)/shard_map/all_to_all | solution.py:76
  284.7 13.4 %all_to_all.53 = f32[16,32,256]{2,1,0:T(8,128)S(1)} all-to-all(f32[16,32,256]{2,1,0:T(8,128)S(1)} %broadcast_in_dim.25), channel_id=1, replica_groups=mesh['prow'=16,'pcol'=8] {'prow'}, dimensions={0} | all-to-all | bytes 1048576 | tf_op jit(solution)/shard_map/all_to_all | solution.py:81
  299.6 3.7 collective-permute-start.44
  307.0 1.7 fusion.2
  310.1 4.1 %collective-permute-done.46 = f32[256,128]{1,0:T(8,128)S(1)} collective-permute-done((f32[256,128]{1,0:T(8,128)S(1)}, f32[256,128]{1,0:T(8,128)S(1)}, u32[]{:S(2)}, u32[]{:S(2)}) %collective-permute-start.46) | collective-permute-done | bytes 131104 | tf_op jit(solution)/shard_map/ppermute | solution.py:48
  317.1 18.7 %all_to_all.54 = f32[16,64,256]{2,1,0:T(8,128)S(1)} all-to-all(f32[16,64,256]{2,1,0:T(8,128)S(1)} %fusion), channel_id=1, replica_groups=mesh['prow'=16,'pcol'=8] {'prow'}, dimensions={0} | all-to-all | bytes 2097152 | tf_op jit(solution)/shard_map/all_to_all | solution.py:76
  337.1 4.4 %all-to-all-start.9 = ((f32[16,64,256]{2,1,0:T(8,128)}), f32[16,64,256]{2,1,0:T(8,128)S(1)}, u32[]{:S(2)}, u32[]{:S(2)}) async-start(f32[16,64,256]{2,1,0:T(8,128)} %broadcast_in_dim.29), calls=%async_computation.9 | async-start | bytes 2097152 | tf_op jit(solution)/shard_map/all_to_all | solution.py:81
  343.0 13.7 %all-to-all-done.9 = f32[16,64,256]{2,1,0:T(8,128)S(1)} async-done(((f32[16,64,256]{2,1,0:T(8,128)}), f32[16,64,256]{2,1,0:T(8,128)S(1)}, u32[]{:S(2)}, u32[]{:S(2)}) %all-to-all-start.9) | async-done | bytes 1048608 | tf_op jit(solution)/shard_map/all_to_all | solution.py:81
  358.5 3.2 collective-permute-start.49
  364.4 1.7 collective-permute-start.50
  366.1 4.4 %collective-permute-done.52 = f32[512,128]{1,0:T(8,128)S(1)} collective-permute-done((f32[512,128]{1,0:T(8,128)S(1)}, f32[512,128]{1,0:T(8,128)S(1)}, u32[]{:S(2)}, u32[]{:S(2)}) %collective-permute-start.52) | collective-permute-done | bytes 262176 | tf_op jit(solution)/shard_map/ppermute | solution.py:48
  370.5 2.5 collective-permute-done.51
  373.0 4.5 %collective-permute-done.50 = f32[512,128]{1,0:T(8,128)S(1)} collective-permute-done((f32[512,128]{1,0:T(8,128)S(1)}, f32[512,128]{1,0:T(8,128)S(1)}, u32[]{:S(2)}, u32[]{:S(2)}) %collective-permute-start.50) | collective-permute-done | bytes 262176 | tf_op jit(solution)/shard_map/ppermute | solution.py:48
  377.6 2.1 collective-permute-start.53
  (220 shorter events, 86.4 us)
Async XLA Ops:
  10.2 24.1 %all-to-all-start = ((f32[16,64,256]{2,1,0:T(8,128)}), f32[16,64,256]{2,1,0:T(8,128)S(1)}, u32[]{:S(2)}, u32[]{:S(2)}) async-start(f32[16,64,256]{2,1,0:T(8,128)} %fusion.20), calls=%async_computation | async-start | bytes 2097152 | tf_op jit(solution)/shard_map/all_to_all | solution.py:76
  18.7 123.5 %all-gather.3.cloned.1.call-start = ((), (), s32[]{:S(2)}) async-start(), calls=%async_computation.10 | async-start | bytes 8519680 | tf_op jit(solution)/shard_map/all_gather | solution.py:128
  20.0 55.9 %copy-start.5 = (bf16[31,256,128]{2,1,0:T(8,128)(2,1)S(1)}, bf16[31,256,128]{2,1,0:T(8,128)(2,1)}, u32[]{:S(2)}) copy-start(bf16[31,256,128]{2,1,0:T(8,128)(2,1)} %param.6) | copy-start | bytes 6094852
  35.5 18.4 %all-to-all-start.1 = ((f32[16,64,256]{2,1,0:T(8,128)}), f32[16,64,256]{2,1,0:T(8,128)S(1)}, u32[]{:S(2)}, u32[]{:S(2)}) async-start(f32[16,64,256]{2,1,0:T(8,128)} %broadcast_in_dim.20), calls=%async_computation.1 | async-start | bytes 2097152 | tf_op jit(solution)/shard_map/all_to_all | solution.py:81
  39.5 127.7 %copy-start.16 = (f32[98]{0:T(128)}, f32[98]{0:T(128)S(1)}, u32[]{:S(2)}) copy-start(f32[98]{0:T(128)S(1)} %convert_element_type.66) | copy-start | bytes 1180
  57.1 4.9 %collective-permute-start = (f32[256,128]{1,0:T(8,128)}, f32[256,128]{1,0:T(8,128)S(1)}, u32[]{:S(2)}, u32[]{:S(2)}) collective-permute-start(f32[256,128]{1,0:T(8,128)} %dynamic-slice_bitcast_fusion.2), channel_id=1, source_target_pairs={{0,1},{1,0},{2,3},{3,2},{4,5},{5,4},{6,7},{7,6},{8,9},{9,8},{10,11... | collective-permute-start | bytes 393224 | tf_op jit(solution)/shard_map/ppermute | solution.py:62
  62.1 5.3 %collective-permute-start.3 = (f32[256,128]{1,0:T(8,128)S(1)}, f32[256,128]{1,0:T(8,128)S(1)}, u32[]{:S(2)}, u32[]{:S(2)}) collective-permute-start(f32[256,128]{1,0:T(8,128)S(1)} %bitcast_add_fusion.2), channel_id=1, source_target_pairs={{0,6},{1,7},{2,0},{3,1},{4,2},{5,3},{6,4},{7,5},{8,14},{9,15},{10,... | collective-permute-start | bytes 393224 | tf_op jit(solution)/shard_map/ppermute | solution.py:48
  64.9 8.7 %collective-permute-start.2 = (f32[256,128]{1,0:T(8,128)S(1)}, f32[256,128]{1,0:T(8,128)S(1)}, u32[]{:S(2)}, u32[]{:S(2)}) collective-permute-start(f32[256,128]{1,0:T(8,128)S(1)} %bitcast_add_fusion.2), channel_id=1, source_target_pairs={{0,2},{1,3},{2,4},{3,5},{4,6},{5,7},{6,0},{7,1},{8,10},{9,11},{10,... | collective-permute-start | bytes 393224 | tf_op jit(solution)/shard_map/ppermute | solution.py:48
  64.9 8.7 %collective-permute-start.1 = (f32[256,128]{1,0:T(8,128)S(1)}, f32[256,128]{1,0:T(8,128)S(1)}, u32[]{:S(2)}, u32[]{:S(2)}) collective-permute-start(f32[256,128]{1,0:T(8,128)S(1)} %bitcast_add_fusion.2), channel_id=1, source_target_pairs={{0,4},{1,5},{2,6},{3,7},{4,0},{5,1},{6,2},{7,3},{8,12},{9,13},{10,... | collective-permute-start | bytes 393224 | tf_op jit(solution)/shard_map/ppermute | solution.py:48
  73.6 2.3 collective-permute-start.4
  78.0 15.3 %all-to-all-start.2 = ((f32[16,32,256]{2,1,0:T(8,128)}), f32[16,32,256]{2,1,0:T(8,128)}, u32[]{:S(2)}, u32[]{:S(2)}) async-start(f32[16,32,256]{2,1,0:T(8,128)} %bitcast.154), calls=%async_computation.2 | async-start | bytes 1048576 | tf_op jit(solution)/shard_map/all_to_all | solution.py:76
  95.3 14.4 %all-to-all-start.3 = ((f32[16,32,256]{2,1,0:T(8,128)}), f32[16,32,256]{2,1,0:T(8,128)S(1)}, u32[]{:S(2)}, u32[]{:S(2)}) async-start(f32[16,32,256]{2,1,0:T(8,128)} %broadcast_in_dim.21), calls=%async_computation.3 | async-start | bytes 1048576 | tf_op jit(solution)/shard_map/all_to_all | solution.py:81
  111.3 6.9 %collective-permute-start.5 = (f32[256,128]{1,0:T(8,128)S(1)}, f32[256,128]{1,0:T(8,128)S(1)}, u32[]{:S(2)}, u32[]{:S(2)}) collective-permute-start(f32[256,128]{1,0:T(8,128)S(1)} %bitcast.175), channel_id=1, source_target_pairs={{0,1},{1,0},{2,3},{3,2},{4,5},{5,4},{6,7},{7,6},{8,9},{9,8},{10,11... | collective-permute-start | bytes 393224 | tf_op jit(solution)/shard_map/ppermute | solution.py:56
  118.2 5.2 %collective-permute-start.8 = (f32[256,128]{1,0:T(8,128)S(1)}, f32[256,128]{1,0:T(8,128)S(1)}, u32[]{:S(2)}, u32[]{:S(2)}) collective-permute-start(f32[256,128]{1,0:T(8,128)S(1)} %bitcast_add_fusion.6), channel_id=1, source_target_pairs={{0,6},{1,7},{2,0},{3,1},{4,2},{5,3},{6,4},{7,5},{8,14},{9,15},{10,... | collective-permute-start | bytes 393224 | tf_op jit(solution)/shard_map/ppermute | solution.py:48
  118.5 8.8 %collective-permute-start.7 = (f32[256,128]{1,0:T(8,128)S(1)}, f32[256,128]{1,0:T(8,128)S(1)}, u32[]{:S(2)}, u32[]{:S(2)}) collective-permute-start(f32[256,128]{1,0:T(8,128)S(1)} %bitcast_add_fusion.6), channel_id=1, source_target_pairs={{0,2},{1,3},{2,4},{3,5},{4,6},{5,7},{6,0},{7,1},{8,10},{9,11},{10,... | collective-permute-start | bytes 393224 | tf_op jit(solution)/shard_map/ppermute | solution.py:48
  119.8 7.5 %collective-permute-start.6 = (f32[256,128]{1,0:T(8,128)S(1)}, f32[256,128]{1,0:T(8,128)S(1)}, u32[]{:S(2)}, u32[]{:S(2)}) collective-permute-start(f32[256,128]{1,0:T(8,128)S(1)} %bitcast_add_fusion.6), channel_id=1, source_target_pairs={{0,4},{1,5},{2,6},{3,7},{4,0},{5,1},{6,2},{7,3},{8,12},{9,13},{10,... | collective-permute-start | bytes 393224 | tf_op jit(solution)/shard_map/ppermute | solution.py:48
  142.2 6.5 %collective-permute-start.10 = (f32[64,256]{1,0:T(8,128)}, f32[64,256]{1,0:T(8,128)S(1)}, u32[]{:S(2)}, u32[]{:S(2)}) collective-permute-start(f32[64,256]{1,0:T(8,128)} %bitcast.206), channel_id=1, source_target_pairs={{0,32},{8,40},{16,48},{24,56},{32,64},{40,72},{48,80},{56,88},{64,... | collective-permute-start | bytes 196616 | tf_op jit(solution)/shard_map/ppermute | solution.py:48
  142.3 6.4 %collective-permute-start.11 = (f32[64,256]{1,0:T(8,128)}, f32[64,256]{1,0:T(8,128)S(1)}, u32[]{:S(2)}, u32[]{:S(2)}) collective-permute-start(f32[64,256]{1,0:T(8,128)} %bitcast.207), channel_id=1, source_target_pairs={{0,96},{8,104},{16,112},{24,120},{32,0},{40,8},{48,16},{56,24},{64... | collective-permute-start | bytes 196616 | tf_op jit(solution)/shard_map/ppermute | solution.py:48
  145.0 5.1 %collective-permute-start.9 = (f32[64,256]{1,0:T(8,128)}, f32[64,256]{1,0:T(8,128)S(1)}, u32[]{:S(2)}, u32[]{:S(2)}) collective-permute-start(f32[64,256]{1,0:T(8,128)} %bitcast.208), channel_id=1, source_target_pairs={{0,64},{8,72},{16,80},{24,88},{32,96},{40,104},{48,112},{56,120},{... | collective-permute-start | bytes 196616 | tf_op jit(solution)/shard_map/ppermute | solution.py:48
  150.1 85.9 %copy-start.6 = (f32[64,256]{1,0:T(8,128)}, f32[64,256]{1,0:T(8,128)S(1)}, u32[]{:S(2)}) copy-start(f32[64,256]{1,0:T(8,128)S(1)} %add_add_fusion.7) | copy-start | bytes 196612
  151.8 4.8 %collective-permute-start.12 = (f32[32,512]{1,0:T(8,128)S(1)}, f32[32,512]{1,0:T(8,128)S(1)}, u32[]{:S(2)}, u32[]{:S(2)}) collective-permute-start(f32[32,512]{1,0:T(8,128)S(1)} %bitcast.186), channel_id=1, source_target_pairs={{0,1},{1,0},{2,3},{3,2},{4,5},{5,4},{6,7},{7,6},{8,9},{9,8},{10,11... | collective-permute-start | bytes 196616 | tf_op jit(solution)/shard_map/ppermute | solution.py:56
  156.5 5.2 %collective-permute-start.15 = (f32[32,512]{1,0:T(8,128)S(1)}, f32[32,512]{1,0:T(8,128)S(1)}, u32[]{:S(2)}, u32[]{:S(2)}) collective-permute-start(f32[32,512]{1,0:T(8,128)S(1)} %bitcast_add_fusion.5), channel_id=1, source_target_pairs={{0,6},{1,7},{2,0},{3,1},{4,2},{5,3},{6,4},{7,5},{8,14},{9,15},{10,... | collective-permute-start | bytes 196616 | tf_op jit(solution)/shard_map/ppermute | solution.py:48
  157.9 4.6 %collective-permute-start.14 = (f32[32,512]{1,0:T(8,128)S(1)}, f32[32,512]{1,0:T(8,128)S(1)}, u32[]{:S(2)}, u32[]{:S(2)}) collective-permute-start(f32[32,512]{1,0:T(8,128)S(1)} %bitcast_add_fusion.5), channel_id=1, source_target_pairs={{0,2},{1,3},{2,4},{3,5},{4,6},{5,7},{6,0},{7,1},{8,10},{9,11},{10,... | collective-permute-start | bytes 196616 | tf_op jit(solution)/shard_map/ppermute | solution.py:48
  158.1 5.1 %collective-permute-start.13 = (f32[32,512]{1,0:T(8,128)S(1)}, f32[32,512]{1,0:T(8,128)S(1)}, u32[]{:S(2)}, u32[]{:S(2)}) collective-permute-start(f32[32,512]{1,0:T(8,128)S(1)} %bitcast_add_fusion.5), channel_id=1, source_target_pairs={{0,4},{1,5},{2,6},{3,7},{4,0},{5,1},{6,2},{7,3},{8,12},{9,13},{10,... | collective-permute-start | bytes 196616 | tf_op jit(solution)/shard_map/ppermute | solution.py:48
  164.5 8.4 %collective-permute-start.17 = (f32[32,256]{1,0:T(8,128)S(1)}, f32[32,256]{1,0:T(8,128)S(1)}, u32[]{:S(2)}, u32[]{:S(2)}) collective-permute-start(f32[32,256]{1,0:T(8,128)S(1)} %bitcast.197), channel_id=1, source_target_pairs={{0,32},{8,40},{16,48},{24,56},{32,64},{40,72},{48,80},{56,88},{64,... | collective-permute-start | bytes 98312 | tf_op jit(solution)/shard_map/ppermute | solution.py:48
  164.5 8.4 %collective-permute-start.18 = (f32[32,256]{1,0:T(8,128)S(1)}, f32[32,256]{1,0:T(8,128)S(1)}, u32[]{:S(2)}, u32[]{:S(2)}) collective-permute-start(f32[32,256]{1,0:T(8,128)S(1)} %bitcast.198), channel_id=1, source_target_pairs={{0,96},{8,104},{16,112},{24,120},{32,0},{40,8},{48,16},{56,24},{64... | collective-permute-start | bytes 98312 | tf_op jit(solution)/shard_map/ppermute | solution.py:48
  167.2 5.7 %collective-permute-start.16 = (f32[32,256]{1,0:T(8,128)S(1)}, f32[32,256]{1,0:T(8,128)S(1)}, u32[]{:S(2)}, u32[]{:S(2)}) collective-permute-start(f32[32,256]{1,0:T(8,128)S(1)} %bitcast.199), channel_id=1, source_target_pairs={{0,64},{8,72},{16,80},{24,88},{32,96},{40,104},{48,112},{56,120},{... | collective-permute-start | bytes 98312 | tf_op jit(solution)/shard_map/ppermute | solution.py:48
  174.9 3.4 collective-permute-start.19
  178.3 5.2 %collective-permute-start.22 = (f32[16,512]{1,0:T(8,128)S(1)}, f32[16,512]{1,0:T(8,128)S(1)}, u32[]{:S(2)}, u32[]{:S(2)}) collective-permute-start(f32[16,512]{1,0:T(8,128)S(1)} %add.243), channel_id=1, source_target_pairs={{0,6},{1,7},{2,0},{3,1},{4,2},{5,3},{6,4},{7,5},{8,14},{9,15},{10,... | collective-permute-start | bytes 98312 | tf_op jit(solution)/shard_map/ppermute | solution.py:48
  180.4 4.0 %collective-permute-start.21 = (f32[16,512]{1,0:T(8,128)S(1)}, f32[16,512]{1,0:T(8,128)S(1)}, u32[]{:S(2)}, u32[]{:S(2)}) collective-permute-start(f32[16,512]{1,0:T(8,128)S(1)} %add.243), channel_id=1, source_target_pairs={{0,2},{1,3},{2,4},{3,5},{4,6},{5,7},{6,0},{7,1},{8,10},{9,11},{10,... | collective-permute-start | bytes 98312 | tf_op jit(solution)/shard_map/ppermute | solution.py:48
  180.4 4.3 %collective-permute-start.20 = (f32[16,512]{1,0:T(8,128)S(1)}, f32[16,512]{1,0:T(8,128)S(1)}, u32[]{:S(2)}, u32[]{:S(2)}) collective-permute-start(f32[16,512]{1,0:T(8,128)S(1)} %add.243), channel_id=1, source_target_pairs={{0,4},{1,5},{2,6},{3,7},{4,0},{5,1},{6,2},{7,3},{8,12},{9,13},{10,... | collective-permute-start | bytes 98312 | tf_op jit(solution)/shard_map/ppermute | solution.py:48
  185.9 4.7 %collective-permute-start.25 = (f32[16,256]{1,0:T(8,128)S(1)}, f32[16,256]{1,0:T(8,128)S(1)}, u32[]{:S(2)}, u32[]{:S(2)}) collective-permute-start(f32[16,256]{1,0:T(8,128)S(1)} %fusion.37), channel_id=1, source_target_pairs={{0,96},{8,104},{16,112},{24,120},{32,0},{40,8},{48,16},{56,24},{64... | collective-permute-start | bytes 49160 | tf_op jit(solution)/shard_map/ppermute | solution.py:48
  187.1 3.8 collective-permute-start.24
  187.4 4.5 %collective-permute-start.23 = (f32[16,256]{1,0:T(8,128)S(1)}, f32[16,256]{1,0:T(8,128)S(1)}, u32[]{:S(2)}, u32[]{:S(2)}) collective-permute-start(f32[16,256]{1,0:T(8,128)S(1)} %fusion.37), channel_id=1, source_target_pairs={{0,64},{8,72},{16,80},{24,88},{32,96},{40,104},{48,112},{56,120},{... | collective-permute-start | bytes 49160 | tf_op jit(solution)/shard_map/ppermute | solution.py:48
  193.0 4.1 %collective-permute-start.26 = (f32[16,512]{1,0:T(8,128)S(1)}, f32[16,512]{1,0:T(8,128)S(1)}, u32[]{:S(2)}, u32[]{:S(2)}) collective-permute-start(f32[16,512]{1,0:T(8,128)S(1)} %fusion.35), channel_id=1, source_target_pairs={{0,1},{1,0},{2,3},{3,2},{4,5},{5,4},{6,7},{7,6},{8,9},{9,8},{10,11... | collective-permute-start | bytes 98312 | tf_op jit(solution)/shard_map/ppermute | solution.py:56
  197.1 4.2 %collective-permute-start.29 = (f32[16,512]{1,0:T(8,128)S(1)}, f32[16,512]{1,0:T(8,128)S(1)}, u32[]{:S(2)}, u32[]{:S(2)}) collective-permute-start(f32[16,512]{1,0:T(8,128)S(1)} %add.250), channel_id=1, source_target_pairs={{0,6},{1,7},{2,0},{3,1},{4,2},{5,3},{6,4},{7,5},{8,14},{9,15},{10,... | collective-permute-start | bytes 98312 | tf_op jit(solution)/shard_map/ppermute | solution.py:48
  200.0 4.0 %collective-permute-start.28 = (f32[16,512]{1,0:T(8,128)S(1)}, f32[16,512]{1,0:T(8,128)S(1)}, u32[]{:S(2)}, u32[]{:S(2)}) collective-permute-start(f32[16,512]{1,0:T(8,128)S(1)} %add.250), channel_id=1, source_target_pairs={{0,2},{1,3},{2,4},{3,5},{4,6},{5,7},{6,0},{7,1},{8,10},{9,11},{10,... | collective-permute-start | bytes 98312 | tf_op jit(solution)/shard_map/ppermute | solution.py:48
  200.0 4.3 %collective-permute-start.27 = (f32[16,512]{1,0:T(8,128)S(1)}, f32[16,512]{1,0:T(8,128)S(1)}, u32[]{:S(2)}, u32[]{:S(2)}) collective-permute-start(f32[16,512]{1,0:T(8,128)S(1)} %add.250), channel_id=1, source_target_pairs={{0,4},{1,5},{2,6},{3,7},{4,0},{5,1},{6,2},{7,3},{8,12},{9,13},{10,... | collective-permute-start | bytes 98312 | tf_op jit(solution)/shard_map/ppermute | solution.py:48
  206.2 4.6 %collective-permute-start.31 = (f32[32,256]{1,0:T(8,128)S(1)}, f32[32,256]{1,0:T(8,128)S(1)}, u32[]{:S(2)}, u32[]{:S(2)}) collective-permute-start(f32[32,256]{1,0:T(8,128)S(1)} %bitcast.200), channel_id=1, source_target_pairs={{0,32},{8,40},{16,48},{24,56},{32,64},{40,72},{48,80},{56,88},{64,... | collective-permute-start | bytes 98312 | tf_op jit(solution)/shard_map/ppermute | solution.py:48
  207.2 3.5 collective-permute-start.32
  208.9 4.6 %collective-permute-start.30 = (f32[32,256]{1,0:T(8,128)S(1)}, f32[32,256]{1,0:T(8,128)S(1)}, u32[]{:S(2)}, u32[]{:S(2)}) collective-permute-start(f32[32,256]{1,0:T(8,128)S(1)} %bitcast.202), channel_id=1, source_target_pairs={{0,64},{8,72},{16,80},{24,88},{32,96},{40,104},{48,112},{56,120},{... | collective-permute-start | bytes 98312 | tf_op jit(solution)/shard_map/ppermute | solution.py:48
  214.7 4.1 %collective-permute-start.33 = (f32[32,512]{1,0:T(8,128)S(1)}, f32[32,512]{1,0:T(8,128)S(1)}, u32[]{:S(2)}, u32[]{:S(2)}) collective-permute-start(f32[32,512]{1,0:T(8,128)S(1)} %bitcast.187), channel_id=1, source_target_pairs={{0,1},{1,0},{2,3},{3,2},{4,5},{5,4},{6,7},{7,6},{8,9},{9,8},{10,11... | collective-permute-start | bytes 196616 | tf_op jit(solution)/shard_map/ppermute | solution.py:56
  218.8 4.3 %collective-permute-start.36 = (f32[32,512]{1,0:T(8,128)S(1)}, f32[32,512]{1,0:T(8,128)S(1)}, u32[]{:S(2)}, u32[]{:S(2)}) collective-permute-start(f32[32,512]{1,0:T(8,128)S(1)} %bitcast_add_fusion.4), channel_id=1, source_target_pairs={{0,6},{1,7},{2,0},{3,1},{4,2},{5,3},{6,4},{7,5},{8,14},{9,15},{10,... | collective-permute-start | bytes 196616 | tf_op jit(solution)/shard_map/ppermute | solution.py:48
  221.8 6.3 %collective-permute-start.35 = (f32[32,512]{1,0:T(8,128)S(1)}, f32[32,512]{1,0:T(8,128)S(1)}, u32[]{:S(2)}, u32[]{:S(2)}) collective-permute-start(f32[32,512]{1,0:T(8,128)S(1)} %bitcast_add_fusion.4), channel_id=1, source_target_pairs={{0,2},{1,3},{2,4},{3,5},{4,6},{5,7},{6,0},{7,1},{8,10},{9,11},{10,... | collective-permute-start | bytes 196616 | tf_op jit(solution)/shard_map/ppermute | solution.py:48
  221.8 6.3 %collective-permute-start.34 = (f32[32,512]{1,0:T(8,128)S(1)}, f32[32,512]{1,0:T(8,128)S(1)}, u32[]{:S(2)}, u32[]{:S(2)}) collective-permute-start(f32[32,512]{1,0:T(8,128)S(1)} %bitcast_add_fusion.4), channel_id=1, source_target_pairs={{0,4},{1,5},{2,6},{3,7},{4,0},{5,1},{6,2},{7,3},{8,12},{9,13},{10,... | collective-permute-start | bytes 196616 | tf_op jit(solution)/shard_map/ppermute | solution.py:48
  228.7 4.3 %collective-permute-start.38 = (f32[64,256]{1,0:T(8,128)S(1)}, f32[64,256]{1,0:T(8,128)S(1)}, u32[]{:S(2)}, u32[]{:S(2)}) collective-permute-start(f32[64,256]{1,0:T(8,128)S(1)} %bitcast.183), channel_id=1, source_target_pairs={{0,32},{8,40},{16,48},{24,56},{32,64},{40,72},{48,80},{56,88},{64,... | collective-permute-start | bytes 196616 | tf_op jit(solution)/shard_map/ppermute | solution.py:48
  228.7 4.3 %collective-permute-start.39 = (f32[64,256]{1,0:T(8,128)S(1)}, f32[64,256]{1,0:T(8,128)S(1)}, u32[]{:S(2)}, u32[]{:S(2)}) collective-permute-start(f32[64,256]{1,0:T(8,128)S(1)} %bitcast.184), channel_id=1, source_target_pairs={{0,96},{8,104},{16,112},{24,120},{32,0},{40,8},{48,16},{56,24},{64... | collective-permute-start | bytes 196616 | tf_op jit(solution)/shard_map/ppermute | solution.py:48
  231.3 4.6 %collective-permute-start.37 = (f32[64,256]{1,0:T(8,128)S(1)}, f32[64,256]{1,0:T(8,128)S(1)}, u32[]{:S(2)}, u32[]{:S(2)}) collective-permute-start(f32[64,256]{1,0:T(8,128)S(1)} %bitcast.185), channel_id=1, source_target_pairs={{0,64},{8,72},{16,80},{24,88},{32,96},{40,104},{48,112},{56,120},{... | collective-permute-start | bytes 196616 | tf_op jit(solution)/shard_map/ppermute | solution.py:48
  236.6 61.4 %copy-start.3 = (f32[16,32,256]{2,1,0:T(8,128)S(1)}, f32[16,32,256]{2,1,0:T(8,128)}, u32[]{:S(2)}) copy-start(f32[16,32,256]{2,1,0:T(8,128)} %copy-done.2) | copy-start | bytes 1572868
  256.0 4.8 %collective-permute-start.40 = (f32[256,128]{1,0:T(8,128)}, f32[256,128]{1,0:T(8,128)S(1)}, u32[]{:S(2)}, u32[]{:S(2)}) collective-permute-start(f32[256,128]{1,0:T(8,128)} %bitcast.194), channel_id=1, source_target_pairs={{0,1},{1,0},{2,3},{3,2},{4,5},{5,4},{6,7},{7,6},{8,9},{9,8},{10,11... | collective-permute-start | bytes 393224 | tf_op jit(solution)/shard_map/ppermute | solution.py:56
  261.8 4.9 %collective-permute-start.43 = (f32[256,128]{1,0:T(8,128)S(1)}, f32[256,128]{1,0:T(8,128)S(1)}, u32[]{:S(2)}, u32[]{:S(2)}) collective-permute-start(f32[256,128]{1,0:T(8,128)S(1)} %bitcast_add_fusion.3), channel_id=1, source_target_pairs={{0,6},{1,7},{2,0},{3,1},{4,2},{5,3},{6,4},{7,5},{8,14},{9,15},{10,... | collective-permute-start | bytes 393224 | tf_op jit(solution)/shard_map/ppermute | solution.py:48
  262.9 8.7 %collective-permute-start.42 = (f32[256,128]{1,0:T(8,128)S(1)}, f32[256,128]{1,0:T(8,128)S(1)}, u32[]{:S(2)}, u32[]{:S(2)}) collective-permute-start(f32[256,128]{1,0:T(8,128)S(1)} %bitcast_add_fusion.3), channel_id=1, source_target_pairs={{0,2},{1,3},{2,4},{3,5},{4,6},{5,7},{6,0},{7,1},{8,10},{9,11},{10,... | collective-permute-start | bytes 393224 | tf_op jit(solution)/shard_map/ppermute | solution.py:48
  263.3 8.3 %collective-permute-start.41 = (f32[256,128]{1,0:T(8,128)S(1)}, f32[256,128]{1,0:T(8,128)S(1)}, u32[]{:S(2)}, u32[]{:S(2)}) collective-permute-start(f32[256,128]{1,0:T(8,128)S(1)} %bitcast_add_fusion.3), channel_id=1, source_target_pairs={{0,4},{1,5},{2,6},{3,7},{4,0},{5,1},{6,2},{7,3},{8,12},{9,13},{10,... | collective-permute-start | bytes 393224 | tf_op jit(solution)/shard_map/ppermute | solution.py:48
  299.6 5.2 %collective-permute-start.44 = (f32[256,128]{1,0:T(8,128)S(1)}, f32[256,128]{1,0:T(8,128)S(1)}, u32[]{:S(2)}, u32[]{:S(2)}) collective-permute-start(f32[256,128]{1,0:T(8,128)S(1)} %dynamic-slice_bitcast_fusion.1), channel_id=1, source_target_pairs={{0,1},{1,0},{2,3},{3,2},{4,5},{5,4},{6,7},{7,6},{8,9},{9,8},{10,11... | collective-permute-start | bytes 393224 | tf_op jit(solution)/shard_map/ppermute | solution.py:62
  304.9 5.2 %collective-permute-start.47 = (f32[256,128]{1,0:T(8,128)S(1)}, f32[256,128]{1,0:T(8,128)S(1)}, u32[]{:S(2)}, u32[]{:S(2)}) collective-permute-start(f32[256,128]{1,0:T(8,128)S(1)} %bitcast_add_fusion.1), channel_id=1, source_target_pairs={{0,6},{1,7},{2,0},{3,1},{4,2},{5,3},{6,4},{7,5},{8,14},{9,15},{10,... | collective-permute-start | bytes 393224 | tf_op jit(solution)/shard_map/ppermute | solution.py:48
  305.0 9.2 %collective-permute-start.46 = (f32[256,128]{1,0:T(8,128)S(1)}, f32[256,128]{1,0:T(8,128)S(1)}, u32[]{:S(2)}, u32[]{:S(2)}) collective-permute-start(f32[256,128]{1,0:T(8,128)S(1)} %bitcast_add_fusion.1), channel_id=1, source_target_pairs={{0,2},{1,3},{2,4},{3,5},{4,6},{5,7},{6,0},{7,1},{8,10},{9,11},{10,... | collective-permute-start | bytes 393224 | tf_op jit(solution)/shard_map/ppermute | solution.py:48
  306.4 7.7 %collective-permute-start.45 = (f32[256,128]{1,0:T(8,128)S(1)}, f32[256,128]{1,0:T(8,128)S(1)}, u32[]{:S(2)}, u32[]{:S(2)}) collective-permute-start(f32[256,128]{1,0:T(8,128)S(1)} %bitcast_add_fusion.1), channel_id=1, source_target_pairs={{0,4},{1,5},{2,6},{3,7},{4,0},{5,1},{6,2},{7,3},{8,12},{9,13},{10,... | collective-permute-start | bytes 393224 | tf_op jit(solution)/shard_map/ppermute | solution.py:48
  314.2 2.5 collective-permute-start.48
  337.1 19.6 %all-to-all-start.9 = ((f32[16,64,256]{2,1,0:T(8,128)}), f32[16,64,256]{2,1,0:T(8,128)S(1)}, u32[]{:S(2)}, u32[]{:S(2)}) async-start(f32[16,64,256]{2,1,0:T(8,128)} %broadcast_in_dim.29), calls=%async_computation.9 | async-start | bytes 2097152 | tf_op jit(solution)/shard_map/all_to_all | solution.py:81
  358.5 4.4 %collective-permute-start.49 = (f32[512,128]{1,0:T(8,128)S(1)}, f32[512,128]{1,0:T(8,128)S(1)}, u32[]{:S(2)}, u32[]{:S(2)}) collective-permute-start(f32[512,128]{1,0:T(8,128)S(1)} %dynamic-slice_bitcast_fusion), channel_id=1, source_target_pairs={{0,1},{1,0},{2,3},{3,2},{4,5},{5,4},{6,7},{7,6},{8,9},{9,8},{10,11... | collective-permute-start | bytes 786440 | tf_op jit(solution)/shard_map/ppermute | solution.py:62
  362.9 7.6 %collective-permute-start.52 = (f32[512,128]{1,0:T(8,128)S(1)}, f32[512,128]{1,0:T(8,128)S(1)}, u32[]{:S(2)}, u32[]{:S(2)}) collective-permute-start(f32[512,128]{1,0:T(8,128)S(1)} %bitcast_add_fusion), channel_id=1, source_target_pairs={{0,6},{1,7},{2,0},{3,1},{4,2},{5,3},{6,4},{7,5},{8,14},{9,15},{10,... | collective-permute-start | bytes 786440 | tf_op jit(solution)/shard_map/ppermute | solution.py:48
  364.0 9.0 %collective-permute-start.51 = (f32[512,128]{1,0:T(8,128)S(1)}, f32[512,128]{1,0:T(8,128)S(1)}, u32[]{:S(2)}, u32[]{:S(2)}) collective-permute-start(f32[512,128]{1,0:T(8,128)S(1)} %bitcast_add_fusion), channel_id=1, source_target_pairs={{0,2},{1,3},{2,4},{3,5},{4,6},{5,7},{6,0},{7,1},{8,10},{9,11},{10,... | collective-permute-start | bytes 786440 | tf_op jit(solution)/shard_map/ppermute | solution.py:48
  364.4 13.1 %collective-permute-start.50 = (f32[512,128]{1,0:T(8,128)S(1)}, f32[512,128]{1,0:T(8,128)S(1)}, u32[]{:S(2)}, u32[]{:S(2)}) collective-permute-start(f32[512,128]{1,0:T(8,128)S(1)} %bitcast_add_fusion), channel_id=1, source_target_pairs={{0,4},{1,5},{2,6},{3,7},{4,0},{5,1},{6,2},{7,3},{8,12},{9,13},{10,... | collective-permute-start | bytes 786440 | tf_op jit(solution)/shard_map/ppermute | solution.py:48
  377.6 3.3 collective-permute-start.53
  (19 other events, 443.5 us)
Sparse Core Ops, SparseCore 0:
  34.4 87.7 all-gather.2

commit v2 on v1

--- a/solution.py
+++ b/solution.py
@@ -85,6 +85,29 @@
     return share_rows(scatter_rows(values), values.shape)
 
 
+def resident(array, first, last, step):
+    blocks = range(first, last, step)
+
+    def kernel(source, target, arrived):
+        copies = [
+            pltpu.make_async_copy(source.at[block], target.at[i], arrived.at[i])
+            for i, block in enumerate(blocks)
+        ]
+        for copy in copies:
+            copy.start()
+        for copy in copies:
+            copy.wait()
+
+    return pl.pallas_call(
+        kernel,
+        out_shape=pltpu.VMEM((len(blocks),) + array.shape[1:], array.dtype),
+        in_specs=[pl.BlockSpec(memory_space=pltpu.HBM)],
+        out_specs=pl.BlockSpec(memory_space=pltpu.VMEM),
+        scratch_shapes=[pltpu.SemaphoreType.DMA((len(blocks),))],
+        compiler_params=pltpu.CompilerParams(vmem_limit_bytes=4 << 20),
+    )(array)
+
+
 def round_inverses(whole, count, at):
     def kernel(blocks, out):
         for i in range(count):
@@ -93,7 +116,7 @@
 
     return pl.pallas_call(
         kernel,
-        out_shape=jax.ShapeDtypeStruct((count, 256, 512), jnp.bfloat16),
+        out_shape=pltpu.VMEM((count, 256, 512), jnp.bfloat16),
         grid=(1,),
         in_specs=[pl.BlockSpec((4, count, 256, 128), lambda i: (0, at, 0, 0))],
         out_specs=pl.BlockSpec((count, 256, 512), lambda i: (0, 0, 0)),
@@ -111,7 +134,7 @@
 
     return pl.pallas_call(
         kernel,
-        out_shape=jax.ShapeDtypeStruct((count, 512, 256), jnp.bfloat16),
+        out_shape=pltpu.VMEM((count, 512, 256), jnp.bfloat16),
         grid=(1,),
         in_specs=[
             pl.BlockSpec(memory_space=pltpu.SMEM),
@@ -130,7 +153,7 @@
 
 
 def call(kernel, shapes, *operands):
-    outs = [jax.ShapeDtypeStruct(shape, jnp.float32) for shape in shapes]
+    outs = [pltpu.VMEM(shape, jnp.float32) for shape in shapes]
     return pl.pallas_call(kernel, out_shape=outs)(*operands)
 
 
@@ -154,7 +177,7 @@
     specs = [pl.BlockSpec(memory_space=pltpu.SMEM)] + [pl.BlockSpec(memory_space=pltpu.VMEM)] * 5
     return pl.pallas_call(
         kernel,
-        out_shape=jax.ShapeDtypeStruct((4, 16, 1408), jnp.float32),
+        out_shape=pltpu.VMEM((4, 16, 1408), jnp.float32),
         in_specs=specs,
     )(here.reshape(1), order, total, inverses, sums_1, sums_0)
 
@@ -209,11 +232,13 @@
     live = pattern.astype(jnp.float32)
     bf16 = jnp.bfloat16
     forward_levels = [None] * LEV
+    far = (inverse, factor)
     partial_value = [[] for _ in range(LEV)]
 
     def push_up(narrow, tree_depth):
         for upward in range(1, tree_depth + 1):
-            terms = product(narrow, blocks_of(factor, tree_depth, upward), "nrc,nwc->nrw")
+            blocks = parent_at[tree_depth] if upward == 1 else blocks_of(factor, tree_depth, upward)
+            terms = product(narrow, blocks, "nrc,nwc->nrw")
             terms = terms * blocks_of(live, tree_depth, upward)[:, None, None]
             partial_value[tree_depth - upward].append(sum_children(terms, upward))
 
@@ -222,9 +247,13 @@
         if tree_depth < LEV - 1:
             residual = residual - sum_columns(sum(partial_value[tree_depth]))
         pieces = product(residual.astype(bf16), nodes_of(inverse, tree_depth), "nrc,nwc->nrw")
+        if tree_depth == LEV - 1:
+            pieces, near, inverse = lax.optimization_barrier((pieces, factor, inverse))
+            inverse = resident(inverse, 0, 31, 1)
+            parent_at = {4: resident(near, 34, 98, 4), 3: resident(near, 10, 34, 3)}
         part = scatter_rows(pieces)
         if tree_depth == LEV - 1:
-            whole, part = gather_blocks(top_inverses(inverse), top_order(factor), part)
+            whole, part = gather_blocks(top_inverses(far[0]), top_order(far[1]), part)
         forward = share_rows(part, pieces.shape)
         forward_levels[tree_depth] = forward
         push_up(forward.astype(bf16), tree_depth)
@@ -286,7 +315,8 @@
         for lower in range(max(tree_depth + 1, TOP), LEV):
             upward = lower - tree_depth
             above = jnp.repeat(narrow, 2**upward, axis=0)
-            terms = product(above, blocks_of(factor, lower, upward), "nrw,nwc->nrc")
+            blocks = parent_at[lower] if upward == 1 else blocks_of(factor, lower, upward)
+            terms = product(above, blocks, "nrw,nwc->nrc")
             gathered[lower].append(terms * blocks_of(live, lower, upward)[:, None, None])
 
     for tree_depth in (0, 1):

time: 391 us -> 387 us (0.990)
  local copies, waits for them, and re-layouts: 10.5 us -> 19.7 us
  matrix products: 38.4 us -> 29.6 us
  waiting for transfers between devices: 117 us -> 110 us
  other arithmetic: 11.2 us -> 18 us
    unnamed x40 -> x72, local copies, waits for them, and re-layouts: 0.87 us -> 10.1 us
    dot_general x28, matrix products: 38.4 us -> 29.6 us  [product(): return jnp.einsum(form, left, right, preferred_element_type=jnp.float32)]
    all_to_all x3, waiting for transfers between devices: 31.3 us -> 26.4 us  [share_rows(): return lax.all_to_all(copies, 'prow', 0, 0).reshape(shape)]
    all_to_all x2, waiting for transfers between devices: 20.3 us -> 15.7 us  [scatter_rows(): return lax.all_to_all(chunks, 'prow', 0, 0).sum(axis=0)]
    pallas_call x6 -> x9, Pallas kernels: 13.8 us -> 13.8 us  [the longest x3 5.14 us: resident(): pl.pallas_call(kernel, out_shape=pltpu.VMEM((len(blocks),) + array.shape[...]
where the time goes in v2:
time: 387 us; the launch traced here: 385 us
  waiting for transfers between devices  110 us (28%)
  starting transfers between devices  108 us (28%)
  blocking collectives  68.1 us (18%)
  matrix products  29.6 us (8%)
  local copies, waits for them, and re-layouts  19.7 us (5%)
  other arithmetic  18 us (5%)
  Pallas kernels  17.2 us (4%)
  between operations  15.1 us (4%)
    ppermute x42, waiting for transfers between devices, sum_ring(): across, right, left = [lax.ppermute(values, axis, step) for step in ring]  60 us
    ppermute x42, starting transfers between devices, sum_ring(): across, right, left = [lax.ppermute(values, axis, step) for step in ring]  46 us
    all_to_all x2, blocking collectives, scatter_rows(): return lax.all_to_all(chunks, 'prow', 0, 0).sum(axis=0)  33 us
    dot_general x28, matrix products, product(): return jnp.einsum(form, left, right, preferred_element_type=jnp.float32)  29.6 us
    all_to_all x3, waiting for transfers between devices, share_rows(): return lax.all_to_all(copies, 'prow', 0, 0).reshape(shape)  26.4 us
    all_to_all x2, blocking collectives, per_device(): got = lax.all_to_all(sent, 'prow', 0, 0, axis_index_groups=ZGROUPS)  22.7 us
    ppermute x6, starting transfers between devices, sum_columns(): flat = flat + lax.ppermute(flat, 'pcol', TWIN)  19.5 us
    all_to_all x2, waiting for transfers between devices, scatter_rows(): return lax.all_to_all(chunks, 'prow', 0, 0).sum(axis=0)  15.7 us
  transfers between devices with their start and end apart: 60, of which 38 were waited for; matrix products, arithmetic and copies ran while one was open for 9% of the time, Pallas kernels for 4%

profile of v2, /device:TPU:1, one launch (start us, length us, event | category | flops | bytes accessed | tf_op | source)
XLA Modules:
  0.0 385.2 jit_solution(17692568077466474812)
XLA Ops:
  7.2 2.9 fusion.12
  10.1 8.6 %all-to-all-start = ((f32[16,64,256]{2,1,0:T(8,128)}), f32[16,64,256]{2,1,0:T(8,128)S(1)}, u32[]{:S(2)}, u32[]{:S(2)}) async-start(f32[16,64,256]{2,1,0:T(8,128)} %fusion.12), calls=%async_computation | async-start | bytes 2097152 | tf_op jit(solution)/shard_map/all_to_all | solution.py:76
  21.3 12.9 %all-to-all-done = f32[16,64,256]{2,1,0:T(8,128)S(1)} async-done(((f32[16,64,256]{2,1,0:T(8,128)}), f32[16,64,256]{2,1,0:T(8,128)S(1)}, u32[]{:S(2)}, u32[]{:S(2)}) %all-to-all-start) | async-done | bytes 1048608 | tf_op jit(solution)/shard_map/all_to_all | solution.py:76
  35.4 4.0 %all-to-all-start.1 = ((f32[16,64,256]{2,1,0:T(8,128)}), f32[16,64,256]{2,1,0:T(8,128)S(1)}, u32[]{:S(2)}, u32[]{:S(2)}) async-start(f32[16,64,256]{2,1,0:T(8,128)} %broadcast_in_dim.20), calls=%async_computation.1 | async-start | bytes 2097152 | tf_op jit(solution)/shard_map/all_to_all | solution.py:81
  39.6 2.8 copy-done
  43.9 9.9 %all-to-all-done.1 = f32[16,64,256]{2,1,0:T(8,128)S(1)} async-done(((f32[16,64,256]{2,1,0:T(8,128)}), f32[16,64,256]{2,1,0:T(8,128)S(1)}, u32[]{:S(2)}, u32[]{:S(2)}) %all-to-all-start.1) | async-done | bytes 1048608 | tf_op jit(solution)/shard_map/all_to_all | solution.py:81
  54.4 3.8 collective-permute-start
  59.2 2.8 collective-permute-start.3
  62.0 1.6 collective-permute-start.1
  64.5 6.2 %collective-permute-done.2 = f32[256,128]{1,0:T(8,128)S(1)} collective-permute-done((f32[256,128]{1,0:T(8,128)S(1)}, f32[256,128]{1,0:T(8,128)S(1)}, u32[]{:S(2)}, u32[]{:S(2)}) %collective-permute-start.2) | collective-permute-done | bytes 131104 | tf_op jit(solution)/shard_map/ppermute | solution.py:48
  73.7 2.9 shard_map.60
  76.6 2.3 fusion.25
  78.9 4.9 %all-to-all-start.2 = ((f32[16,32,256]{2,1,0:T(8,128)}), f32[16,32,256]{2,1,0:T(8,128)}, u32[]{:S(2)}, u32[]{:S(2)}) async-start(f32[16,32,256]{2,1,0:T(8,128)} %bitcast.159), calls=%async_computation.2 | async-start | bytes 1048576 | tf_op jit(solution)/shard_map/all_to_all | solution.py:76
  84.4 1.7 slice.104.order
  86.1 2.8 copy-done.1
  91.2 2.9 all-to-all-done.2
  96.0 5.7 %all-to-all-start.3 = ((f32[16,32,256]{2,1,0:T(8,128)}), f32[16,32,256]{2,1,0:T(8,128)}, u32[]{:S(2)}, u32[]{:S(2)}) async-start(f32[16,32,256]{2,1,0:T(8,128)} %broadcast_in_dim.21), calls=%async_computation.3 | async-start | bytes 1048576 | tf_op jit(solution)/shard_map/all_to_all | solution.py:81
  101.7 1.9 fusion.5
  103.6 1.9 bitcast_reduce_fusion
  105.5 1.9 bitcast_reduce_fusion.2
  107.4 4.6 %all-to-all-done.3 = f32[16,32,256]{2,1,0:T(8,128)} async-done(((f32[16,32,256]{2,1,0:T(8,128)}), f32[16,32,256]{2,1,0:T(8,128)}, u32[]{:S(2)}, u32[]{:S(2)}) %all-to-all-start.3) | async-done | bytes 524320 | tf_op jit(solution)/shard_map/all_to_all | solution.py:81
  113.4 2.3 collective-permute-start.5
  121.6 2.7 collective-permute-done.8
  124.3 3.9 %collective-permute-done.7 = f32[256,128]{1,0:T(8,128)S(1)} collective-permute-done((f32[256,128]{1,0:T(8,128)S(1)}, f32[256,128]{1,0:T(8,128)S(1)}, u32[]{:S(2)}, u32[]{:S(2)}) %collective-permute-start.7) | collective-permute-done | bytes 131104 | tf_op jit(solution)/shard_map/ppermute | solution.py:48
  130.2 9.4 %all_to_all.50.got = f32[4,16,1408]{2,1,0:T(8,128)} all-to-all(f32[4,16,1408]{2,1,0:T(8,128)S(1)} %shard_map.62), channel_id=1, replica_groups={{0,8,16,24},{32,40,48,56},{64,72,80,88},{96,104,112,120},{1,9,17,25},{3..., dimensions={0} | all-to-all | bytes 720896 | tf_op jit(solution)/shard_map/all_to_all | solution.py:266
  140.7 2.7 collective-permute-start.11
  144.2 1.8 shard_map.65
  146.0 2.3 collective-permute-done.9
  148.7 3.9 %collective-permute-start.12 = (f32[32,512]{1,0:T(8,128)S(1)}, f32[32,512]{1,0:T(8,128)S(1)}, u32[]{:S(2)}, u32[]{:S(2)}) collective-permute-start(f32[32,512]{1,0:T(8,128)S(1)} %bitcast.193), channel_id=1, source_target_pairs={{0,1},{1,0},{2,3},{3,2},{4,5},{5,4},{6,7},{7,6},{8,9},{9,8},{10,11... | collective-permute-start | bytes 196616 | tf_op jit(solution)/shard_map/ppermute | solution.py:56
  160.4 2.7 collective-permute-start.18
  165.9 1.8 shard_map.64
  169.7 3.0 collective-permute-start.19
  173.6 2.2 collective-permute-start.22
  178.1 1.6 collective-permute-done.21
  181.8 2.7 collective-permute-start.23
  186.0 3.5 collective-permute-start.26
  190.4 2.9 collective-permute-start.29
  194.5 2.7 collective-permute-done.28
  200.1 2.0 collective-permute-start.32
  203.6 3.0 collective-permute-done.30
  206.8 3.3 collective-permute-start.33
  211.0 3.0 collective-permute-start.36
  215.3 5.0 %collective-permute-done.35 = f32[32,512]{1,0:T(8,128)S(1)} collective-permute-done((f32[32,512]{1,0:T(8,128)S(1)}, f32[32,512]{1,0:T(8,128)S(1)}, u32[]{:S(2)}, u32[]{:S(2)}) %collective-permute-start.35) | collective-permute-done | bytes 65568 | tf_op jit(solution)/shard_map/ppermute | solution.py:48
  222.1 2.7 collective-permute-start.39
  226.4 3.0 collective-permute-done.37
  231.1 13.3 %all_to_all.51 = f32[4,16,3200]{2,1,0:T(8,128)} all-to-all(f32[4,16,3200]{2,1,0:T(8,128)S(1)} %shard_map.69), channel_id=1, replica_groups={{0,8,16,24},{32,40,48,56},{64,72,80,88},{96,104,112,120},{1,9,17,25},{3..., dimensions={0} | all-to-all | bytes 1638400 | tf_op jit(solution)/shard_map/all_to_all | solution.py:309
  245.8 3.5 collective-permute-start.40
  255.8 4.8 %collective-permute-done.42 = f32[256,128]{1,0:T(8,128)S(1)} collective-permute-done((f32[256,128]{1,0:T(8,128)S(1)}, f32[256,128]{1,0:T(8,128)S(1)}, u32[]{:S(2)}, u32[]{:S(2)}) %collective-permute-start.42) | collective-permute-done | bytes 131104 | tf_op jit(solution)/shard_map/ppermute | solution.py:48
  262.6 13.4 %all_to_all.52 = f32[16,32,256]{2,1,0:T(8,128)} all-to-all(f32[16,32,256]{2,1,0:T(8,128)S(1)} %bitcast.160), channel_id=1, replica_groups=mesh['prow'=16,'pcol'=8] {'prow'}, dimensions={0} | all-to-all | bytes 1048576 | tf_op jit(solution)/shard_map/all_to_all | solution.py:76
  276.0 1.7 reduce_sum.132
  278.5 12.5 %all_to_all.53 = f32[16,32,256]{2,1,0:T(8,128)S(1)} all-to-all(f32[16,32,256]{2,1,0:T(8,128)S(1)} %broadcast_in_dim.25), channel_id=1, replica_groups=mesh['prow'=16,'pcol'=8] {'prow'}, dimensions={0} | all-to-all | bytes 1048576 | tf_op jit(solution)/shard_map/all_to_all | solution.py:81
  293.6 3.5 collective-permute-start.44
  303.9 4.1 %collective-permute-done.46 = f32[256,128]{1,0:T(8,128)S(1)} collective-permute-done((f32[256,128]{1,0:T(8,128)S(1)}, f32[256,128]{1,0:T(8,128)S(1)}, u32[]{:S(2)}, u32[]{:S(2)}) %collective-permute-start.46) | collective-permute-done | bytes 131104 | tf_op jit(solution)/shard_map/ppermute | solution.py:48
  311.0 19.5 %all_to_all.54 = f32[16,64,256]{2,1,0:T(8,128)} all-to-all(f32[16,64,256]{2,1,0:T(8,128)S(1)} %fusion), channel_id=1, replica_groups=mesh['prow'=16,'pcol'=8] {'prow'}, dimensions={0} | all-to-all | bytes 2097152 | tf_op jit(solution)/shard_map/all_to_all | solution.py:76
  332.9 4.3 %all-to-all-start.9 = ((f32[16,64,256]{2,1,0:T(8,128)}), f32[16,64,256]{2,1,0:T(8,128)}, u32[]{:S(2)}, u32[]{:S(2)}) async-start(f32[16,64,256]{2,1,0:T(8,128)} %broadcast_in_dim.29), calls=%async_computation.9 | async-start | bytes 2097152 | tf_op jit(solution)/shard_map/all_to_all | solution.py:81
  337.2 3.0 pad_maximum_fusion
  340.2 11.9 %all-to-all-done.9 = f32[16,64,256]{2,1,0:T(8,128)} async-done(((f32[16,64,256]{2,1,0:T(8,128)}), f32[16,64,256]{2,1,0:T(8,128)}, u32[]{:S(2)}, u32[]{:S(2)}) %all-to-all-start.9) | async-done | bytes 1048608 | tf_op jit(solution)/shard_map/all_to_all | solution.py:81
  353.9 3.2 collective-permute-start.49
  359.8 1.7 collective-permute-start.50
  361.5 4.4 %collective-permute-done.52 = f32[512,128]{1,0:T(8,128)S(1)} collective-permute-done((f32[512,128]{1,0:T(8,128)S(1)}, f32[512,128]{1,0:T(8,128)S(1)}, u32[]{:S(2)}, u32[]{:S(2)}) %collective-permute-start.52) | collective-permute-done | bytes 262176 | tf_op jit(solution)/shard_map/ppermute | solution.py:48
  365.9 2.6 collective-permute-done.51
  368.5 4.4 %collective-permute-done.50 = f32[512,128]{1,0:T(8,128)S(1)} collective-permute-done((f32[512,128]{1,0:T(8,128)S(1)}, f32[512,128]{1,0:T(8,128)S(1)}, u32[]{:S(2)}, u32[]{:S(2)}) %collective-permute-start.50) | collective-permute-done | bytes 262176 | tf_op jit(solution)/shard_map/ppermute | solution.py:48
  373.0 2.2 collective-permute-start.53
  376.4 2.0 pad_maximum_fusion.1
  (255 shorter events, 91.3 us)
Async XLA Ops:
  10.1 24.1 %all-to-all-start = ((f32[16,64,256]{2,1,0:T(8,128)}), f32[16,64,256]{2,1,0:T(8,128)S(1)}, u32[]{:S(2)}, u32[]{:S(2)}) async-start(f32[16,64,256]{2,1,0:T(8,128)} %fusion.12), calls=%async_computation | async-start | bytes 2097152 | tf_op jit(solution)/shard_map/all_to_all | solution.py:76
  18.7 122.0 %all-gather.3.cloned.1.call-start = ((), (), s32[]{:S(2)}) async-start(), calls=%async_computation.10 | async-start | bytes 8519680 | tf_op jit(solution)/shard_map/all_gather | solution.py:151
  35.4 18.4 %all-to-all-start.1 = ((f32[16,64,256]{2,1,0:T(8,128)}), f32[16,64,256]{2,1,0:T(8,128)S(1)}, u32[]{:S(2)}, u32[]{:S(2)}) async-start(f32[16,64,256]{2,1,0:T(8,128)} %broadcast_in_dim.20), calls=%async_computation.1 | async-start | bytes 2097152 | tf_op jit(solution)/shard_map/all_to_all | solution.py:81
  39.4 123.7 %copy-start.32 = (f32[98]{0:T(128)}, f32[98]{0:T(128)S(1)}, u32[]{:S(2)}) copy-start(f32[98]{0:T(128)S(1)} %convert_element_type.66) | copy-start | bytes 1180
  54.4 4.8 %collective-permute-start = (f32[256,128]{1,0:T(8,128)S(1)}, f32[256,128]{1,0:T(8,128)S(1)}, u32[]{:S(2)}, u32[]{:S(2)}) collective-permute-start(f32[256,128]{1,0:T(8,128)S(1)} %dynamic-slice_bitcast_fusion.2), channel_id=1, source_target_pairs={{0,1},{1,0},{2,3},{3,2},{4,5},{5,4},{6,7},{7,6},{8,9},{9,8},{10,11... | collective-permute-start | bytes 393224 | tf_op jit(solution)/shard_map/ppermute | solution.py:62
  59.2 5.3 %collective-permute-start.3 = (f32[256,128]{1,0:T(8,128)S(1)}, f32[256,128]{1,0:T(8,128)S(1)}, u32[]{:S(2)}, u32[]{:S(2)}) collective-permute-start(f32[256,128]{1,0:T(8,128)S(1)} %bitcast_add_fusion.2), channel_id=1, source_target_pairs={{0,6},{1,7},{2,0},{3,1},{4,2},{5,3},{6,4},{7,5},{8,14},{9,15},{10,... | collective-permute-start | bytes 393224 | tf_op jit(solution)/shard_map/ppermute | solution.py:48
  62.0 8.7 %collective-permute-start.2 = (f32[256,128]{1,0:T(8,128)S(1)}, f32[256,128]{1,0:T(8,128)S(1)}, u32[]{:S(2)}, u32[]{:S(2)}) collective-permute-start(f32[256,128]{1,0:T(8,128)S(1)} %bitcast_add_fusion.2), channel_id=1, source_target_pairs={{0,2},{1,3},{2,4},{3,5},{4,6},{5,7},{6,0},{7,1},{8,10},{9,11},{10,... | collective-permute-start | bytes 393224 | tf_op jit(solution)/shard_map/ppermute | solution.py:48
  62.0 8.7 %collective-permute-start.1 = (f32[256,128]{1,0:T(8,128)S(1)}, f32[256,128]{1,0:T(8,128)S(1)}, u32[]{:S(2)}, u32[]{:S(2)}) collective-permute-start(f32[256,128]{1,0:T(8,128)S(1)} %bitcast_add_fusion.2), channel_id=1, source_target_pairs={{0,4},{1,5},{2,6},{3,7},{4,0},{5,1},{6,2},{7,3},{8,12},{9,13},{10,... | collective-permute-start | bytes 393224 | tf_op jit(solution)/shard_map/ppermute | solution.py:48
  70.8 5.8 %collective-permute-start.4 = (f32[256,128]{1,0:T(8,128)S(1)}, f32[256,128]{1,0:T(8,128)S(1)}, u32[]{:S(2)}, u32[]{:S(2)}) collective-permute-start(f32[256,128]{1,0:T(8,128)S(1)} %add_add_fusion.4), channel_id=1, source_target_pairs={{0,1},{1,0},{2,3},{3,2},{4,5},{5,4},{6,7},{7,6},{8,9},{9,8},{10,11... | collective-permute-start | bytes 393224 | tf_op jit(solution)/shard_map/ppermute | solution.py:64
  78.9 15.1 %all-to-all-start.2 = ((f32[16,32,256]{2,1,0:T(8,128)}), f32[16,32,256]{2,1,0:T(8,128)}, u32[]{:S(2)}, u32[]{:S(2)}) async-start(f32[16,32,256]{2,1,0:T(8,128)} %bitcast.159), calls=%async_computation.2 | async-start | bytes 1048576 | tf_op jit(solution)/shard_map/all_to_all | solution.py:76
  96.0 16.1 %all-to-all-start.3 = ((f32[16,32,256]{2,1,0:T(8,128)}), f32[16,32,256]{2,1,0:T(8,128)}, u32[]{:S(2)}, u32[]{:S(2)}) async-start(f32[16,32,256]{2,1,0:T(8,128)} %broadcast_in_dim.21), calls=%async_computation.3 | async-start | bytes 1048576 | tf_op jit(solution)/shard_map/all_to_all | solution.py:81
  113.4 5.6 %collective-permute-start.5 = (f32[256,128]{1,0:T(8,128)S(1)}, f32[256,128]{1,0:T(8,128)S(1)}, u32[]{:S(2)}, u32[]{:S(2)}) collective-permute-start(f32[256,128]{1,0:T(8,128)S(1)} %bitcast.182), channel_id=1, source_target_pairs={{0,1},{1,0},{2,3},{3,2},{4,5},{5,4},{6,7},{7,6},{8,9},{9,8},{10,11... | collective-permute-start | bytes 393224 | tf_op jit(solution)/shard_map/ppermute | solution.py:56
  119.1 5.2 %collective-permute-start.8 = (f32[256,128]{1,0:T(8,128)S(1)}, f32[256,128]{1,0:T(8,128)S(1)}, u32[]{:S(2)}, u32[]{:S(2)}) collective-permute-start(f32[256,128]{1,0:T(8,128)S(1)} %bitcast_add_fusion.6), channel_id=1, source_target_pairs={{0,6},{1,7},{2,0},{3,1},{4,2},{5,3},{6,4},{7,5},{8,14},{9,15},{10,... | collective-permute-start | bytes 393224 | tf_op jit(solution)/shard_map/ppermute | solution.py:48
  119.4 8.8 %collective-permute-start.7 = (f32[256,128]{1,0:T(8,128)S(1)}, f32[256,128]{1,0:T(8,128)S(1)}, u32[]{:S(2)}, u32[]{:S(2)}) collective-permute-start(f32[256,128]{1,0:T(8,128)S(1)} %bitcast_add_fusion.6), channel_id=1, source_target_pairs={{0,2},{1,3},{2,4},{3,5},{4,6},{5,7},{6,0},{7,1},{8,10},{9,11},{10,... | collective-permute-start | bytes 393224 | tf_op jit(solution)/shard_map/ppermute | solution.py:48
  120.6 7.5 %collective-permute-start.6 = (f32[256,128]{1,0:T(8,128)S(1)}, f32[256,128]{1,0:T(8,128)S(1)}, u32[]{:S(2)}, u32[]{:S(2)}) collective-permute-start(f32[256,128]{1,0:T(8,128)S(1)} %bitcast_add_fusion.6), channel_id=1, source_target_pairs={{0,4},{1,5},{2,6},{3,7},{4,0},{5,1},{6,2},{7,3},{8,12},{9,13},{10,... | collective-permute-start | bytes 393224 | tf_op jit(solution)/shard_map/ppermute | solution.py:48
  140.7 5.3 %collective-permute-start.10 = (f32[64,256]{1,0:T(8,128)S(1)}, f32[64,256]{1,0:T(8,128)S(1)}, u32[]{:S(2)}, u32[]{:S(2)}) collective-permute-start(f32[64,256]{1,0:T(8,128)S(1)} %bitcast.147), channel_id=1, source_target_pairs={{0,32},{8,40},{16,48},{24,56},{32,64},{40,72},{48,80},{56,88},{64,... | collective-permute-start | bytes 196616 | tf_op jit(solution)/shard_map/ppermute | solution.py:48
  140.7 5.2 %collective-permute-start.11 = (f32[64,256]{1,0:T(8,128)S(1)}, f32[64,256]{1,0:T(8,128)S(1)}, u32[]{:S(2)}, u32[]{:S(2)}) collective-permute-start(f32[64,256]{1,0:T(8,128)S(1)} %bitcast.148), channel_id=1, source_target_pairs={{0,96},{8,104},{16,112},{24,120},{32,0},{40,8},{48,16},{56,24},{64... | collective-permute-start | bytes 196616 | tf_op jit(solution)/shard_map/ppermute | solution.py:48
  143.4 4.9 %collective-permute-start.9 = (f32[64,256]{1,0:T(8,128)S(1)}, f32[64,256]{1,0:T(8,128)S(1)}, u32[]{:S(2)}, u32[]{:S(2)}) collective-permute-start(f32[64,256]{1,0:T(8,128)S(1)} %bitcast.149), channel_id=1, source_target_pairs={{0,64},{8,72},{16,80},{24,88},{32,96},{40,104},{48,112},{56,120},{... | collective-permute-start | bytes 196616 | tf_op jit(solution)/shard_map/ppermute | solution.py:48
  148.3 81.1 %copy-start.16 = (f32[64,256]{1,0:T(8,128)}, f32[64,256]{1,0:T(8,128)S(1)}, u32[]{:S(2)}) copy-start(f32[64,256]{1,0:T(8,128)S(1)} %add_add_fusion.7) | copy-start | bytes 196612
  148.7 4.8 %collective-permute-start.12 = (f32[32,512]{1,0:T(8,128)S(1)}, f32[32,512]{1,0:T(8,128)S(1)}, u32[]{:S(2)}, u32[]{:S(2)}) collective-permute-start(f32[32,512]{1,0:T(8,128)S(1)} %bitcast.193), channel_id=1, source_target_pairs={{0,1},{1,0},{2,3},{3,2},{4,5},{5,4},{6,7},{7,6},{8,9},{9,8},{10,11... | collective-permute-start | bytes 196616 | tf_op jit(solution)/shard_map/ppermute | solution.py:56
  153.5 4.4 %collective-permute-start.15 = (f32[32,512]{1,0:T(8,128)S(1)}, f32[32,512]{1,0:T(8,128)S(1)}, u32[]{:S(2)}, u32[]{:S(2)}) collective-permute-start(f32[32,512]{1,0:T(8,128)S(1)} %bitcast_add_fusion.5), channel_id=1, source_target_pairs={{0,6},{1,7},{2,0},{3,1},{4,2},{5,3},{6,4},{7,5},{8,14},{9,15},{10,... | collective-permute-start | bytes 196616 | tf_op jit(solution)/shard_map/ppermute | solution.py:48
  154.9 4.6 %collective-permute-start.14 = (f32[32,512]{1,0:T(8,128)S(1)}, f32[32,512]{1,0:T(8,128)S(1)}, u32[]{:S(2)}, u32[]{:S(2)}) collective-permute-start(f32[32,512]{1,0:T(8,128)S(1)} %bitcast_add_fusion.5), channel_id=1, source_target_pairs={{0,2},{1,3},{2,4},{3,5},{4,6},{5,7},{6,0},{7,1},{8,10},{9,11},{10,... | collective-permute-start | bytes 196616 | tf_op jit(solution)/shard_map/ppermute | solution.py:48
  155.1 5.1 %collective-permute-start.13 = (f32[32,512]{1,0:T(8,128)S(1)}, f32[32,512]{1,0:T(8,128)S(1)}, u32[]{:S(2)}, u32[]{:S(2)}) collective-permute-start(f32[32,512]{1,0:T(8,128)S(1)} %bitcast_add_fusion.5), channel_id=1, source_target_pairs={{0,4},{1,5},{2,6},{3,7},{4,0},{5,1},{6,2},{7,3},{8,12},{9,13},{10,... | collective-permute-start | bytes 196616 | tf_op jit(solution)/shard_map/ppermute | solution.py:48
  160.4 7.2 %collective-permute-start.17 = (f32[32,256]{1,0:T(8,128)S(1)}, f32[32,256]{1,0:T(8,128)S(1)}, u32[]{:S(2)}, u32[]{:S(2)}) collective-permute-start(f32[32,256]{1,0:T(8,128)S(1)} %bitcast.201), channel_id=1, source_target_pairs={{0,32},{8,40},{16,48},{24,56},{32,64},{40,72},{48,80},{56,88},{64,... | collective-permute-start | bytes 98312 | tf_op jit(solution)/shard_map/ppermute | solution.py:48
  160.4 7.2 %collective-permute-start.18 = (f32[32,256]{1,0:T(8,128)S(1)}, f32[32,256]{1,0:T(8,128)S(1)}, u32[]{:S(2)}, u32[]{:S(2)}) collective-permute-start(f32[32,256]{1,0:T(8,128)S(1)} %bitcast.202), channel_id=1, source_target_pairs={{0,96},{8,104},{16,112},{24,120},{32,0},{40,8},{48,16},{56,24},{64... | collective-permute-start | bytes 98312 | tf_op jit(solution)/shard_map/ppermute | solution.py:48
  163.1 4.6 %collective-permute-start.16 = (f32[32,256]{1,0:T(8,128)S(1)}, f32[32,256]{1,0:T(8,128)S(1)}, u32[]{:S(2)}, u32[]{:S(2)}) collective-permute-start(f32[32,256]{1,0:T(8,128)S(1)} %bitcast.203), channel_id=1, source_target_pairs={{0,64},{8,72},{16,80},{24,88},{32,96},{40,104},{48,112},{56,120},{... | collective-permute-start | bytes 98312 | tf_op jit(solution)/shard_map/ppermute | solution.py:48
  167.7 52.9 %copy-start.20 = (f32[32,256]{1,0:T(8,128)}, f32[32,256]{1,0:T(8,128)S(1)}, u32[]{:S(2)}) copy-start(f32[32,256]{1,0:T(8,128)S(1)} %add_add_fusion.10) | copy-start | bytes 98308
  169.7 3.9 %collective-permute-start.19 = (f32[16,512]{1,0:T(8,128)S(1)}, f32[16,512]{1,0:T(8,128)S(1)}, u32[]{:S(2)}, u32[]{:S(2)}) collective-permute-start(f32[16,512]{1,0:T(8,128)S(1)} %fusion.9), channel_id=1, source_target_pairs={{0,1},{1,0},{2,3},{3,2},{4,5},{5,4},{6,7},{7,6},{8,9},{9,8},{10,11... | collective-permute-start | bytes 98312 | tf_op jit(solution)/shard_map/ppermute | solution.py:56
  173.6 4.5 %collective-permute-start.22 = (f32[16,512]{1,0:T(8,128)S(1)}, f32[16,512]{1,0:T(8,128)S(1)}, u32[]{:S(2)}, u32[]{:S(2)}) collective-permute-start(f32[16,512]{1,0:T(8,128)S(1)} %add.243), channel_id=1, source_target_pairs={{0,6},{1,7},{2,0},{3,1},{4,2},{5,3},{6,4},{7,5},{8,14},{9,15},{10,... | collective-permute-start | bytes 98312 | tf_op jit(solution)/shard_map/ppermute | solution.py:48
  175.8 4.0 %collective-permute-start.21 = (f32[16,512]{1,0:T(8,128)S(1)}, f32[16,512]{1,0:T(8,128)S(1)}, u32[]{:S(2)}, u32[]{:S(2)}) collective-permute-start(f32[16,512]{1,0:T(8,128)S(1)} %add.243), channel_id=1, source_target_pairs={{0,2},{1,3},{2,4},{3,5},{4,6},{5,7},{6,0},{7,1},{8,10},{9,11},{10,... | collective-permute-start | bytes 98312 | tf_op jit(solution)/shard_map/ppermute | solution.py:48
  175.8 4.3 %collective-permute-start.20 = (f32[16,512]{1,0:T(8,128)S(1)}, f32[16,512]{1,0:T(8,128)S(1)}, u32[]{:S(2)}, u32[]{:S(2)}) collective-permute-start(f32[16,512]{1,0:T(8,128)S(1)} %add.243), channel_id=1, source_target_pairs={{0,4},{1,5},{2,6},{3,7},{4,0},{5,1},{6,2},{7,3},{8,12},{9,13},{10,... | collective-permute-start | bytes 98312 | tf_op jit(solution)/shard_map/ppermute | solution.py:48
  180.3 4.2 %collective-permute-start.25 = (f32[16,256]{1,0:T(8,128)S(1)}, f32[16,256]{1,0:T(8,128)S(1)}, u32[]{:S(2)}, u32[]{:S(2)}) collective-permute-start(f32[16,256]{1,0:T(8,128)S(1)} %fusion.33), channel_id=1, source_target_pairs={{0,96},{8,104},{16,112},{24,120},{32,0},{40,8},{48,16},{56,24},{64... | collective-permute-start | bytes 49160 | tf_op jit(solution)/shard_map/ppermute | solution.py:48
  181.2 3.8 collective-permute-start.24
  181.8 4.1 %collective-permute-start.23 = (f32[16,256]{1,0:T(8,128)S(1)}, f32[16,256]{1,0:T(8,128)S(1)}, u32[]{:S(2)}, u32[]{:S(2)}) collective-permute-start(f32[16,256]{1,0:T(8,128)S(1)} %fusion.33), channel_id=1, source_target_pairs={{0,64},{8,72},{16,80},{24,88},{32,96},{40,104},{48,112},{56,120},{... | collective-permute-start | bytes 49160 | tf_op jit(solution)/shard_map/ppermute | solution.py:48
  186.0 4.4 %collective-permute-start.26 = (f32[16,512]{1,0:T(8,128)S(1)}, f32[16,512]{1,0:T(8,128)S(1)}, u32[]{:S(2)}, u32[]{:S(2)}) collective-permute-start(f32[16,512]{1,0:T(8,128)S(1)} %fusion.31), channel_id=1, source_target_pairs={{0,1},{1,0},{2,3},{3,2},{4,5},{5,4},{6,7},{7,6},{8,9},{9,8},{10,11... | collective-permute-start | bytes 98312 | tf_op jit(solution)/shard_map/ppermute | solution.py:56
  190.4 4.2 %collective-permute-start.29 = (f32[16,512]{1,0:T(8,128)S(1)}, f32[16,512]{1,0:T(8,128)S(1)}, u32[]{:S(2)}, u32[]{:S(2)}) collective-permute-start(f32[16,512]{1,0:T(8,128)S(1)} %add.250), channel_id=1, source_target_pairs={{0,6},{1,7},{2,0},{3,1},{4,2},{5,3},{6,4},{7,5},{8,14},{9,15},{10,... | collective-permute-start | bytes 98312 | tf_op jit(solution)/shard_map/ppermute | solution.py:48
  193.3 4.0 %collective-permute-start.28 = (f32[16,512]{1,0:T(8,128)S(1)}, f32[16,512]{1,0:T(8,128)S(1)}, u32[]{:S(2)}, u32[]{:S(2)}) collective-permute-start(f32[16,512]{1,0:T(8,128)S(1)} %add.250), channel_id=1, source_target_pairs={{0,2},{1,3},{2,4},{3,5},{4,6},{5,7},{6,0},{7,1},{8,10},{9,11},{10,... | collective-permute-start | bytes 98312 | tf_op jit(solution)/shard_map/ppermute | solution.py:48
  193.3 4.3 %collective-permute-start.27 = (f32[16,512]{1,0:T(8,128)S(1)}, f32[16,512]{1,0:T(8,128)S(1)}, u32[]{:S(2)}, u32[]{:S(2)}) collective-permute-start(f32[16,512]{1,0:T(8,128)S(1)} %add.250), channel_id=1, source_target_pairs={{0,4},{1,5},{2,6},{3,7},{4,0},{5,1},{6,2},{7,3},{8,12},{9,13},{10,... | collective-permute-start | bytes 98312 | tf_op jit(solution)/shard_map/ppermute | solution.py:48
  199.4 4.2 %collective-permute-start.31 = (f32[32,256]{1,0:T(8,128)S(1)}, f32[32,256]{1,0:T(8,128)S(1)}, u32[]{:S(2)}, u32[]{:S(2)}) collective-permute-start(f32[32,256]{1,0:T(8,128)S(1)} %bitcast.204), channel_id=1, source_target_pairs={{0,32},{8,40},{16,48},{24,56},{32,64},{40,72},{48,80},{56,88},{64,... | collective-permute-start | bytes 98312 | tf_op jit(solution)/shard_map/ppermute | solution.py:48
  200.1 3.5 collective-permute-start.32
  202.1 4.5 %collective-permute-start.30 = (f32[32,256]{1,0:T(8,128)S(1)}, f32[32,256]{1,0:T(8,128)S(1)}, u32[]{:S(2)}, u32[]{:S(2)}) collective-permute-start(f32[32,256]{1,0:T(8,128)S(1)} %bitcast.206), channel_id=1, source_target_pairs={{0,64},{8,72},{16,80},{24,88},{32,96},{40,104},{48,112},{56,120},{... | collective-permute-start | bytes 98312 | tf_op jit(solution)/shard_map/ppermute | solution.py:48
  206.8 4.2 %collective-permute-start.33 = (f32[32,512]{1,0:T(8,128)S(1)}, f32[32,512]{1,0:T(8,128)S(1)}, u32[]{:S(2)}, u32[]{:S(2)}) collective-permute-start(f32[32,512]{1,0:T(8,128)S(1)} %bitcast.194), channel_id=1, source_target_pairs={{0,1},{1,0},{2,3},{3,2},{4,5},{5,4},{6,7},{7,6},{8,9},{9,8},{10,11... | collective-permute-start | bytes 196616 | tf_op jit(solution)/shard_map/ppermute | solution.py:56
  211.0 4.3 %collective-permute-start.36 = (f32[32,512]{1,0:T(8,128)S(1)}, f32[32,512]{1,0:T(8,128)S(1)}, u32[]{:S(2)}, u32[]{:S(2)}) collective-permute-start(f32[32,512]{1,0:T(8,128)S(1)} %bitcast_add_fusion.4), channel_id=1, source_target_pairs={{0,6},{1,7},{2,0},{3,1},{4,2},{5,3},{6,4},{7,5},{8,14},{9,15},{10,... | collective-permute-start | bytes 196616 | tf_op jit(solution)/shard_map/ppermute | solution.py:48
  214.0 6.3 %collective-permute-start.35 = (f32[32,512]{1,0:T(8,128)S(1)}, f32[32,512]{1,0:T(8,128)S(1)}, u32[]{:S(2)}, u32[]{:S(2)}) collective-permute-start(f32[32,512]{1,0:T(8,128)S(1)} %bitcast_add_fusion.4), channel_id=1, source_target_pairs={{0,2},{1,3},{2,4},{3,5},{4,6},{5,7},{6,0},{7,1},{8,10},{9,11},{10,... | collective-permute-start | bytes 196616 | tf_op jit(solution)/shard_map/ppermute | solution.py:48
  214.0 6.3 %collective-permute-start.34 = (f32[32,512]{1,0:T(8,128)S(1)}, f32[32,512]{1,0:T(8,128)S(1)}, u32[]{:S(2)}, u32[]{:S(2)}) collective-permute-start(f32[32,512]{1,0:T(8,128)S(1)} %bitcast_add_fusion.4), channel_id=1, source_target_pairs={{0,4},{1,5},{2,6},{3,7},{4,0},{5,1},{6,2},{7,3},{8,12},{9,13},{10,... | collective-permute-start | bytes 196616 | tf_op jit(solution)/shard_map/ppermute | solution.py:48
  222.1 4.3 %collective-permute-start.38 = (f32[64,256]{1,0:T(8,128)S(1)}, f32[64,256]{1,0:T(8,128)S(1)}, u32[]{:S(2)}, u32[]{:S(2)}) collective-permute-start(f32[64,256]{1,0:T(8,128)S(1)} %bitcast.190), channel_id=1, source_target_pairs={{0,32},{8,40},{16,48},{24,56},{32,64},{40,72},{48,80},{56,88},{64,... | collective-permute-start | bytes 196616 | tf_op jit(solution)/shard_map/ppermute | solution.py:48
  222.1 4.3 %collective-permute-start.39 = (f32[64,256]{1,0:T(8,128)S(1)}, f32[64,256]{1,0:T(8,128)S(1)}, u32[]{:S(2)}, u32[]{:S(2)}) collective-permute-start(f32[64,256]{1,0:T(8,128)S(1)} %bitcast.191), channel_id=1, source_target_pairs={{0,96},{8,104},{16,112},{24,120},{32,0},{40,8},{48,16},{56,24},{64... | collective-permute-start | bytes 196616 | tf_op jit(solution)/shard_map/ppermute | solution.py:48
  224.8 4.6 %collective-permute-start.37 = (f32[64,256]{1,0:T(8,128)S(1)}, f32[64,256]{1,0:T(8,128)S(1)}, u32[]{:S(2)}, u32[]{:S(2)}) collective-permute-start(f32[64,256]{1,0:T(8,128)S(1)} %bitcast.192), channel_id=1, source_target_pairs={{0,64},{8,72},{16,80},{24,88},{32,96},{40,104},{48,112},{56,120},{... | collective-permute-start | bytes 196616 | tf_op jit(solution)/shard_map/ppermute | solution.py:48
  245.8 4.8 %collective-permute-start.40 = (f32[256,128]{1,0:T(8,128)S(1)}, f32[256,128]{1,0:T(8,128)S(1)}, u32[]{:S(2)}, u32[]{:S(2)}) collective-permute-start(f32[256,128]{1,0:T(8,128)S(1)} %bitcast.146), channel_id=1, source_target_pairs={{0,1},{1,0},{2,3},{3,2},{4,5},{5,4},{6,7},{7,6},{8,9},{9,8},{10,11... | collective-permute-start | bytes 393224 | tf_op jit(solution)/shard_map/ppermute | solution.py:56
  250.6 5.1 %collective-permute-start.43 = (f32[256,128]{1,0:T(8,128)S(1)}, f32[256,128]{1,0:T(8,128)S(1)}, u32[]{:S(2)}, u32[]{:S(2)}) collective-permute-start(f32[256,128]{1,0:T(8,128)S(1)} %bitcast_add_fusion.3), channel_id=1, source_target_pairs={{0,6},{1,7},{2,0},{3,1},{4,2},{5,3},{6,4},{7,5},{8,14},{9,15},{10,... | collective-permute-start | bytes 393224 | tf_op jit(solution)/shard_map/ppermute | solution.py:48
  251.8 8.8 %collective-permute-start.42 = (f32[256,128]{1,0:T(8,128)S(1)}, f32[256,128]{1,0:T(8,128)S(1)}, u32[]{:S(2)}, u32[]{:S(2)}) collective-permute-start(f32[256,128]{1,0:T(8,128)S(1)} %bitcast_add_fusion.3), channel_id=1, source_target_pairs={{0,2},{1,3},{2,4},{3,5},{4,6},{5,7},{6,0},{7,1},{8,10},{9,11},{10,... | collective-permute-start | bytes 393224 | tf_op jit(solution)/shard_map/ppermute | solution.py:48
  252.2 8.4 %collective-permute-start.41 = (f32[256,128]{1,0:T(8,128)S(1)}, f32[256,128]{1,0:T(8,128)S(1)}, u32[]{:S(2)}, u32[]{:S(2)}) collective-permute-start(f32[256,128]{1,0:T(8,128)S(1)} %bitcast_add_fusion.3), channel_id=1, source_target_pairs={{0,4},{1,5},{2,6},{3,7},{4,0},{5,1},{6,2},{7,3},{8,12},{9,13},{10,... | collective-permute-start | bytes 393224 | tf_op jit(solution)/shard_map/ppermute | solution.py:48
  260.6 48.3 %slice-start = ((s8[6422528]{0:T(1024)(128)(4,1)}), s8[2228224]{0:T(1024)(128)(4,1)S(1)}, s32[]{:S(2)}) async-start(s8[6422528]{0:T(1024)(128)(4,1)} %bitcast.144), calls=%async_computation.11 | async-start | bytes 4456448
  293.6 5.1 %collective-permute-start.44 = (f32[256,128]{1,0:T(8,128)S(1)}, f32[256,128]{1,0:T(8,128)S(1)}, u32[]{:S(2)}, u32[]{:S(2)}) collective-permute-start(f32[256,128]{1,0:T(8,128)S(1)} %dynamic-slice_bitcast_fusion.1), channel_id=1, source_target_pairs={{0,1},{1,0},{2,3},{3,2},{4,5},{5,4},{6,7},{7,6},{8,9},{9,8},{10,11... | collective-permute-start | bytes 393224 | tf_op jit(solution)/shard_map/ppermute | solution.py:62
  298.7 5.2 %collective-permute-start.47 = (f32[256,128]{1,0:T(8,128)S(1)}, f32[256,128]{1,0:T(8,128)S(1)}, u32[]{:S(2)}, u32[]{:S(2)}) collective-permute-start(f32[256,128]{1,0:T(8,128)S(1)} %bitcast_add_fusion.1), channel_id=1, source_target_pairs={{0,6},{1,7},{2,0},{3,1},{4,2},{5,3},{6,4},{7,5},{8,14},{9,15},{10,... | collective-permute-start | bytes 393224 | tf_op jit(solution)/shard_map/ppermute | solution.py:48
  298.8 9.2 %collective-permute-start.46 = (f32[256,128]{1,0:T(8,128)S(1)}, f32[256,128]{1,0:T(8,128)S(1)}, u32[]{:S(2)}, u32[]{:S(2)}) collective-permute-start(f32[256,128]{1,0:T(8,128)S(1)} %bitcast_add_fusion.1), channel_id=1, source_target_pairs={{0,2},{1,3},{2,4},{3,5},{4,6},{5,7},{6,0},{7,1},{8,10},{9,11},{10,... | collective-permute-start | bytes 393224 | tf_op jit(solution)/shard_map/ppermute | solution.py:48
  300.2 7.8 %collective-permute-start.45 = (f32[256,128]{1,0:T(8,128)S(1)}, f32[256,128]{1,0:T(8,128)S(1)}, u32[]{:S(2)}, u32[]{:S(2)}) collective-permute-start(f32[256,128]{1,0:T(8,128)S(1)} %bitcast_add_fusion.1), channel_id=1, source_target_pairs={{0,4},{1,5},{2,6},{3,7},{4,0},{5,1},{6,2},{7,3},{8,12},{9,13},{10,... | collective-permute-start | bytes 393224 | tf_op jit(solution)/shard_map/ppermute | solution.py:48
  308.0 1.9 collective-permute-start.48
  332.9 19.2 %all-to-all-start.9 = ((f32[16,64,256]{2,1,0:T(8,128)}), f32[16,64,256]{2,1,0:T(8,128)}, u32[]{:S(2)}, u32[]{:S(2)}) async-start(f32[16,64,256]{2,1,0:T(8,128)} %broadcast_in_dim.29), calls=%async_computation.9 | async-start | bytes 2097152 | tf_op jit(solution)/shard_map/all_to_all | solution.py:81
  353.9 4.4 %collective-permute-start.49 = (f32[512,128]{1,0:T(8,128)S(1)}, f32[512,128]{1,0:T(8,128)S(1)}, u32[]{:S(2)}, u32[]{:S(2)}) collective-permute-start(f32[512,128]{1,0:T(8,128)S(1)} %dynamic-slice_bitcast_fusion), channel_id=1, source_target_pairs={{0,1},{1,0},{2,3},{3,2},{4,5},{5,4},{6,7},{7,6},{8,9},{9,8},{10,11... | collective-permute-start | bytes 786440 | tf_op jit(solution)/shard_map/ppermute | solution.py:62
  358.3 7.6 %collective-permute-start.52 = (f32[512,128]{1,0:T(8,128)S(1)}, f32[512,128]{1,0:T(8,128)S(1)}, u32[]{:S(2)}, u32[]{:S(2)}) collective-permute-start(f32[512,128]{1,0:T(8,128)S(1)} %bitcast_add_fusion), channel_id=1, source_target_pairs={{0,6},{1,7},{2,0},{3,1},{4,2},{5,3},{6,4},{7,5},{8,14},{9,15},{10,... | collective-permute-start | bytes 786440 | tf_op jit(solution)/shard_map/ppermute | solution.py:48
  359.5 9.0 %collective-permute-start.51 = (f32[512,128]{1,0:T(8,128)S(1)}, f32[512,128]{1,0:T(8,128)S(1)}, u32[]{:S(2)}, u32[]{:S(2)}) collective-permute-start(f32[512,128]{1,0:T(8,128)S(1)} %bitcast_add_fusion), channel_id=1, source_target_pairs={{0,2},{1,3},{2,4},{3,5},{4,6},{5,7},{6,0},{7,1},{8,10},{9,11},{10,... | collective-permute-start | bytes 786440 | tf_op jit(solution)/shard_map/ppermute | solution.py:48
  359.8 13.1 %collective-permute-start.50 = (f32[512,128]{1,0:T(8,128)S(1)}, f32[512,128]{1,0:T(8,128)S(1)}, u32[]{:S(2)}, u32[]{:S(2)}) collective-permute-start(f32[512,128]{1,0:T(8,128)S(1)} %bitcast_add_fusion), channel_id=1, source_target_pairs={{0,4},{1,5},{2,6},{3,7},{4,0},{5,1},{6,2},{7,3},{8,12},{9,13},{10,... | collective-permute-start | bytes 786440 | tf_op jit(solution)/shard_map/ppermute | solution.py:48
  373.0 3.3 collective-permute-start.53
  (35 other events, 629.6 us)
Sparse Core Ops, SparseCore 0:
  34.4 87.7 all-gather.2

commit v3 on v2

--- a/solution.py
+++ b/solution.py
@@ -73,11 +73,18 @@
 
 def scatter_rows(values):
     chunks = values.reshape(ROWS, -1, values.shape[-1])
-    return lax.all_to_all(chunks, "prow", 0, 0).sum(axis=0)
-
-
-def share_rows(part, shape):
-    copies = jnp.broadcast_to(part[None], (ROWS,) + part.shape)
+    return lax.all_to_all(chunks, "prow", 0, 0)
+
+
+def share_rows(parts, shape):
+    def kernel(parts, out):
+        total = parts[0]
+        for i in range(1, ROWS):
+            total = total + parts[i]
+        for i in range(ROWS):
+            out[i] = total
+
+    copies = call(kernel, [parts.shape], parts)[0]
     return lax.all_to_all(copies, "prow", 0, 0).reshape(shape)
 
 
@@ -85,14 +92,16 @@
     return share_rows(scatter_rows(values), values.shape)
 
 
-def resident(array, first, last, step):
-    blocks = range(first, last, step)
-
-    def kernel(source, target, arrived):
-        copies = [
-            pltpu.make_async_copy(source.at[block], target.at[i], arrived.at[i])
-            for i, block in enumerate(blocks)
-        ]
+def resident(array, *ranges):
+    total = sum(len(blocks) for blocks in ranges)
+
+    def kernel(source, *refs):
+        arrived = refs[-1]
+        copies = []
+        for target, blocks in zip(refs, ranges):
+            for i, block in enumerate(blocks):
+                at = arrived.at[len(copies)]
+                copies.append(pltpu.make_async_copy(source.at[block], target.at[i], at))
         for copy in copies:
             copy.start()
         for copy in copies:
@@ -100,10 +109,10 @@
 
     return pl.pallas_call(
         kernel,
-        out_shape=pltpu.VMEM((len(blocks),) + array.shape[1:], array.dtype),
+        out_shape=[pltpu.VMEM((len(blocks),) + array.shape[1:], array.dtype) for blocks in ranges],
         in_specs=[pl.BlockSpec(memory_space=pltpu.HBM)],
-        out_specs=pl.BlockSpec(memory_space=pltpu.VMEM),
-        scratch_shapes=[pltpu.SemaphoreType.DMA((len(blocks),))],
+        out_specs=[pl.BlockSpec(memory_space=pltpu.VMEM)] * len(ranges),
+        scratch_shapes=[pltpu.SemaphoreType.DMA((total,))],
         compiler_params=pltpu.CompilerParams(vmem_limit_bytes=4 << 20),
     )(array)
 
@@ -235,33 +244,47 @@
     far = (inverse, factor)
     partial_value = [[] for _ in range(LEV)]
 
-    def push_up(narrow, tree_depth):
-        for upward in range(1, tree_depth + 1):
+    def push_up(narrow, tree_depth, first, last):
+        for upward in range(first, last + 1):
             blocks = parent_at[tree_depth] if upward == 1 else blocks_of(factor, tree_depth, upward)
             terms = product(narrow, blocks, "nrc,nwc->nrw")
             terms = terms * blocks_of(live, tree_depth, upward)[:, None, None]
             partial_value[tree_depth - upward].append(sum_children(terms, upward))
 
     for tree_depth in range(LEV - 1, TOP - 1, -1):
-        residual = nodes_of(rhs, tree_depth)
-        if tree_depth < LEV - 1:
-            residual = residual - sum_columns(sum(partial_value[tree_depth]))
-        pieces = product(residual.astype(bf16), nodes_of(inverse, tree_depth), "nrc,nwc->nrw")
         if tree_depth == LEV - 1:
-            pieces, near, inverse = lax.optimization_barrier((pieces, factor, inverse))
-            inverse = resident(inverse, 0, 31, 1)
-            parent_at = {4: resident(near, 34, 98, 4), 3: resident(near, 10, 34, 3)}
+            residual = nodes_of(rhs, tree_depth)
+            blocks = nodes_of(inverse, tree_depth)
+        else:
+            residual = order[0] - sum_columns(sum(partial_value[tree_depth]))
+            blocks = inverses[0]
+        pieces = product(residual.astype(bf16), blocks, "nrc,nwc->nrw")
+        if tree_depth == LEV - 1:
+            near = lax.optimization_barrier((pieces, factor, inverse, rhs))
+            pieces = near[0]
+            parents = resident(near[1], range(34, 98, 4), range(10, 34, 3))
+            inverses = resident(near[2], range(7, 15), range(3, 7))
+            order = resident(near[3], range(7, 15))
         part = scatter_rows(pieces)
         if tree_depth == LEV - 1:
+            part, parents, inverses, order = lax.optimization_barrier(
+                (part, parents, inverses, order)
+            )
+            parent_at = {4: parents[0], 3: parents[1]}
             whole, part = gather_blocks(top_inverses(far[0]), top_order(far[1]), part)
         forward = share_rows(part, pieces.shape)
         forward_levels[tree_depth] = forward
-        push_up(forward.astype(bf16), tree_depth)
+        narrow = forward.astype(bf16)
+        push_up(narrow, tree_depth, 1, tree_depth if tree_depth > TOP else 1)
 
     here = (lax.axis_index("pcol") == 0).astype(jnp.float32)
-    total = sum_columns(sum(partial_value[2]))
+    total = sum(partial_value[2]).reshape(-1, 128)
+    total = total + lax.ppermute(total, "pcol", TWIN)
+    total, narrow = lax.optimization_barrier((total, narrow))
+    total = sum_ring(total, "pcol", YRING).reshape(4, 64, 128)
+    push_up(narrow, TOP, 2, TOP)
     sent = enter_split(
-        rhs[0:7], total, inverse[3:7], sum(partial_value[1]), sum(partial_value[0]), here
+        rhs[0:7], total, inverses[1], sum(partial_value[1]), sum(partial_value[0]), here
     )
     got = lax.all_to_all(sent, "prow", 0, 0, axis_index_groups=ZGROUPS)
     pieces, sums_1, sums_0 = entered_split(got)
@@ -307,7 +330,7 @@
 
     sent = leave_split(target, *top_forward[::-1], top_solved[1], top_solved[0])
     got = lax.all_to_all(sent, "prow", 0, 0, axis_index_groups=ZGROUPS)
-    pieces, top_forward, top_solved = left_split(got, inverse[3:7])
+    pieces, top_forward, top_solved = left_split(got, inverses[1])
 
     gathered = [[] for _ in range(LEV)]
 
@@ -327,12 +350,16 @@
             target = forward_levels[tree_depth] - sum_rows(sum(gathered[tree_depth]))
             if tree_depth == LEV - 1:
                 forward_whole = jnp.concatenate([top_forward] + forward_levels[TOP:])
-                target, forward_whole = lax.optimization_barrier((target, forward_whole))
-            pieces = product(target.astype(bf16), nodes_of(inverse, tree_depth), "nrw,nwc->nrc")
+                upper = jnp.zeros(rhs.shape, jnp.float32).at[:15].set(jnp.concatenate(solved))
+                target, forward_whole, upper = lax.optimization_barrier(
+                    (target, forward_whole, upper)
+                )
+            blocks = inverses[0] if tree_depth == TOP else nodes_of(inverse, tree_depth)
+            pieces = product(target.astype(bf16), blocks, "nrw,nwc->nrc")
         solution = sum_columns(pieces)
         solved.append(solution)
         push_down(solution.astype(bf16), tree_depth)
-    return jnp.concatenate(solved), forward_whole
+    return upper.at[15:].set(solved[-1]), forward_whole
 
 
 def solution(mesh):

time: 387 us -> 375 us (0.969)
  blocking collectives: 68.1 us -> 83.7 us
  waiting for transfers between devices: 110 us -> 97.2 us
  Pallas kernels: 17.2 us -> 23.9 us
  matrix products: 29.6 us -> 23.4 us
  local copies, waits for them, and re-layouts: 19.7 us -> 14.1 us
  other arithmetic: 18 us -> 12.9 us
  starting transfers between devices: 108 us -> 103 us
    all_to_all x2 -> x3, blocking collectives: 33 us -> 48 us  [scatter_rows(): return lax.all_to_all(chunks, 'prow', 0, 0)]
    all_to_all x2 -> x1, waiting for transfers between devices: 15.7 us -> 3.94 us  [scatter_rows(): return lax.all_to_all(chunks, 'prow', 0, 0)]
    pallas_call x3 -> x7, Pallas kernels: 3.4 us -> 11.2 us  [call(): return pl.pallas_call(kernel, out_shape=outs)(*operands)]
    dot_general x28, matrix products: 29.6 us -> 23.4 us  [product(): return jnp.einsum(form, left, right, preferred_element_type=jnp.float32)]
    all_to_all x2 -> x1, starting transfers between devices: 13.4 us -> 8.61 us  [scatter_rows(): return lax.all_to_all(chunks, 'prow', 0, 0)]
    reduce_sum x4 -> x0, other arithmetic: 4.11 us -> none  [scatter_rows(): return lax.all_to_all(chunks, 'prow', 0, 0).sum(axis=0)]
    broadcast_in_dim x4 -> x0, local copies, waits for them, and re-layouts: 3.91 us -> none  [share_rows(): copies = jnp.broadcast_to(part[None], (ROWS,) + part.shape)]
    ppermute x6 -> x5, starting transfers between devices: 19.5 us -> 17.7 us  [sum_columns(): flat = flat + lax.ppermute(flat, 'pcol', TWIN)]
  transfers between devices with their start and end apart: 60 -> 59, of which waited for: 38 -> 40; matrix products, arithmetic and copies ran while one was open for 9% -> 7% of each run, Pallas kernels for 4% -> 5%
where the time goes in v3:
time: 375 us; the launch traced here: 374 us
  starting transfers between devices  103 us (27%)
  waiting for transfers between devices  97.2 us (26%)
  blocking collectives  83.7 us (22%)
  Pallas kernels  23.9 us (6%)
  matrix products  23.4 us (6%)
  between operations  15.1 us (4%)
  local copies, waits for them, and re-layouts  14.1 us (4%)
  other arithmetic  12.9 us (3%)
    ppermute x42, waiting for transfers between devices, sum_ring(): across, right, left = [lax.ppermute(values, axis, step) for step in ring]  58.1 us
    all_to_all x3, blocking collectives, scatter_rows(): return lax.all_to_all(chunks, 'prow', 0, 0)  48 us
    ppermute x42, starting transfers between devices, sum_ring(): across, right, left = [lax.ppermute(values, axis, step) for step in ring]  43.9 us
    all_to_all x3, waiting for transfers between devices, share_rows(): return lax.all_to_all(copies, 'prow', 0, 0).reshape(shape)  26.7 us
    dot_general x28, matrix products, product(): return jnp.einsum(form, left, right, preferred_element_type=jnp.float32)  23.4 us
    all_to_all x2, blocking collectives, per_device(): got = lax.all_to_all(sent, 'prow', 0, 0, axis_index_groups=ZGROUPS)  23.2 us
    ppermute x5, starting transfers between devices, sum_columns(): flat = flat + lax.ppermute(flat, 'pcol', TWIN)  17.7 us
    all_to_all x3, starting transfers between devices, share_rows(): return lax.all_to_all(copies, 'prow', 0, 0).reshape(shape)  13.8 us
  transfers between devices with their start and end apart: 59, of which 40 were waited for; matrix products, arithmetic and copies ran while one was open for 7% of the time, Pallas kernels for 5%

profile of v3, /device:TPU:1, one launch (start us, length us, event | category | flops | bytes accessed | tf_op | source)
XLA Modules:
  0.0 373.6 jit_solution(4992259221365444224)
XLA Ops:
  7.2 3.0 fusion.18
  10.2 8.6 %all-to-all-start = ((f32[16,64,256]{2,1,0:T(8,128)}), f32[16,64,256]{2,1,0:T(8,128)}, u32[]{:S(2)}, u32[]{:S(2)}) async-start(f32[16,64,256]{2,1,0:T(8,128)} %fusion.18), calls=%async_computation | async-start | bytes 2097152 | tf_op jit(solution)/shard_map/all_to_all | solution.py:76
  22.7 2.8 copy-done
  25.5 2.3 shard_map.59
  30.4 3.9 %all-to-all-done.parts = f32[16,64,256]{2,1,0:T(8,128)} async-done(((f32[16,64,256]{2,1,0:T(8,128)}), f32[16,64,256]{2,1,0:T(8,128)}, u32[]{:S(2)}, u32[]{:S(2)}) %all-to-all-start) | async-done | bytes 1048608 | tf_op jit(solution)/shard_map/all_to_all | solution.py:76
  34.4 2.3 shard_map.62
  36.7 4.0 %all-to-all-start.1 = ((f32[16,64,256]{2,1,0:T(8,128)}), f32[16,64,256]{2,1,0:T(8,128)S(1)}, u32[]{:S(2)}, u32[]{:S(2)}) async-start(f32[16,64,256]{2,1,0:T(8,128)} %shard_map.62), calls=%async_computation.1 | async-start | bytes 2097152 | tf_op jit(solution)/shard_map/all_to_all | solution.py:88
  40.8 14.2 %all-to-all-done.1 = f32[16,64,256]{2,1,0:T(8,128)S(1)} async-done(((f32[16,64,256]{2,1,0:T(8,128)}), f32[16,64,256]{2,1,0:T(8,128)S(1)}, u32[]{:S(2)}, u32[]{:S(2)}) %all-to-all-start.1) | async-done | bytes 1048608 | tf_op jit(solution)/shard_map/all_to_all | solution.py:88
  56.7 3.8 %collective-permute-start = (f32[256,128]{1,0:T(8,128)S(1)}, f32[256,128]{1,0:T(8,128)S(1)}, u32[]{:S(2)}, u32[]{:S(2)}) collective-permute-start(f32[256,128]{1,0:T(8,128)S(1)} %dynamic-slice_bitcast_fusion.2), channel_id=1, source_target_pairs={{0,1},{1,0},{2,3},{3,2},{4,5},{5,4},{6,7},{7,6},{8,9},{9,8},{10,11... | collective-permute-start | bytes 393224 | tf_op jit(solution)/shard_map/ppermute | solution.py:62
  61.6 2.8 collective-permute-start.3
  66.9 6.2 %collective-permute-done.2 = f32[256,128]{1,0:T(8,128)S(1)} collective-permute-done((f32[256,128]{1,0:T(8,128)S(1)}, f32[256,128]{1,0:T(8,128)S(1)}, u32[]{:S(2)}, u32[]{:S(2)}) %collective-permute-start.2) | collective-permute-done | bytes 131104 | tf_op jit(solution)/shard_map/ppermute | solution.py:48
  75.8 15.3 %all_to_all.50.parts = f32[16,32,256]{2,1,0:T(8,128)} all-to-all(f32[16,32,256]{2,1,0:T(8,128)S(1)} %bitcast.164), channel_id=1, replica_groups=mesh['prow'=16,'pcol'=8] {'prow'}, dimensions={0} | all-to-all | bytes 1048576 | tf_op jit(solution)/shard_map/all_to_all | solution.py:76
  91.1 1.9 shard_map.63
  93.0 5.4 %all-to-all-start.3 = ((f32[16,32,256]{2,1,0:T(8,128)}), f32[16,32,256]{2,1,0:T(8,128)S(1)}, u32[]{:S(2)}, u32[]{:S(2)}) async-start(f32[16,32,256]{2,1,0:T(8,128)} %shard_map.63), calls=%async_computation.3 | async-start | bytes 1048576 | tf_op jit(solution)/shard_map/all_to_all | solution.py:88
  99.7 1.7 slice.141.order
  101.4 1.7 fusion.5
  103.1 1.7 bitcast_reduce_fusion.2
  104.9 2.6 all-to-all-done.3
  107.8 3.6 collective-permute-start.5
  111.4 1.7 bitcast_reduce_fusion
  118.9 3.4 collective-permute-done.7
  124.4 9.8 %all_to_all.51.got = f32[4,16,1408]{2,1,0:T(8,128)} all-to-all(f32[4,16,1408]{2,1,0:T(8,128)S(1)} %shard_map.64), channel_id=1, replica_groups={{0,8,16,24},{32,40,48,56},{64,72,80,88},{96,104,112,120},{1,9,17,25},{3..., dimensions={0} | all-to-all | bytes 720896 | tf_op jit(solution)/shard_map/all_to_all | solution.py:289
  135.3 2.7 collective-permute-start.11
  138.6 1.8 shard_map.67
  140.4 2.3 collective-permute-done.9
  143.1 3.6 collective-permute-start.12
  154.6 2.7 collective-permute-start.18
  159.3 2.0 shard_map.66
  162.2 3.6 collective-permute-start.19
  166.7 2.1 collective-permute-start.22
  174.8 1.8 collective-permute-start.23
  177.1 1.7 collective-permute-done.23
  179.0 3.5 collective-permute-start.26
  183.4 2.9 collective-permute-start.29
  187.6 2.7 collective-permute-done.28
  192.5 2.7 collective-permute-start.32
  196.5 3.0 collective-permute-done.30
  199.6 3.5 collective-permute-start.33
  204.0 3.0 collective-permute-start.36
  208.3 5.0 %collective-permute-done.35 = f32[32,512]{1,0:T(8,128)S(1)} collective-permute-done((f32[32,512]{1,0:T(8,128)S(1)}, f32[32,512]{1,0:T(8,128)S(1)}, u32[]{:S(2)}, u32[]{:S(2)}) %collective-permute-start.35) | collective-permute-done | bytes 65568 | tf_op jit(solution)/shard_map/ppermute | solution.py:48
  213.9 2.7 collective-permute-start.39
  216.6 1.6 collective-permute-done.38
  218.2 3.0 collective-permute-done.37
  222.9 13.4 %all_to_all.52 = f32[4,16,3200]{2,1,0:T(8,128)} all-to-all(f32[4,16,3200]{2,1,0:T(8,128)S(1)} %shard_map.71), channel_id=1, replica_groups={{0,8,16,24},{32,40,48,56},{64,72,80,88},{96,104,112,120},{1,9,17,25},{3..., dimensions={0} | all-to-all | bytes 1638400 | tf_op jit(solution)/shard_map/all_to_all | solution.py:332
  237.8 3.5 collective-permute-start.40
  247.7 4.8 %collective-permute-done.42 = f32[256,128]{1,0:T(8,128)S(1)} collective-permute-done((f32[256,128]{1,0:T(8,128)S(1)}, f32[256,128]{1,0:T(8,128)S(1)}, u32[]{:S(2)}, u32[]{:S(2)}) %collective-permute-start.42) | collective-permute-done | bytes 131104 | tf_op jit(solution)/shard_map/ppermute | solution.py:48
  254.5 13.4 %all_to_all.53.parts = f32[16,32,256]{2,1,0:T(8,128)} all-to-all(f32[16,32,256]{2,1,0:T(8,128)S(1)} %bitcast.165), channel_id=1, replica_groups=mesh['prow'=16,'pcol'=8] {'prow'}, dimensions={0} | all-to-all | bytes 1048576 | tf_op jit(solution)/shard_map/all_to_all | solution.py:76
  269.1 12.5 %all_to_all.54 = f32[16,32,256]{2,1,0:T(8,128)S(1)} all-to-all(f32[16,32,256]{2,1,0:T(8,128)S(1)} %shard_map.73), channel_id=1, replica_groups=mesh['prow'=16,'pcol'=8] {'prow'}, dimensions={0} | all-to-all | bytes 1048576 | tf_op jit(solution)/shard_map/all_to_all | solution.py:88
  283.0 3.3 collective-permute-start.44
  293.0 1.7 collective-permute-done.46
  294.8 1.7 collective-permute-done.45
  296.5 1.8 collective-permute-start.48
  300.3 19.3 %all_to_all.55.parts = f32[16,64,256]{2,1,0:T(8,128)} all-to-all(f32[16,64,256]{2,1,0:T(8,128)S(1)} %fusion), channel_id=1, replica_groups=mesh['prow'=16,'pcol'=8] {'prow'}, dimensions={0} | all-to-all | bytes 2097152 | tf_op jit(solution)/shard_map/all_to_all | solution.py:76
  319.6 2.5 shard_map.74
  322.1 4.5 %all-to-all-start.9 = ((f32[16,64,256]{2,1,0:T(8,128)}), f32[16,64,256]{2,1,0:T(8,128)}, u32[]{:S(2)}, u32[]{:S(2)}) async-start(f32[16,64,256]{2,1,0:T(8,128)} %shard_map.74), calls=%async_computation.9 | async-start | bytes 2097152 | tf_op jit(solution)/shard_map/all_to_all | solution.py:88
  326.6 2.9 pad_maximum_fusion
  329.4 2.1 select_maximum_fusion
  331.5 9.9 %all-to-all-done.9 = f32[16,64,256]{2,1,0:T(8,128)} async-done(((f32[16,64,256]{2,1,0:T(8,128)}), f32[16,64,256]{2,1,0:T(8,128)}, u32[]{:S(2)}, u32[]{:S(2)}) %all-to-all-start.9) | async-done | bytes 1048608 | tf_op jit(solution)/shard_map/all_to_all | solution.py:88
  343.3 3.3 collective-permute-start.49
  349.3 1.7 collective-permute-start.50
  350.9 4.4 %collective-permute-done.52 = f32[512,128]{1,0:T(8,128)S(1)} collective-permute-done((f32[512,128]{1,0:T(8,128)S(1)}, f32[512,128]{1,0:T(8,128)S(1)}, u32[]{:S(2)}, u32[]{:S(2)}) %collective-permute-start.52) | collective-permute-done | bytes 262176 | tf_op jit(solution)/shard_map/ppermute | solution.py:48
  355.3 2.6 collective-permute-done.51
  357.9 4.4 %collective-permute-done.50 = f32[512,128]{1,0:T(8,128)S(1)} collective-permute-done((f32[512,128]{1,0:T(8,128)S(1)}, f32[512,128]{1,0:T(8,128)S(1)}, u32[]{:S(2)}, u32[]{:S(2)}) %collective-permute-start.50) | collective-permute-done | bytes 262176 | tf_op jit(solution)/shard_map/ppermute | solution.py:48
  362.4 2.2 collective-permute-start.53
  (260 shorter events, 82.2 us)
Async XLA Ops:
  10.2 24.2 %all-to-all-start = ((f32[16,64,256]{2,1,0:T(8,128)}), f32[16,64,256]{2,1,0:T(8,128)}, u32[]{:S(2)}, u32[]{:S(2)}) async-start(f32[16,64,256]{2,1,0:T(8,128)} %fusion.18), calls=%async_computation | async-start | bytes 2097152 | tf_op jit(solution)/shard_map/all_to_all | solution.py:76
  18.8 116.4 %all-gather.3.cloned.1.call-start = ((), (), s32[]{:S(2)}) async-start(), calls=%async_computation.10 | async-start | bytes 8519680 | tf_op jit(solution)/shard_map/all_gather | solution.py:160
  36.7 18.4 %all-to-all-start.1 = ((f32[16,64,256]{2,1,0:T(8,128)}), f32[16,64,256]{2,1,0:T(8,128)S(1)}, u32[]{:S(2)}, u32[]{:S(2)}) async-start(f32[16,64,256]{2,1,0:T(8,128)} %shard_map.62), calls=%async_computation.1 | async-start | bytes 2097152 | tf_op jit(solution)/shard_map/all_to_all | solution.py:88
  40.7 58.1 %copy-start.36 = (f32[98]{0:T(128)}, f32[98]{0:T(128)S(1)}, u32[]{:S(2)}) copy-start(f32[98]{0:T(128)S(1)} %convert_element_type.66) | copy-start | bytes 1180
  56.7 4.8 %collective-permute-start = (f32[256,128]{1,0:T(8,128)S(1)}, f32[256,128]{1,0:T(8,128)S(1)}, u32[]{:S(2)}, u32[]{:S(2)}) collective-permute-start(f32[256,128]{1,0:T(8,128)S(1)} %dynamic-slice_bitcast_fusion.2), channel_id=1, source_target_pairs={{0,1},{1,0},{2,3},{3,2},{4,5},{5,4},{6,7},{7,6},{8,9},{9,8},{10,11... | collective-permute-start | bytes 393224 | tf_op jit(solution)/shard_map/ppermute | solution.py:62
  61.6 5.3 %collective-permute-start.3 = (f32[256,128]{1,0:T(8,128)S(1)}, f32[256,128]{1,0:T(8,128)S(1)}, u32[]{:S(2)}, u32[]{:S(2)}) collective-permute-start(f32[256,128]{1,0:T(8,128)S(1)} %bitcast_add_fusion.2), channel_id=1, source_target_pairs={{0,6},{1,7},{2,0},{3,1},{4,2},{5,3},{6,4},{7,5},{8,14},{9,15},{10,... | collective-permute-start | bytes 393224 | tf_op jit(solution)/shard_map/ppermute | solution.py:48
  64.4 8.7 %collective-permute-start.2 = (f32[256,128]{1,0:T(8,128)S(1)}, f32[256,128]{1,0:T(8,128)S(1)}, u32[]{:S(2)}, u32[]{:S(2)}) collective-permute-start(f32[256,128]{1,0:T(8,128)S(1)} %bitcast_add_fusion.2), channel_id=1, source_target_pairs={{0,2},{1,3},{2,4},{3,5},{4,6},{5,7},{6,0},{7,1},{8,10},{9,11},{10,... | collective-permute-start | bytes 393224 | tf_op jit(solution)/shard_map/ppermute | solution.py:48
  64.4 8.7 %collective-permute-start.1 = (f32[256,128]{1,0:T(8,128)S(1)}, f32[256,128]{1,0:T(8,128)S(1)}, u32[]{:S(2)}, u32[]{:S(2)}) collective-permute-start(f32[256,128]{1,0:T(8,128)S(1)} %bitcast_add_fusion.2), channel_id=1, source_target_pairs={{0,4},{1,5},{2,6},{3,7},{4,0},{5,1},{6,2},{7,3},{8,12},{9,13},{10,... | collective-permute-start | bytes 393224 | tf_op jit(solution)/shard_map/ppermute | solution.py:48
  73.2 2.3 collective-permute-start.4
  93.0 14.4 %all-to-all-start.3 = ((f32[16,32,256]{2,1,0:T(8,128)}), f32[16,32,256]{2,1,0:T(8,128)S(1)}, u32[]{:S(2)}, u32[]{:S(2)}) async-start(f32[16,32,256]{2,1,0:T(8,128)} %shard_map.63), calls=%async_computation.3 | async-start | bytes 1048576 | tf_op jit(solution)/shard_map/all_to_all | solution.py:88
  107.8 5.3 %collective-permute-start.5 = (f32[256,128]{1,0:T(8,128)S(1)}, f32[256,128]{1,0:T(8,128)S(1)}, u32[]{:S(2)}, u32[]{:S(2)}) collective-permute-start(f32[256,128]{1,0:T(8,128)S(1)} %bitcast.188), channel_id=1, source_target_pairs={{0,1},{1,0},{2,3},{3,2},{4,5},{5,4},{6,7},{7,6},{8,9},{9,8},{10,11... | collective-permute-start | bytes 393224 | tf_op jit(solution)/shard_map/ppermute | solution.py:282
  113.1 5.8 %collective-permute-start.8 = (f32[256,128]{1,0:T(8,128)S(1)}, f32[256,128]{1,0:T(8,128)S(1)}, u32[]{:S(2)}, u32[]{:S(2)}) collective-permute-start(f32[256,128]{1,0:T(8,128)S(1)} %bitcast_add_fusion.6), channel_id=1, source_target_pairs={{0,6},{1,7},{2,0},{3,1},{4,2},{5,3},{6,4},{7,5},{8,14},{9,15},{10,... | collective-permute-start | bytes 393224 | tf_op jit(solution)/shard_map/ppermute | solution.py:48
  113.4 8.9 %collective-permute-start.7 = (f32[256,128]{1,0:T(8,128)S(1)}, f32[256,128]{1,0:T(8,128)S(1)}, u32[]{:S(2)}, u32[]{:S(2)}) collective-permute-start(f32[256,128]{1,0:T(8,128)S(1)} %bitcast_add_fusion.6), channel_id=1, source_target_pairs={{0,2},{1,3},{2,4},{3,5},{4,6},{5,7},{6,0},{7,1},{8,10},{9,11},{10,... | collective-permute-start | bytes 393224 | tf_op jit(solution)/shard_map/ppermute | solution.py:48
  114.7 7.6 %collective-permute-start.6 = (f32[256,128]{1,0:T(8,128)S(1)}, f32[256,128]{1,0:T(8,128)S(1)}, u32[]{:S(2)}, u32[]{:S(2)}) collective-permute-start(f32[256,128]{1,0:T(8,128)S(1)} %bitcast_add_fusion.6), channel_id=1, source_target_pairs={{0,4},{1,5},{2,6},{3,7},{4,0},{5,1},{6,2},{7,3},{8,12},{9,13},{10,... | collective-permute-start | bytes 393224 | tf_op jit(solution)/shard_map/ppermute | solution.py:48
  135.2 5.1 %collective-permute-start.10 = (f32[64,256]{1,0:T(8,128)S(1)}, f32[64,256]{1,0:T(8,128)S(1)}, u32[]{:S(2)}, u32[]{:S(2)}) collective-permute-start(f32[64,256]{1,0:T(8,128)S(1)} %bitcast.149), channel_id=1, source_target_pairs={{0,32},{8,40},{16,48},{24,56},{32,64},{40,72},{48,80},{56,88},{64,... | collective-permute-start | bytes 196616 | tf_op jit(solution)/shard_map/ppermute | solution.py:48
  135.3 5.1 %collective-permute-start.11 = (f32[64,256]{1,0:T(8,128)S(1)}, f32[64,256]{1,0:T(8,128)S(1)}, u32[]{:S(2)}, u32[]{:S(2)}) collective-permute-start(f32[64,256]{1,0:T(8,128)S(1)} %bitcast.150), channel_id=1, source_target_pairs={{0,96},{8,104},{16,112},{24,120},{32,0},{40,8},{48,16},{56,24},{64... | collective-permute-start | bytes 196616 | tf_op jit(solution)/shard_map/ppermute | solution.py:48
  138.0 4.7 %collective-permute-start.9 = (f32[64,256]{1,0:T(8,128)S(1)}, f32[64,256]{1,0:T(8,128)S(1)}, u32[]{:S(2)}, u32[]{:S(2)}) collective-permute-start(f32[64,256]{1,0:T(8,128)S(1)} %bitcast.151), channel_id=1, source_target_pairs={{0,64},{8,72},{16,80},{24,88},{32,96},{40,104},{48,112},{56,120},{... | collective-permute-start | bytes 196616 | tf_op jit(solution)/shard_map/ppermute | solution.py:48
  142.7 78.5 %copy-start.23 = (f32[64,256]{1,0:T(8,128)}, f32[64,256]{1,0:T(8,128)S(1)}, u32[]{:S(2)}) copy-start(f32[64,256]{1,0:T(8,128)S(1)} %add_add_fusion.7) | copy-start | bytes 196612
  143.1 4.5 %collective-permute-start.12 = (f32[32,512]{1,0:T(8,128)S(1)}, f32[32,512]{1,0:T(8,128)S(1)}, u32[]{:S(2)}, u32[]{:S(2)}) collective-permute-start(f32[32,512]{1,0:T(8,128)S(1)} %bitcast.198), channel_id=1, source_target_pairs={{0,1},{1,0},{2,3},{3,2},{4,5},{5,4},{6,7},{7,6},{8,9},{9,8},{10,11... | collective-permute-start | bytes 196616 | tf_op jit(solution)/shard_map/ppermute | solution.py:56
  147.7 4.4 %collective-permute-start.15 = (f32[32,512]{1,0:T(8,128)S(1)}, f32[32,512]{1,0:T(8,128)S(1)}, u32[]{:S(2)}, u32[]{:S(2)}) collective-permute-start(f32[32,512]{1,0:T(8,128)S(1)} %bitcast_add_fusion.5), channel_id=1, source_target_pairs={{0,6},{1,7},{2,0},{3,1},{4,2},{5,3},{6,4},{7,5},{8,14},{9,15},{10,... | collective-permute-start | bytes 196616 | tf_op jit(solution)/shard_map/ppermute | solution.py:48
  149.0 4.5 %collective-permute-start.14 = (f32[32,512]{1,0:T(8,128)S(1)}, f32[32,512]{1,0:T(8,128)S(1)}, u32[]{:S(2)}, u32[]{:S(2)}) collective-permute-start(f32[32,512]{1,0:T(8,128)S(1)} %bitcast_add_fusion.5), channel_id=1, source_target_pairs={{0,2},{1,3},{2,4},{3,5},{4,6},{5,7},{6,0},{7,1},{8,10},{9,11},{10,... | collective-permute-start | bytes 196616 | tf_op jit(solution)/shard_map/ppermute | solution.py:48
  149.2 5.1 %collective-permute-start.13 = (f32[32,512]{1,0:T(8,128)S(1)}, f32[32,512]{1,0:T(8,128)S(1)}, u32[]{:S(2)}, u32[]{:S(2)}) collective-permute-start(f32[32,512]{1,0:T(8,128)S(1)} %bitcast_add_fusion.5), channel_id=1, source_target_pairs={{0,4},{1,5},{2,6},{3,7},{4,0},{5,1},{6,2},{7,3},{8,12},{9,13},{10,... | collective-permute-start | bytes 196616 | tf_op jit(solution)/shard_map/ppermute | solution.py:48
  154.6 6.7 %collective-permute-start.17 = (f32[32,256]{1,0:T(8,128)S(1)}, f32[32,256]{1,0:T(8,128)S(1)}, u32[]{:S(2)}, u32[]{:S(2)}) collective-permute-start(f32[32,256]{1,0:T(8,128)S(1)} %bitcast.206), channel_id=1, source_target_pairs={{0,32},{8,40},{16,48},{24,56},{32,64},{40,72},{48,80},{56,88},{64,... | collective-permute-start | bytes 98312 | tf_op jit(solution)/shard_map/ppermute | solution.py:48
  154.6 6.7 %collective-permute-start.18 = (f32[32,256]{1,0:T(8,128)S(1)}, f32[32,256]{1,0:T(8,128)S(1)}, u32[]{:S(2)}, u32[]{:S(2)}) collective-permute-start(f32[32,256]{1,0:T(8,128)S(1)} %bitcast.207), channel_id=1, source_target_pairs={{0,96},{8,104},{16,112},{24,120},{32,0},{40,8},{48,16},{56,24},{64... | collective-permute-start | bytes 98312 | tf_op jit(solution)/shard_map/ppermute | solution.py:48
  157.3 4.3 %collective-permute-start.16 = (f32[32,256]{1,0:T(8,128)S(1)}, f32[32,256]{1,0:T(8,128)S(1)}, u32[]{:S(2)}, u32[]{:S(2)}) collective-permute-start(f32[32,256]{1,0:T(8,128)S(1)} %bitcast.208), channel_id=1, source_target_pairs={{0,64},{8,72},{16,80},{24,88},{32,96},{40,104},{48,112},{56,120},{... | collective-permute-start | bytes 98312 | tf_op jit(solution)/shard_map/ppermute | solution.py:48
  161.6 52.0 %copy-start.28 = (f32[32,256]{1,0:T(8,128)}, f32[32,256]{1,0:T(8,128)S(1)}, u32[]{:S(2)}) copy-start(f32[32,256]{1,0:T(8,128)S(1)} %add_add_fusion.10) | copy-start | bytes 98308
  162.2 4.4 %collective-permute-start.19 = (f32[16,512]{1,0:T(8,128)S(1)}, f32[16,512]{1,0:T(8,128)S(1)}, u32[]{:S(2)}, u32[]{:S(2)}) collective-permute-start(f32[16,512]{1,0:T(8,128)S(1)} %fusion.9), channel_id=1, source_target_pairs={{0,1},{1,0},{2,3},{3,2},{4,5},{5,4},{6,7},{7,6},{8,9},{9,8},{10,11... | collective-permute-start | bytes 98312 | tf_op jit(solution)/shard_map/ppermute | solution.py:56
  166.7 4.5 %collective-permute-start.22 = (f32[16,512]{1,0:T(8,128)S(1)}, f32[16,512]{1,0:T(8,128)S(1)}, u32[]{:S(2)}, u32[]{:S(2)}) collective-permute-start(f32[16,512]{1,0:T(8,128)S(1)} %add.249), channel_id=1, source_target_pairs={{0,6},{1,7},{2,0},{3,1},{4,2},{5,3},{6,4},{7,5},{8,14},{9,15},{10,... | collective-permute-start | bytes 98312 | tf_op jit(solution)/shard_map/ppermute | solution.py:48
  168.8 4.0 %collective-permute-start.21 = (f32[16,512]{1,0:T(8,128)S(1)}, f32[16,512]{1,0:T(8,128)S(1)}, u32[]{:S(2)}, u32[]{:S(2)}) collective-permute-start(f32[16,512]{1,0:T(8,128)S(1)} %add.249), channel_id=1, source_target_pairs={{0,2},{1,3},{2,4},{3,5},{4,6},{5,7},{6,0},{7,1},{8,10},{9,11},{10,... | collective-permute-start | bytes 98312 | tf_op jit(solution)/shard_map/ppermute | solution.py:48
  168.8 4.3 %collective-permute-start.20 = (f32[16,512]{1,0:T(8,128)S(1)}, f32[16,512]{1,0:T(8,128)S(1)}, u32[]{:S(2)}, u32[]{:S(2)}) collective-permute-start(f32[16,512]{1,0:T(8,128)S(1)} %add.249), channel_id=1, source_target_pairs={{0,4},{1,5},{2,6},{3,7},{4,0},{5,1},{6,2},{7,3},{8,12},{9,13},{10,... | collective-permute-start | bytes 98312 | tf_op jit(solution)/shard_map/ppermute | solution.py:48
  171.1 70.1 %copy-start.35 = (f32[8]{0:T(128)S(1)}, f32[8]{0:T(128)}, u32[]{:S(2)}) copy-start(f32[8]{0:T(128)} %copy-done.34) | copy-start | bytes 100
  173.3 3.3 collective-permute-start.25
  173.3 3.8 %collective-permute-start.24 = (f32[16,256]{1,0:T(8,128)S(1)}, f32[16,256]{1,0:T(8,128)S(1)}, u32[]{:S(2)}, u32[]{:S(2)}) collective-permute-start(f32[16,256]{1,0:T(8,128)S(1)} %fusion.29), channel_id=1, source_target_pairs={{0,32},{8,40},{16,48},{24,56},{32,64},{40,72},{48,80},{56,88},{64,... | collective-permute-start | bytes 49160 | tf_op jit(solution)/shard_map/ppermute | solution.py:48
  174.8 4.1 %collective-permute-start.23 = (f32[16,256]{1,0:T(8,128)S(1)}, f32[16,256]{1,0:T(8,128)S(1)}, u32[]{:S(2)}, u32[]{:S(2)}) collective-permute-start(f32[16,256]{1,0:T(8,128)S(1)} %fusion.29), channel_id=1, source_target_pairs={{0,64},{8,72},{16,80},{24,88},{32,96},{40,104},{48,112},{56,120},{... | collective-permute-start | bytes 49160 | tf_op jit(solution)/shard_map/ppermute | solution.py:48
  179.0 4.4 %collective-permute-start.26 = (f32[16,512]{1,0:T(8,128)S(1)}, f32[16,512]{1,0:T(8,128)S(1)}, u32[]{:S(2)}, u32[]{:S(2)}) collective-permute-start(f32[16,512]{1,0:T(8,128)S(1)} %fusion.27), channel_id=1, source_target_pairs={{0,1},{1,0},{2,3},{3,2},{4,5},{5,4},{6,7},{7,6},{8,9},{9,8},{10,11... | collective-permute-start | bytes 98312 | tf_op jit(solution)/shard_map/ppermute | solution.py:56
  183.4 4.2 %collective-permute-start.29 = (f32[16,512]{1,0:T(8,128)S(1)}, f32[16,512]{1,0:T(8,128)S(1)}, u32[]{:S(2)}, u32[]{:S(2)}) collective-permute-start(f32[16,512]{1,0:T(8,128)S(1)} %add.256), channel_id=1, source_target_pairs={{0,6},{1,7},{2,0},{3,1},{4,2},{5,3},{6,4},{7,5},{8,14},{9,15},{10,... | collective-permute-start | bytes 98312 | tf_op jit(solution)/shard_map/ppermute | solution.py:48
  186.3 4.0 %collective-permute-start.28 = (f32[16,512]{1,0:T(8,128)S(1)}, f32[16,512]{1,0:T(8,128)S(1)}, u32[]{:S(2)}, u32[]{:S(2)}) collective-permute-start(f32[16,512]{1,0:T(8,128)S(1)} %add.256), channel_id=1, source_target_pairs={{0,2},{1,3},{2,4},{3,5},{4,6},{5,7},{6,0},{7,1},{8,10},{9,11},{10,... | collective-permute-start | bytes 98312 | tf_op jit(solution)/shard_map/ppermute | solution.py:48
  186.3 4.3 %collective-permute-start.27 = (f32[16,512]{1,0:T(8,128)S(1)}, f32[16,512]{1,0:T(8,128)S(1)}, u32[]{:S(2)}, u32[]{:S(2)}) collective-permute-start(f32[16,512]{1,0:T(8,128)S(1)} %add.256), channel_id=1, source_target_pairs={{0,4},{1,5},{2,6},{3,7},{4,0},{5,1},{6,2},{7,3},{8,12},{9,13},{10,... | collective-permute-start | bytes 98312 | tf_op jit(solution)/shard_map/ppermute | solution.py:48
  192.5 4.0 %collective-permute-start.31 = (f32[32,256]{1,0:T(8,128)S(1)}, f32[32,256]{1,0:T(8,128)S(1)}, u32[]{:S(2)}, u32[]{:S(2)}) collective-permute-start(f32[32,256]{1,0:T(8,128)S(1)} %bitcast.209), channel_id=1, source_target_pairs={{0,32},{8,40},{16,48},{24,56},{32,64},{40,72},{48,80},{56,88},{64,... | collective-permute-start | bytes 98312 | tf_op jit(solution)/shard_map/ppermute | solution.py:48
  192.5 4.0 %collective-permute-start.32 = (f32[32,256]{1,0:T(8,128)S(1)}, f32[32,256]{1,0:T(8,128)S(1)}, u32[]{:S(2)}, u32[]{:S(2)}) collective-permute-start(f32[32,256]{1,0:T(8,128)S(1)} %bitcast.210), channel_id=1, source_target_pairs={{0,96},{8,104},{16,112},{24,120},{32,0},{40,8},{48,16},{56,24},{64... | collective-permute-start | bytes 98312 | tf_op jit(solution)/shard_map/ppermute | solution.py:48
  195.1 4.3 %collective-permute-start.30 = (f32[32,256]{1,0:T(8,128)S(1)}, f32[32,256]{1,0:T(8,128)S(1)}, u32[]{:S(2)}, u32[]{:S(2)}) collective-permute-start(f32[32,256]{1,0:T(8,128)S(1)} %bitcast.211), channel_id=1, source_target_pairs={{0,64},{8,72},{16,80},{24,88},{32,96},{40,104},{48,112},{56,120},{... | collective-permute-start | bytes 98312 | tf_op jit(solution)/shard_map/ppermute | solution.py:48
  199.6 4.4 %collective-permute-start.33 = (f32[32,512]{1,0:T(8,128)S(1)}, f32[32,512]{1,0:T(8,128)S(1)}, u32[]{:S(2)}, u32[]{:S(2)}) collective-permute-start(f32[32,512]{1,0:T(8,128)S(1)} %bitcast.199), channel_id=1, source_target_pairs={{0,1},{1,0},{2,3},{3,2},{4,5},{5,4},{6,7},{7,6},{8,9},{9,8},{10,11... | collective-permute-start | bytes 196616 | tf_op jit(solution)/shard_map/ppermute | solution.py:56
  204.0 4.3 %collective-permute-start.36 = (f32[32,512]{1,0:T(8,128)S(1)}, f32[32,512]{1,0:T(8,128)S(1)}, u32[]{:S(2)}, u32[]{:S(2)}) collective-permute-start(f32[32,512]{1,0:T(8,128)S(1)} %bitcast_add_fusion.4), channel_id=1, source_target_pairs={{0,6},{1,7},{2,0},{3,1},{4,2},{5,3},{6,4},{7,5},{8,14},{9,15},{10,... | collective-permute-start | bytes 196616 | tf_op jit(solution)/shard_map/ppermute | solution.py:48
  207.0 6.3 %collective-permute-start.35 = (f32[32,512]{1,0:T(8,128)S(1)}, f32[32,512]{1,0:T(8,128)S(1)}, u32[]{:S(2)}, u32[]{:S(2)}) collective-permute-start(f32[32,512]{1,0:T(8,128)S(1)} %bitcast_add_fusion.4), channel_id=1, source_target_pairs={{0,2},{1,3},{2,4},{3,5},{4,6},{5,7},{6,0},{7,1},{8,10},{9,11},{10,... | collective-permute-start | bytes 196616 | tf_op jit(solution)/shard_map/ppermute | solution.py:48
  207.0 6.3 %collective-permute-start.34 = (f32[32,512]{1,0:T(8,128)S(1)}, f32[32,512]{1,0:T(8,128)S(1)}, u32[]{:S(2)}, u32[]{:S(2)}) collective-permute-start(f32[32,512]{1,0:T(8,128)S(1)} %bitcast_add_fusion.4), channel_id=1, source_target_pairs={{0,4},{1,5},{2,6},{3,7},{4,0},{5,1},{6,2},{7,3},{8,12},{9,13},{10,... | collective-permute-start | bytes 196616 | tf_op jit(solution)/shard_map/ppermute | solution.py:48
  213.9 4.3 %collective-permute-start.38 = (f32[64,256]{1,0:T(8,128)S(1)}, f32[64,256]{1,0:T(8,128)S(1)}, u32[]{:S(2)}, u32[]{:S(2)}) collective-permute-start(f32[64,256]{1,0:T(8,128)S(1)} %bitcast.195), channel_id=1, source_target_pairs={{0,32},{8,40},{16,48},{24,56},{32,64},{40,72},{48,80},{56,88},{64,... | collective-permute-start | bytes 196616 | tf_op jit(solution)/shard_map/ppermute | solution.py:48
  213.9 4.3 %collective-permute-start.39 = (f32[64,256]{1,0:T(8,128)S(1)}, f32[64,256]{1,0:T(8,128)S(1)}, u32[]{:S(2)}, u32[]{:S(2)}) collective-permute-start(f32[64,256]{1,0:T(8,128)S(1)} %bitcast.196), channel_id=1, source_target_pairs={{0,96},{8,104},{16,112},{24,120},{32,0},{40,8},{48,16},{56,24},{64... | collective-permute-start | bytes 196616 | tf_op jit(solution)/shard_map/ppermute | solution.py:48
  216.6 4.6 %collective-permute-start.37 = (f32[64,256]{1,0:T(8,128)S(1)}, f32[64,256]{1,0:T(8,128)S(1)}, u32[]{:S(2)}, u32[]{:S(2)}) collective-permute-start(f32[64,256]{1,0:T(8,128)S(1)} %bitcast.197), channel_id=1, source_target_pairs={{0,64},{8,72},{16,80},{24,88},{32,96},{40,104},{48,112},{56,120},{... | collective-permute-start | bytes 196616 | tf_op jit(solution)/shard_map/ppermute | solution.py:48
  222.9 59.8 %copy-start.9 = (bf16[8,256,128]{2,1,0:T(8,128)(2,1)S(1)}, bf16[8,256,128]{2,1,0:T(8,128)(2,1)}, u32[]{:S(2)}) copy-start(bf16[8,256,128]{2,1,0:T(8,128)(2,1)} %copy-done.7) | copy-start | bytes 1572868
  237.8 4.8 %collective-permute-start.40 = (f32[256,128]{1,0:T(8,128)S(1)}, f32[256,128]{1,0:T(8,128)S(1)}, u32[]{:S(2)}, u32[]{:S(2)}) collective-permute-start(f32[256,128]{1,0:T(8,128)S(1)} %bitcast.148), channel_id=1, source_target_pairs={{0,1},{1,0},{2,3},{3,2},{4,5},{5,4},{6,7},{7,6},{8,9},{9,8},{10,11... | collective-permute-start | bytes 393224 | tf_op jit(solution)/shard_map/ppermute | solution.py:56
  242.6 5.1 %collective-permute-start.43 = (f32[256,128]{1,0:T(8,128)S(1)}, f32[256,128]{1,0:T(8,128)S(1)}, u32[]{:S(2)}, u32[]{:S(2)}) collective-permute-start(f32[256,128]{1,0:T(8,128)S(1)} %bitcast_add_fusion.3), channel_id=1, source_target_pairs={{0,6},{1,7},{2,0},{3,1},{4,2},{5,3},{6,4},{7,5},{8,14},{9,15},{10,... | collective-permute-start | bytes 393224 | tf_op jit(solution)/shard_map/ppermute | solution.py:48
  243.7 8.8 %collective-permute-start.42 = (f32[256,128]{1,0:T(8,128)S(1)}, f32[256,128]{1,0:T(8,128)S(1)}, u32[]{:S(2)}, u32[]{:S(2)}) collective-permute-start(f32[256,128]{1,0:T(8,128)S(1)} %bitcast_add_fusion.3), channel_id=1, source_target_pairs={{0,2},{1,3},{2,4},{3,5},{4,6},{5,7},{6,0},{7,1},{8,10},{9,11},{10,... | collective-permute-start | bytes 393224 | tf_op jit(solution)/shard_map/ppermute | solution.py:48
  244.1 8.4 %collective-permute-start.41 = (f32[256,128]{1,0:T(8,128)S(1)}, f32[256,128]{1,0:T(8,128)S(1)}, u32[]{:S(2)}, u32[]{:S(2)}) collective-permute-start(f32[256,128]{1,0:T(8,128)S(1)} %bitcast_add_fusion.3), channel_id=1, source_target_pairs={{0,4},{1,5},{2,6},{3,7},{4,0},{5,1},{6,2},{7,3},{8,12},{9,13},{10,... | collective-permute-start | bytes 393224 | tf_op jit(solution)/shard_map/ppermute | solution.py:48
  283.0 4.9 %collective-permute-start.44 = (f32[256,128]{1,0:T(8,128)S(1)}, f32[256,128]{1,0:T(8,128)S(1)}, u32[]{:S(2)}, u32[]{:S(2)}) collective-permute-start(f32[256,128]{1,0:T(8,128)S(1)} %dynamic-slice_bitcast_fusion.1), channel_id=1, source_target_pairs={{0,1},{1,0},{2,3},{3,2},{4,5},{5,4},{6,7},{7,6},{8,9},{9,8},{10,11... | collective-permute-start | bytes 393224 | tf_op jit(solution)/shard_map/ppermute | solution.py:62
  287.8 5.2 %collective-permute-start.47 = (f32[256,128]{1,0:T(8,128)S(1)}, f32[256,128]{1,0:T(8,128)S(1)}, u32[]{:S(2)}, u32[]{:S(2)}) collective-permute-start(f32[256,128]{1,0:T(8,128)S(1)} %bitcast_add_fusion.1), channel_id=1, source_target_pairs={{0,6},{1,7},{2,0},{3,1},{4,2},{5,3},{6,4},{7,5},{8,14},{9,15},{10,... | collective-permute-start | bytes 393224 | tf_op jit(solution)/shard_map/ppermute | solution.py:48
  288.2 6.6 %collective-permute-start.46 = (f32[256,128]{1,0:T(8,128)S(1)}, f32[256,128]{1,0:T(8,128)S(1)}, u32[]{:S(2)}, u32[]{:S(2)}) collective-permute-start(f32[256,128]{1,0:T(8,128)S(1)} %bitcast_add_fusion.1), channel_id=1, source_target_pairs={{0,2},{1,3},{2,4},{3,5},{4,6},{5,7},{6,0},{7,1},{8,10},{9,11},{10,... | collective-permute-start | bytes 393224 | tf_op jit(solution)/shard_map/ppermute | solution.py:48
  289.6 6.8 %collective-permute-start.45 = (f32[256,128]{1,0:T(8,128)S(1)}, f32[256,128]{1,0:T(8,128)S(1)}, u32[]{:S(2)}, u32[]{:S(2)}) collective-permute-start(f32[256,128]{1,0:T(8,128)S(1)} %bitcast_add_fusion.1), channel_id=1, source_target_pairs={{0,4},{1,5},{2,6},{3,7},{4,0},{5,1},{6,2},{7,3},{8,12},{9,13},{10,... | collective-permute-start | bytes 393224 | tf_op jit(solution)/shard_map/ppermute | solution.py:48
  296.5 2.8 collective-permute-start.48
  322.1 19.4 %all-to-all-start.9 = ((f32[16,64,256]{2,1,0:T(8,128)}), f32[16,64,256]{2,1,0:T(8,128)}, u32[]{:S(2)}, u32[]{:S(2)}) async-start(f32[16,64,256]{2,1,0:T(8,128)} %shard_map.74), calls=%async_computation.9 | async-start | bytes 2097152 | tf_op jit(solution)/shard_map/all_to_all | solution.py:88
  343.3 4.4 %collective-permute-start.49 = (f32[512,128]{1,0:T(8,128)S(1)}, f32[512,128]{1,0:T(8,128)S(1)}, u32[]{:S(2)}, u32[]{:S(2)}) collective-permute-start(f32[512,128]{1,0:T(8,128)S(1)} %dynamic-slice_bitcast_fusion), channel_id=1, source_target_pairs={{0,1},{1,0},{2,3},{3,2},{4,5},{5,4},{6,7},{7,6},{8,9},{9,8},{10,11... | collective-permute-start | bytes 786440 | tf_op jit(solution)/shard_map/ppermute | solution.py:62
  347.7 7.6 %collective-permute-start.52 = (f32[512,128]{1,0:T(8,128)S(1)}, f32[512,128]{1,0:T(8,128)S(1)}, u32[]{:S(2)}, u32[]{:S(2)}) collective-permute-start(f32[512,128]{1,0:T(8,128)S(1)} %bitcast_add_fusion), channel_id=1, source_target_pairs={{0,6},{1,7},{2,0},{3,1},{4,2},{5,3},{6,4},{7,5},{8,14},{9,15},{10,... | collective-permute-start | bytes 786440 | tf_op jit(solution)/shard_map/ppermute | solution.py:48
  348.9 9.0 %collective-permute-start.51 = (f32[512,128]{1,0:T(8,128)S(1)}, f32[512,128]{1,0:T(8,128)S(1)}, u32[]{:S(2)}, u32[]{:S(2)}) collective-permute-start(f32[512,128]{1,0:T(8,128)S(1)} %bitcast_add_fusion), channel_id=1, source_target_pairs={{0,2},{1,3},{2,4},{3,5},{4,6},{5,7},{6,0},{7,1},{8,10},{9,11},{10,... | collective-permute-start | bytes 786440 | tf_op jit(solution)/shard_map/ppermute | solution.py:48
  349.3 13.1 %collective-permute-start.50 = (f32[512,128]{1,0:T(8,128)S(1)}, f32[512,128]{1,0:T(8,128)S(1)}, u32[]{:S(2)}, u32[]{:S(2)}) collective-permute-start(f32[512,128]{1,0:T(8,128)S(1)} %bitcast_add_fusion), channel_id=1, source_target_pairs={{0,4},{1,5},{2,6},{3,7},{4,0},{5,1},{6,2},{7,3},{8,12},{9,13},{10,... | collective-permute-start | bytes 786440 | tf_op jit(solution)/shard_map/ppermute | solution.py:48
  362.4 3.4 collective-permute-start.53
  (39 other events, 727.1 us)
Sparse Core Ops, SparseCore 0:
  34.5 88.9 all-gather.2

commit v4 on v3

--- a/solution.py
+++ b/solution.py
@@ -32,6 +32,10 @@
     return jnp.einsum(form, left, right, preferred_element_type=jnp.float32)
 
 
+def grant(megabytes):
+    return pltpu.CompilerParams(vmem_limit_bytes=megabytes << 20)
+
+
 def sum_children(terms, upward):
     return terms.reshape((-1, 2**upward) + terms.shape[1:]).sum(axis=1)
 
@@ -49,7 +53,7 @@
     return (values + across) + (right + left)
 
 
-def sum_columns(values):
+def sum_columns(values, beside=None):
     shape = values.shape
     flat = values.reshape(-1, shape[-1])
     if flat.size <= 32768:
@@ -60,10 +64,15 @@
     mine = lax.dynamic_index_in_dim(halves, core, 0, keepdims=False)
     other = lax.dynamic_index_in_dim(halves, 1 - core, 0, keepdims=False)
     mine = mine + lax.ppermute(other, "pcol", TWIN)
+    extra = None
+    if beside is not None:
+        mine, extra = beside(mine)
     mine = sum_ring(mine, "pcol", YRING)
+    if beside is not None:
+        mine, extra = lax.optimization_barrier((mine, extra))
     other = lax.ppermute(mine, "pcol", TWIN)
     both = jnp.where(core == 0, jnp.stack([mine, other]), jnp.stack([other, mine]))
-    return both.reshape(shape)
+    return both.reshape(shape) if beside is None else (both.reshape(shape), extra)
 
 
 def sum_x_ring(values):
@@ -113,7 +122,7 @@
         in_specs=[pl.BlockSpec(memory_space=pltpu.HBM)],
         out_specs=[pl.BlockSpec(memory_space=pltpu.VMEM)] * len(ranges),
         scratch_shapes=[pltpu.SemaphoreType.DMA((total,))],
-        compiler_params=pltpu.CompilerParams(vmem_limit_bytes=4 << 20),
+        compiler_params=grant(4),
     )(array)
 
 
@@ -129,6 +138,7 @@
         grid=(1,),
         in_specs=[pl.BlockSpec((4, count, 256, 128), lambda i: (0, at, 0, 0))],
         out_specs=pl.BlockSpec((count, 256, 512), lambda i: (0, 0, 0)),
+        compiler_params=grant(12),
     )(whole)
 
 
@@ -150,6 +160,7 @@
             pl.BlockSpec((4, count, 256, 128), lambda i: (0, at, 0, 0)),
         ],
         out_specs=pl.BlockSpec((count, 512, 256), lambda i: (0, 0, 0)),
+        compiler_params=grant(12),
     )(weights, whole)
 
 
@@ -163,7 +174,7 @@
 
 def call(kernel, shapes, *operands):
     outs = [pltpu.VMEM(shape, jnp.float32) for shape in shapes]
-    return pl.pallas_call(kernel, out_shape=outs)(*operands)
+    return pl.pallas_call(kernel, out_shape=outs, compiler_params=grant(8))(*operands)
 
 
 def dot(left, right, contract):
@@ -188,6 +199,7 @@
         kernel,
         out_shape=pltpu.VMEM((4, 16, 1408), jnp.float32),
         in_specs=specs,
+        compiler_params=grant(8),
     )(here.reshape(1), order, total, inverses, sums_1, sums_0)
 
 
@@ -348,18 +360,21 @@
     for tree_depth in range(TOP - 1, LEV):
         if tree_depth >= TOP:
             target = forward_levels[tree_depth] - sum_rows(sum(gathered[tree_depth]))
-            if tree_depth == LEV - 1:
-                forward_whole = jnp.concatenate([top_forward] + forward_levels[TOP:])
-                upper = jnp.zeros(rhs.shape, jnp.float32).at[:15].set(jnp.concatenate(solved))
-                target, forward_whole, upper = lax.optimization_barrier(
-                    (target, forward_whole, upper)
-                )
             blocks = inverses[0] if tree_depth == TOP else nodes_of(inverse, tree_depth)
             pieces = product(target.astype(bf16), blocks, "nrw,nwc->nrc")
-        solution = sum_columns(pieces)
-        solved.append(solution)
-        push_down(solution.astype(bf16), tree_depth)
-    return upper.at[15:].set(solved[-1]), forward_whole
+        if tree_depth < LEV - 1:
+            solution = sum_columns(pieces)
+            solved.append(solution)
+            push_down(solution.astype(bf16), tree_depth)
+
+    def outputs(mine):
+        levels = [top_forward] + forward_levels[TOP:]
+        mine, upper, levels = lax.optimization_barrier((mine, solved, levels))
+        whole = jnp.zeros(rhs.shape, jnp.float32).at[:15].set(jnp.concatenate(upper))
+        return mine, (whole, jnp.concatenate(levels))
+
+    solution, (upper, forward_whole) = sum_columns(pieces, outputs)
+    return upper.at[15:].set(solution), forward_whole
 
 
 def solution(mesh):

time: 375 us -> 364 us (0.971)
  Pallas kernels: 23.9 us -> 8.82 us
  blocking collectives: 83.7 us -> 98.3 us
  waiting for transfers between devices: 97.2 us -> 86.4 us
    all_to_all x1 -> x2, blocking collectives: 12.5 us -> 31.9 us  [share_rows(): return lax.all_to_all(copies, 'prow', 0, 0).reshape(shape)]
    all_to_all x3 -> x2, waiting for transfers between devices: 26.7 us -> 16.5 us  [share_rows(): return lax.all_to_all(copies, 'prow', 0, 0).reshape(shape)]
    pallas_call x7, Pallas kernels: 11.2 us -> 2.64 us  [call(): pl.pallas_call(kernel, out_shape=outs, compiler_params=grant(8))(*operands)]
    unnamed x82 -> x74, local copies, waits for them, and re-layouts: 9.5 us -> 14.8 us
    all_to_all x3 -> x2, starting transfers between devices: 13.8 us -> 9.99 us  [share_rows(): return lax.all_to_all(copies, 'prow', 0, 0).reshape(shape)]
  transfers between devices with their start and end apart: 59 -> 58, of which waited for: 40 -> 40; matrix products, arithmetic and copies ran while one was open for 7% -> 7% of each run, Pallas kernels for 5% -> 2%
where the time goes in v4:
time: 364 us; the launch traced here: 362 us
  starting transfers between devices  103 us (28%)
  blocking collectives  98.3 us (27%)
  waiting for transfers between devices  86.4 us (24%)
  matrix products  20.1 us (6%)
  local copies, waits for them, and re-layouts  17.6 us (5%)
  between operations  15.1 us (4%)
  other arithmetic  13.1 us (4%)
  Pallas kernels  8.82 us (2%)
    ppermute x42, waiting for transfers between devices, sum_ring(): across, right, left = [lax.ppermute(values, axis, step) for step in ring]  55.8 us
    ppermute x42, starting transfers between devices, sum_ring(): across, right, left = [lax.ppermute(values, axis, step) for step in ring]  46.9 us
    all_to_all x3, blocking collectives, scatter_rows(): return lax.all_to_all(chunks, 'prow', 0, 0)  45.3 us
    all_to_all x2, blocking collectives, share_rows(): return lax.all_to_all(copies, 'prow', 0, 0).reshape(shape)  31.9 us
    all_to_all x2, blocking collectives, per_device(): got = lax.all_to_all(sent, 'prow', 0, 0, axis_index_groups=ZGROUPS)  21.1 us
    dot_general x28, matrix products, product(): return jnp.einsum(form, left, right, preferred_element_type=jnp.float32)  20.1 us
    ppermute x5, starting transfers between devices, sum_columns(): flat = flat + lax.ppermute(flat, 'pcol', TWIN)  17 us
    all_to_all x2, waiting for transfers between devices, share_rows(): return lax.all_to_all(copies, 'prow', 0, 0).reshape(shape)  16.5 us
  transfers between devices with their start and end apart: 58, of which 40 were waited for; matrix products, arithmetic and copies ran while one was open for 7% of the time, Pallas kernels for 2%

profile of v4, /device:TPU:1, one launch (start us, length us, event | category | flops | bytes accessed | tf_op | source)
XLA Modules:
  0.0 362.5 jit_solution(10638891522898290544)
XLA Ops:
  7.2 3.0 fusion.18
  10.1 8.6 %all-to-all-start = ((f32[16,64,256]{2,1,0:T(8,128)}), f32[16,64,256]{2,1,0:T(8,128)}, u32[]{:S(2)}, u32[]{:S(2)}) async-start(f32[16,64,256]{2,1,0:T(8,128)} %fusion.18), calls=%async_computation | async-start | bytes 2097152 | tf_op jit(solution)/shard_map/all_to_all | solution.py:85
  21.7 2.8 copy-done.3
  24.5 2.3 shard_map.59
  30.2 4.1 %all-to-all-done.parts = f32[16,64,256]{2,1,0:T(8,128)} async-done(((f32[16,64,256]{2,1,0:T(8,128)}), f32[16,64,256]{2,1,0:T(8,128)}, u32[]{:S(2)}, u32[]{:S(2)}) %all-to-all-start) | async-done | bytes 1048608 | tf_op jit(solution)/shard_map/all_to_all | solution.py:85
  36.7 4.3 %all-to-all-start.1 = ((f32[16,64,256]{2,1,0:T(8,128)}), f32[16,64,256]{2,1,0:T(8,128)}, u32[]{:S(2)}, u32[]{:S(2)}) async-start(f32[16,64,256]{2,1,0:T(8,128)} %copy-done.11), calls=%async_computation.1 | async-start | bytes 2097152 | tf_op jit(solution)/shard_map/all_to_all | solution.py:97
  41.2 14.1 %all-to-all-done.1 = f32[16,64,256]{2,1,0:T(8,128)} async-done(((f32[16,64,256]{2,1,0:T(8,128)}), f32[16,64,256]{2,1,0:T(8,128)}, u32[]{:S(2)}, u32[]{:S(2)}) %all-to-all-start.1) | async-done | bytes 1048608 | tf_op jit(solution)/shard_map/all_to_all | solution.py:97
  58.1 4.2 %collective-permute-start = (f32[256,128]{1,0:T(8,128)S(1)}, f32[256,128]{1,0:T(8,128)S(1)}, u32[]{:S(2)}, u32[]{:S(2)}) collective-permute-start(f32[256,128]{1,0:T(8,128)S(1)} %dynamic-slice_bitcast_fusion.2), channel_id=1, source_target_pairs={{0,1},{1,0},{2,3},{3,2},{4,5},{5,4},{6,7},{7,6},{8,9},{9,8},{10,11... | collective-permute-start | bytes 393224 | tf_op jit(solution)/shard_map/ppermute | solution.py:66
  64.1 2.8 collective-permute-start.3
  66.9 1.6 collective-permute-start.1
  69.5 6.2 %collective-permute-done.2 = f32[256,128]{1,0:T(8,128)S(1)} collective-permute-done((f32[256,128]{1,0:T(8,128)S(1)}, f32[256,128]{1,0:T(8,128)S(1)}, u32[]{:S(2)}, u32[]{:S(2)}) %collective-permute-start.2) | collective-permute-done | bytes 131104 | tf_op jit(solution)/shard_map/ppermute | solution.py:52
  79.3 14.7 %all_to_all.50.parts = f32[16,32,256]{2,1,0:T(8,128)S(1)} all-to-all(f32[16,32,256]{2,1,0:T(8,128)S(1)} %bitcast.176), channel_id=1, replica_groups=mesh['prow'=16,'pcol'=8] {'prow'}, dimensions={0} | all-to-all | bytes 1048576 | tf_op jit(solution)/shard_map/all_to_all | solution.py:85
  94.9 5.7 %all-to-all-start.3 = ((f32[16,32,256]{2,1,0:T(8,128)}), f32[16,32,256]{2,1,0:T(8,128)}, u32[]{:S(2)}, u32[]{:S(2)}) async-start(f32[16,32,256]{2,1,0:T(8,128)} %shard_map.63), calls=%async_computation.3 | async-start | bytes 1048576 | tf_op jit(solution)/shard_map/all_to_all | solution.py:97
  102.8 1.9 fusion.5
  104.6 2.5 bitcast_reduce_fusion.2
  107.2 2.5 all-to-all-done.3
  112.0 3.6 collective-permute-start.5
  115.5 1.9 bitcast_reduce_fusion
  122.7 3.8 %collective-permute-done.7 = f32[256,128]{1,0:T(8,128)S(1)} collective-permute-done((f32[256,128]{1,0:T(8,128)S(1)}, f32[256,128]{1,0:T(8,128)S(1)}, u32[]{:S(2)}, u32[]{:S(2)}) %collective-permute-start.7) | collective-permute-done | bytes 131104 | tf_op jit(solution)/shard_map/ppermute | solution.py:52
  126.7 8.5 %all_to_all.51.got = f32[4,16,1408]{2,1,0:T(8,128)S(1)} all-to-all(f32[4,16,1408]{2,1,0:T(8,128)S(1)} %shard_map.64), channel_id=1, replica_groups={{0,8,16,24},{32,40,48,56},{64,72,80,88},{96,104,112,120},{1,9,17,25},{3..., dimensions={0} | all-to-all | bytes 720896 | tf_op jit(solution)/shard_map/all_to_all | solution.py:301
  136.0 2.0 collective-permute-start.11
  139.1 2.9 copy-done
  144.9 3.9 %collective-permute-start.12 = (f32[32,512]{1,0:T(8,128)S(1)}, f32[32,512]{1,0:T(8,128)S(1)}, u32[]{:S(2)}, u32[]{:S(2)}) collective-permute-start(f32[32,512]{1,0:T(8,128)S(1)} %bitcast.199), channel_id=1, source_target_pairs={{0,1},{1,0},{2,3},{3,2},{4,5},{5,4},{6,7},{7,6},{8,9},{9,8},{10,11... | collective-permute-start | bytes 196616 | tf_op jit(solution)/shard_map/ppermute | solution.py:60
  151.2 1.6 collective-permute-start.13
  152.9 2.8 collective-permute-done.14
  156.6 2.7 collective-permute-start.18
  159.4 2.9 copy-done.2
  163.8 1.4 add_add_fusion.10
  165.8 2.9 collective-permute-start.19
  169.6 2.2 collective-permute-start.22
  173.1 2.7 collective-permute-done.21
  177.8 2.8 collective-permute-start.23
  182.0 3.5 collective-permute-start.26
  186.4 2.9 collective-permute-start.29
  190.5 2.7 collective-permute-done.28
  194.6 1.9 collective-permute-start.32
  196.5 1.6 collective-permute-start.30
  198.1 3.0 collective-permute-done.30
  201.3 3.2 collective-permute-start.33
  205.4 3.0 collective-permute-start.36
  209.7 5.0 %collective-permute-done.35 = f32[32,512]{1,0:T(8,128)S(1)} collective-permute-done((f32[32,512]{1,0:T(8,128)S(1)}, f32[32,512]{1,0:T(8,128)S(1)}, u32[]{:S(2)}, u32[]{:S(2)}) %collective-permute-start.35) | collective-permute-done | bytes 65568 | tf_op jit(solution)/shard_map/ppermute | solution.py:52
  215.2 2.7 collective-permute-start.39
  219.6 3.0 collective-permute-done.37
  222.6 12.7 %all_to_all.52 = f32[4,16,3200]{2,1,0:T(8,128)S(1)} all-to-all(f32[4,16,3200]{2,1,0:T(8,128)S(1)} %shard_map.71), channel_id=1, replica_groups={{0,8,16,24},{32,40,48,56},{64,72,80,88},{96,104,112,120},{1,9,17,25},{3..., dimensions={0} | all-to-all | bytes 1638400 | tf_op jit(solution)/shard_map/all_to_all | solution.py:344
  235.5 3.5 collective-permute-start.40
  242.7 2.1 collective-permute-done.43
  244.8 5.0 %collective-permute-done.42 = f32[256,128]{1,0:T(8,128)S(1)} collective-permute-done((f32[256,128]{1,0:T(8,128)S(1)}, f32[256,128]{1,0:T(8,128)S(1)}, u32[]{:S(2)}, u32[]{:S(2)}) %collective-permute-start.42) | collective-permute-done | bytes 131104 | tf_op jit(solution)/shard_map/ppermute | solution.py:52
  250.2 11.6 %all_to_all.53.parts = f32[16,32,256]{2,1,0:T(8,128)S(1)} all-to-all(f32[16,32,256]{2,1,0:T(8,128)S(1)} %bitcast.177), channel_id=1, replica_groups=mesh['prow'=16,'pcol'=8] {'prow'}, dimensions={0} | all-to-all | bytes 1048576 | tf_op jit(solution)/shard_map/all_to_all | solution.py:85
  261.9 13.5 %all_to_all.54 = f32[16,32,256]{2,1,0:T(8,128)S(1)} all-to-all(f32[16,32,256]{2,1,0:T(8,128)S(1)} %shard_map.73), channel_id=1, replica_groups=mesh['prow'=16,'pcol'=8] {'prow'}, dimensions={0} | all-to-all | bytes 1048576 | tf_op jit(solution)/shard_map/all_to_all | solution.py:97
  276.8 3.6 collective-permute-start.44
  281.5 1.5 collective-permute-start.46
  283.7 2.5 collective-permute-done.47
  286.2 1.5 collective-permute-done.46
  289.1 2.5 collective-permute-start.48
  293.0 19.0 %all_to_all.55.parts = f32[16,64,256]{2,1,0:T(8,128)S(1)} all-to-all(f32[16,64,256]{2,1,0:T(8,128)S(1)} %fusion), channel_id=1, replica_groups=mesh['prow'=16,'pcol'=8] {'prow'}, dimensions={0} | all-to-all | bytes 2097152 | tf_op jit(solution)/shard_map/all_to_all | solution.py:85
  312.1 18.3 %all_to_all.56 = f32[16,64,256]{2,1,0:T(8,128)S(1)} all-to-all(f32[16,64,256]{2,1,0:T(8,128)S(1)} %shard_map.74), channel_id=1, replica_groups=mesh['prow'=16,'pcol'=8] {'prow'}, dimensions={0} | all-to-all | bytes 2097152 | tf_op jit(solution)/shard_map/all_to_all | solution.py:97
  330.4 1.6 fusion.16
  332.0 3.3 collective-permute-start.49
  338.1 1.7 collective-permute-start.50
  339.9 2.9 pad_maximum_fusion
  342.7 1.4 collective-permute-done.52
  344.2 2.6 collective-permute-done.51
  346.8 4.4 %collective-permute-done.50 = f32[512,128]{1,0:T(8,128)S(1)} collective-permute-done((f32[512,128]{1,0:T(8,128)S(1)}, f32[512,128]{1,0:T(8,128)S(1)}, u32[]{:S(2)}, u32[]{:S(2)}) %collective-permute-start.50) | collective-permute-done | bytes 262176 | tf_op jit(solution)/shard_map/ppermute | solution.py:52
  351.2 2.2 collective-permute-start.53
  (251 shorter events, 68.0 us)
Async XLA Ops:
  10.1 24.2 %all-to-all-start = ((f32[16,64,256]{2,1,0:T(8,128)}), f32[16,64,256]{2,1,0:T(8,128)}, u32[]{:S(2)}, u32[]{:S(2)}) async-start(f32[16,64,256]{2,1,0:T(8,128)} %fusion.18), calls=%async_computation | async-start | bytes 2097152 | tf_op jit(solution)/shard_map/all_to_all | solution.py:85
  18.8 116.5 %all-gather.3.cloned.1.call-start = ((), (), s32[]{:S(2)}) async-start(), calls=%async_computation.10 | async-start | bytes 8519680 | tf_op jit(solution)/shard_map/all_gather | solution.py:171
  36.7 18.6 %all-to-all-start.1 = ((f32[16,64,256]{2,1,0:T(8,128)}), f32[16,64,256]{2,1,0:T(8,128)}, u32[]{:S(2)}, u32[]{:S(2)}) async-start(f32[16,64,256]{2,1,0:T(8,128)} %copy-done.11), calls=%async_computation.1 | async-start | bytes 2097152 | tf_op jit(solution)/shard_map/all_to_all | solution.py:97
  57.3 53.4 %copy-start.15 = (bf16[8,128,256]{2,1,0:T(8,128)(2,1)S(1)}, bf16[8,128,256]{2,1,0:T(8,128)(2,1)}, u32[]{:S(2)}) copy-start(bf16[8,128,256]{2,1,0:T(8,128)(2,1)} %copy-done.14) | copy-start | bytes 1572868
  58.1 5.1 %collective-permute-start = (f32[256,128]{1,0:T(8,128)S(1)}, f32[256,128]{1,0:T(8,128)S(1)}, u32[]{:S(2)}, u32[]{:S(2)}) collective-permute-start(f32[256,128]{1,0:T(8,128)S(1)} %dynamic-slice_bitcast_fusion.2), channel_id=1, source_target_pairs={{0,1},{1,0},{2,3},{3,2},{4,5},{5,4},{6,7},{7,6},{8,9},{9,8},{10,11... | collective-permute-start | bytes 393224 | tf_op jit(solution)/shard_map/ppermute | solution.py:66
  64.1 5.3 %collective-permute-start.3 = (f32[256,128]{1,0:T(8,128)S(1)}, f32[256,128]{1,0:T(8,128)S(1)}, u32[]{:S(2)}, u32[]{:S(2)}) collective-permute-start(f32[256,128]{1,0:T(8,128)S(1)} %bitcast_add_fusion.2), channel_id=1, source_target_pairs={{0,6},{1,7},{2,0},{3,1},{4,2},{5,3},{6,4},{7,5},{8,14},{9,15},{10,... | collective-permute-start | bytes 393224 | tf_op jit(solution)/shard_map/ppermute | solution.py:52
  66.9 8.7 %collective-permute-start.2 = (f32[256,128]{1,0:T(8,128)S(1)}, f32[256,128]{1,0:T(8,128)S(1)}, u32[]{:S(2)}, u32[]{:S(2)}) collective-permute-start(f32[256,128]{1,0:T(8,128)S(1)} %bitcast_add_fusion.2), channel_id=1, source_target_pairs={{0,2},{1,3},{2,4},{3,5},{4,6},{5,7},{6,0},{7,1},{8,10},{9,11},{10,... | collective-permute-start | bytes 393224 | tf_op jit(solution)/shard_map/ppermute | solution.py:52
  66.9 8.7 %collective-permute-start.1 = (f32[256,128]{1,0:T(8,128)S(1)}, f32[256,128]{1,0:T(8,128)S(1)}, u32[]{:S(2)}, u32[]{:S(2)}) collective-permute-start(f32[256,128]{1,0:T(8,128)S(1)} %bitcast_add_fusion.2), channel_id=1, source_target_pairs={{0,4},{1,5},{2,6},{3,7},{4,0},{5,1},{6,2},{7,3},{8,12},{9,13},{10,... | collective-permute-start | bytes 393224 | tf_op jit(solution)/shard_map/ppermute | solution.py:52
  75.7 2.3 collective-permute-start.4
  94.9 14.7 %all-to-all-start.3 = ((f32[16,32,256]{2,1,0:T(8,128)}), f32[16,32,256]{2,1,0:T(8,128)}, u32[]{:S(2)}, u32[]{:S(2)}) async-start(f32[16,32,256]{2,1,0:T(8,128)} %shard_map.63), calls=%async_computation.3 | async-start | bytes 1048576 | tf_op jit(solution)/shard_map/all_to_all | solution.py:97
  112.0 5.4 %collective-permute-start.5 = (f32[256,128]{1,0:T(8,128)S(1)}, f32[256,128]{1,0:T(8,128)S(1)}, u32[]{:S(2)}, u32[]{:S(2)}) collective-permute-start(f32[256,128]{1,0:T(8,128)S(1)} %bitcast.193), channel_id=1, source_target_pairs={{0,1},{1,0},{2,3},{3,2},{4,5},{5,4},{6,7},{7,6},{8,9},{9,8},{10,11... | collective-permute-start | bytes 393224 | tf_op jit(solution)/shard_map/ppermute | solution.py:294
  117.4 5.3 %collective-permute-start.8 = (f32[256,128]{1,0:T(8,128)S(1)}, f32[256,128]{1,0:T(8,128)S(1)}, u32[]{:S(2)}, u32[]{:S(2)}) collective-permute-start(f32[256,128]{1,0:T(8,128)S(1)} %bitcast_add_fusion.6), channel_id=1, source_target_pairs={{0,6},{1,7},{2,0},{3,1},{4,2},{5,3},{6,4},{7,5},{8,14},{9,15},{10,... | collective-permute-start | bytes 393224 | tf_op jit(solution)/shard_map/ppermute | solution.py:52
  117.7 8.8 %collective-permute-start.7 = (f32[256,128]{1,0:T(8,128)S(1)}, f32[256,128]{1,0:T(8,128)S(1)}, u32[]{:S(2)}, u32[]{:S(2)}) collective-permute-start(f32[256,128]{1,0:T(8,128)S(1)} %bitcast_add_fusion.6), channel_id=1, source_target_pairs={{0,2},{1,3},{2,4},{3,5},{4,6},{5,7},{6,0},{7,1},{8,10},{9,11},{10,... | collective-permute-start | bytes 393224 | tf_op jit(solution)/shard_map/ppermute | solution.py:52
  119.0 7.5 %collective-permute-start.6 = (f32[256,128]{1,0:T(8,128)S(1)}, f32[256,128]{1,0:T(8,128)S(1)}, u32[]{:S(2)}, u32[]{:S(2)}) collective-permute-start(f32[256,128]{1,0:T(8,128)S(1)} %bitcast_add_fusion.6), channel_id=1, source_target_pairs={{0,4},{1,5},{2,6},{3,7},{4,0},{5,1},{6,2},{7,3},{8,12},{9,13},{10,... | collective-permute-start | bytes 393224 | tf_op jit(solution)/shard_map/ppermute | solution.py:52
  135.3 7.5 %collective-permute-start.10 = (f32[64,256]{1,0:T(8,128)S(1)}, f32[64,256]{1,0:T(8,128)}, u32[]{:S(2)}, u32[]{:S(2)}) collective-permute-start(f32[64,256]{1,0:T(8,128)S(1)} %bitcast.167), channel_id=1, source_target_pairs={{0,32},{8,40},{16,48},{24,56},{32,64},{40,72},{48,80},{56,88},{64,... | collective-permute-start | bytes 196616 | tf_op jit(solution)/shard_map/ppermute | solution.py:52
  136.0 6.7 %collective-permute-start.11 = (f32[64,256]{1,0:T(8,128)S(1)}, f32[64,256]{1,0:T(8,128)}, u32[]{:S(2)}, u32[]{:S(2)}) collective-permute-start(f32[64,256]{1,0:T(8,128)S(1)} %bitcast.168), channel_id=1, source_target_pairs={{0,96},{8,104},{16,112},{24,120},{32,0},{40,8},{48,16},{56,24},{64... | collective-permute-start | bytes 196616 | tf_op jit(solution)/shard_map/ppermute | solution.py:52
  138.0 5.1 %collective-permute-start.9 = (f32[64,256]{1,0:T(8,128)S(1)}, f32[64,256]{1,0:T(8,128)}, u32[]{:S(2)}, u32[]{:S(2)}) collective-permute-start(f32[64,256]{1,0:T(8,128)S(1)} %bitcast.169), channel_id=1, source_target_pairs={{0,64},{8,72},{16,80},{24,88},{32,96},{40,104},{48,112},{56,120},{... | collective-permute-start | bytes 196616 | tf_op jit(solution)/shard_map/ppermute | solution.py:52
  144.9 4.8 %collective-permute-start.12 = (f32[32,512]{1,0:T(8,128)S(1)}, f32[32,512]{1,0:T(8,128)S(1)}, u32[]{:S(2)}, u32[]{:S(2)}) collective-permute-start(f32[32,512]{1,0:T(8,128)S(1)} %bitcast.199), channel_id=1, source_target_pairs={{0,1},{1,0},{2,3},{3,2},{4,5},{5,4},{6,7},{7,6},{8,9},{9,8},{10,11... | collective-permute-start | bytes 196616 | tf_op jit(solution)/shard_map/ppermute | solution.py:60
  149.7 3.2 collective-permute-start.15
  151.1 4.6 %collective-permute-start.14 = (f32[32,512]{1,0:T(8,128)S(1)}, f32[32,512]{1,0:T(8,128)S(1)}, u32[]{:S(2)}, u32[]{:S(2)}) collective-permute-start(f32[32,512]{1,0:T(8,128)S(1)} %bitcast_add_fusion.5), channel_id=1, source_target_pairs={{0,2},{1,3},{2,4},{3,5},{4,6},{5,7},{6,0},{7,1},{8,10},{9,11},{10,... | collective-permute-start | bytes 196616 | tf_op jit(solution)/shard_map/ppermute | solution.py:52
  151.2 5.1 %collective-permute-start.13 = (f32[32,512]{1,0:T(8,128)S(1)}, f32[32,512]{1,0:T(8,128)S(1)}, u32[]{:S(2)}, u32[]{:S(2)}) collective-permute-start(f32[32,512]{1,0:T(8,128)S(1)} %bitcast_add_fusion.5), channel_id=1, source_target_pairs={{0,4},{1,5},{2,6},{3,7},{4,0},{5,1},{6,2},{7,3},{8,12},{9,13},{10,... | collective-permute-start | bytes 196616 | tf_op jit(solution)/shard_map/ppermute | solution.py:52
  156.6 7.1 %collective-permute-start.17 = (f32[32,256]{1,0:T(8,128)S(1)}, f32[32,256]{1,0:T(8,128)S(1)}, u32[]{:S(2)}, u32[]{:S(2)}) collective-permute-start(f32[32,256]{1,0:T(8,128)S(1)} %bitcast.206), channel_id=1, source_target_pairs={{0,32},{8,40},{16,48},{24,56},{32,64},{40,72},{48,80},{56,88},{64,... | collective-permute-start | bytes 98312 | tf_op jit(solution)/shard_map/ppermute | solution.py:52
  156.6 7.1 %collective-permute-start.18 = (f32[32,256]{1,0:T(8,128)S(1)}, f32[32,256]{1,0:T(8,128)S(1)}, u32[]{:S(2)}, u32[]{:S(2)}) collective-permute-start(f32[32,256]{1,0:T(8,128)S(1)} %bitcast.207), channel_id=1, source_target_pairs={{0,96},{8,104},{16,112},{24,120},{32,0},{40,8},{48,16},{56,24},{64... | collective-permute-start | bytes 98312 | tf_op jit(solution)/shard_map/ppermute | solution.py:52
  159.3 4.4 %collective-permute-start.16 = (f32[32,256]{1,0:T(8,128)S(1)}, f32[32,256]{1,0:T(8,128)}, u32[]{:S(2)}, u32[]{:S(2)}) collective-permute-start(f32[32,256]{1,0:T(8,128)S(1)} %bitcast.208), channel_id=1, source_target_pairs={{0,64},{8,72},{16,80},{24,88},{32,96},{40,104},{48,112},{56,120},{... | collective-permute-start | bytes 98312 | tf_op jit(solution)/shard_map/ppermute | solution.py:52
  165.8 3.8 %collective-permute-start.19 = (f32[16,512]{1,0:T(8,128)S(1)}, f32[16,512]{1,0:T(8,128)S(1)}, u32[]{:S(2)}, u32[]{:S(2)}) collective-permute-start(f32[16,512]{1,0:T(8,128)S(1)} %fusion.9), channel_id=1, source_target_pairs={{0,1},{1,0},{2,3},{3,2},{4,5},{5,4},{6,7},{7,6},{8,9},{9,8},{10,11... | collective-permute-start | bytes 98312 | tf_op jit(solution)/shard_map/ppermute | solution.py:60
  169.6 3.5 collective-permute-start.22
  171.8 4.0 %collective-permute-start.21 = (f32[16,512]{1,0:T(8,128)S(1)}, f32[16,512]{1,0:T(8,128)S(1)}, u32[]{:S(2)}, u32[]{:S(2)}) collective-permute-start(f32[16,512]{1,0:T(8,128)S(1)} %add.249), channel_id=1, source_target_pairs={{0,2},{1,3},{2,4},{3,5},{4,6},{5,7},{6,0},{7,1},{8,10},{9,11},{10,... | collective-permute-start | bytes 98312 | tf_op jit(solution)/shard_map/ppermute | solution.py:52
  171.8 4.3 %collective-permute-start.20 = (f32[16,512]{1,0:T(8,128)S(1)}, f32[16,512]{1,0:T(8,128)S(1)}, u32[]{:S(2)}, u32[]{:S(2)}) collective-permute-start(f32[16,512]{1,0:T(8,128)S(1)} %add.249), channel_id=1, source_target_pairs={{0,4},{1,5},{2,6},{3,7},{4,0},{5,1},{6,2},{7,3},{8,12},{9,13},{10,... | collective-permute-start | bytes 98312 | tf_op jit(solution)/shard_map/ppermute | solution.py:52
  173.0 66.0 %slice-start.2 = ((s8[6422528]{0:T(1024)(128)(4,1)}), s8[2228224]{0:T(1024)(128)(4,1)S(1)}, s32[]{:S(2)}) async-start(s8[6422528]{0:T(1024)(128)(4,1)} %bitcast.152), calls=%async_computation.13 | async-start | bytes 4456448
  173.1 66.0 %copy-start.31 = (f32[8]{0:T(128)S(1)}, f32[8]{0:T(128)}, u32[]{:S(2)}) copy-start(f32[8]{0:T(128)} %slice.153) | copy-start | bytes 100
  176.3 4.3 %collective-permute-start.25 = (f32[16,256]{1,0:T(8,128)S(1)}, f32[16,256]{1,0:T(8,128)S(1)}, u32[]{:S(2)}, u32[]{:S(2)}) collective-permute-start(f32[16,256]{1,0:T(8,128)S(1)} %fusion.28), channel_id=1, source_target_pairs={{0,96},{8,104},{16,112},{24,120},{32,0},{40,8},{48,16},{56,24},{64... | collective-permute-start | bytes 49160 | tf_op jit(solution)/shard_map/ppermute | solution.py:52
  177.3 3.8 %collective-permute-start.24 = (f32[16,256]{1,0:T(8,128)S(1)}, f32[16,256]{1,0:T(8,128)S(1)}, u32[]{:S(2)}, u32[]{:S(2)}) collective-permute-start(f32[16,256]{1,0:T(8,128)S(1)} %fusion.28), channel_id=1, source_target_pairs={{0,32},{8,40},{16,48},{24,56},{32,64},{40,72},{48,80},{56,88},{64,... | collective-permute-start | bytes 49160 | tf_op jit(solution)/shard_map/ppermute | solution.py:52
  177.8 4.1 %collective-permute-start.23 = (f32[16,256]{1,0:T(8,128)S(1)}, f32[16,256]{1,0:T(8,128)S(1)}, u32[]{:S(2)}, u32[]{:S(2)}) collective-permute-start(f32[16,256]{1,0:T(8,128)S(1)} %fusion.28), channel_id=1, source_target_pairs={{0,64},{8,72},{16,80},{24,88},{32,96},{40,104},{48,112},{56,120},{... | collective-permute-start | bytes 49160 | tf_op jit(solution)/shard_map/ppermute | solution.py:52
  182.0 4.3 %collective-permute-start.26 = (f32[16,512]{1,0:T(8,128)S(1)}, f32[16,512]{1,0:T(8,128)S(1)}, u32[]{:S(2)}, u32[]{:S(2)}) collective-permute-start(f32[16,512]{1,0:T(8,128)S(1)} %fusion.26), channel_id=1, source_target_pairs={{0,1},{1,0},{2,3},{3,2},{4,5},{5,4},{6,7},{7,6},{8,9},{9,8},{10,11... | collective-permute-start | bytes 98312 | tf_op jit(solution)/shard_map/ppermute | solution.py:60
  186.4 4.2 %collective-permute-start.29 = (f32[16,512]{1,0:T(8,128)S(1)}, f32[16,512]{1,0:T(8,128)S(1)}, u32[]{:S(2)}, u32[]{:S(2)}) collective-permute-start(f32[16,512]{1,0:T(8,128)S(1)} %add.256), channel_id=1, source_target_pairs={{0,6},{1,7},{2,0},{3,1},{4,2},{5,3},{6,4},{7,5},{8,14},{9,15},{10,... | collective-permute-start | bytes 98312 | tf_op jit(solution)/shard_map/ppermute | solution.py:52
  189.3 4.0 %collective-permute-start.28 = (f32[16,512]{1,0:T(8,128)S(1)}, f32[16,512]{1,0:T(8,128)S(1)}, u32[]{:S(2)}, u32[]{:S(2)}) collective-permute-start(f32[16,512]{1,0:T(8,128)S(1)} %add.256), channel_id=1, source_target_pairs={{0,2},{1,3},{2,4},{3,5},{4,6},{5,7},{6,0},{7,1},{8,10},{9,11},{10,... | collective-permute-start | bytes 98312 | tf_op jit(solution)/shard_map/ppermute | solution.py:52
  189.3 4.3 %collective-permute-start.27 = (f32[16,512]{1,0:T(8,128)S(1)}, f32[16,512]{1,0:T(8,128)S(1)}, u32[]{:S(2)}, u32[]{:S(2)}) collective-permute-start(f32[16,512]{1,0:T(8,128)S(1)} %add.256), channel_id=1, source_target_pairs={{0,4},{1,5},{2,6},{3,7},{4,0},{5,1},{6,2},{7,3},{8,12},{9,13},{10,... | collective-permute-start | bytes 98312 | tf_op jit(solution)/shard_map/ppermute | solution.py:52
  193.6 45.4 %slice-start.3 = ((s8[6422528]{0:T(1024)(128)(4,1)}), s8[4194304]{0:T(1024)(128)(4,1)S(1)}, s32[]{:S(2)}) async-start(s8[6422528]{0:T(1024)(128)(4,1)} %bitcast.152), calls=%async_computation.14 | async-start | bytes 8388608
  193.8 56.1 %copy-start.16 = (bf16[8,128,256]{2,1,0:T(8,128)(2,1)S(1)}, bf16[8,128,256]{2,1,0:T(8,128)(2,1)}, u32[]{:S(2)}) copy-start(bf16[8,128,256]{2,1,0:T(8,128)(2,1)} %copy-done.14) | copy-start | bytes 1572868
  193.8 4.3 %collective-permute-start.31 = (f32[32,256]{1,0:T(8,128)S(1)}, f32[32,256]{1,0:T(8,128)S(1)}, u32[]{:S(2)}, u32[]{:S(2)}) collective-permute-start(f32[32,256]{1,0:T(8,128)S(1)} %bitcast.209), channel_id=1, source_target_pairs={{0,32},{8,40},{16,48},{24,56},{32,64},{40,72},{48,80},{56,88},{64,... | collective-permute-start | bytes 98312 | tf_op jit(solution)/shard_map/ppermute | solution.py:52
  194.6 3.5 collective-permute-start.32
  196.5 4.6 %collective-permute-start.30 = (f32[32,256]{1,0:T(8,128)S(1)}, f32[32,256]{1,0:T(8,128)S(1)}, u32[]{:S(2)}, u32[]{:S(2)}) collective-permute-start(f32[32,256]{1,0:T(8,128)S(1)} %bitcast.211), channel_id=1, source_target_pairs={{0,64},{8,72},{16,80},{24,88},{32,96},{40,104},{48,112},{56,120},{... | collective-permute-start | bytes 98312 | tf_op jit(solution)/shard_map/ppermute | solution.py:52
  201.3 4.1 %collective-permute-start.33 = (f32[32,512]{1,0:T(8,128)S(1)}, f32[32,512]{1,0:T(8,128)S(1)}, u32[]{:S(2)}, u32[]{:S(2)}) collective-permute-start(f32[32,512]{1,0:T(8,128)S(1)} %bitcast.200), channel_id=1, source_target_pairs={{0,1},{1,0},{2,3},{3,2},{4,5},{5,4},{6,7},{7,6},{8,9},{9,8},{10,11... | collective-permute-start | bytes 196616 | tf_op jit(solution)/shard_map/ppermute | solution.py:60
  205.4 4.3 %collective-permute-start.36 = (f32[32,512]{1,0:T(8,128)S(1)}, f32[32,512]{1,0:T(8,128)S(1)}, u32[]{:S(2)}, u32[]{:S(2)}) collective-permute-start(f32[32,512]{1,0:T(8,128)S(1)} %bitcast_add_fusion.4), channel_id=1, source_target_pairs={{0,6},{1,7},{2,0},{3,1},{4,2},{5,3},{6,4},{7,5},{8,14},{9,15},{10,... | collective-permute-start | bytes 196616 | tf_op jit(solution)/shard_map/ppermute | solution.py:52
  208.3 6.3 %collective-permute-start.35 = (f32[32,512]{1,0:T(8,128)S(1)}, f32[32,512]{1,0:T(8,128)S(1)}, u32[]{:S(2)}, u32[]{:S(2)}) collective-permute-start(f32[32,512]{1,0:T(8,128)S(1)} %bitcast_add_fusion.4), channel_id=1, source_target_pairs={{0,2},{1,3},{2,4},{3,5},{4,6},{5,7},{6,0},{7,1},{8,10},{9,11},{10,... | collective-permute-start | bytes 196616 | tf_op jit(solution)/shard_map/ppermute | solution.py:52
  208.3 6.3 %collective-permute-start.34 = (f32[32,512]{1,0:T(8,128)S(1)}, f32[32,512]{1,0:T(8,128)S(1)}, u32[]{:S(2)}, u32[]{:S(2)}) collective-permute-start(f32[32,512]{1,0:T(8,128)S(1)} %bitcast_add_fusion.4), channel_id=1, source_target_pairs={{0,4},{1,5},{2,6},{3,7},{4,0},{5,1},{6,2},{7,3},{8,12},{9,13},{10,... | collective-permute-start | bytes 196616 | tf_op jit(solution)/shard_map/ppermute | solution.py:52
  215.2 4.3 %collective-permute-start.38 = (f32[64,256]{1,0:T(8,128)S(1)}, f32[64,256]{1,0:T(8,128)S(1)}, u32[]{:S(2)}, u32[]{:S(2)}) collective-permute-start(f32[64,256]{1,0:T(8,128)S(1)} %bitcast.196), channel_id=1, source_target_pairs={{0,32},{8,40},{16,48},{24,56},{32,64},{40,72},{48,80},{56,88},{64,... | collective-permute-start | bytes 196616 | tf_op jit(solution)/shard_map/ppermute | solution.py:52
  215.2 4.3 %collective-permute-start.39 = (f32[64,256]{1,0:T(8,128)S(1)}, f32[64,256]{1,0:T(8,128)S(1)}, u32[]{:S(2)}, u32[]{:S(2)}) collective-permute-start(f32[64,256]{1,0:T(8,128)S(1)} %bitcast.197), channel_id=1, source_target_pairs={{0,96},{8,104},{16,112},{24,120},{32,0},{40,8},{48,16},{56,24},{64... | collective-permute-start | bytes 196616 | tf_op jit(solution)/shard_map/ppermute | solution.py:52
  217.9 4.6 %collective-permute-start.37 = (f32[64,256]{1,0:T(8,128)S(1)}, f32[64,256]{1,0:T(8,128)S(1)}, u32[]{:S(2)}, u32[]{:S(2)}) collective-permute-start(f32[64,256]{1,0:T(8,128)S(1)} %bitcast.198), channel_id=1, source_target_pairs={{0,64},{8,72},{16,80},{24,88},{32,96},{40,104},{48,112},{56,120},{... | collective-permute-start | bytes 196616 | tf_op jit(solution)/shard_map/ppermute | solution.py:52
  222.6 53.9 %copy-start.13 = (bf16[8,256,128]{2,1,0:T(8,128)(2,1)S(1)}, bf16[8,256,128]{2,1,0:T(8,128)(2,1)}, u32[]{:S(2)}) copy-start(bf16[8,256,128]{2,1,0:T(8,128)(2,1)} %copy-done.12) | copy-start | bytes 1572868
  235.5 4.5 %collective-permute-start.40 = (f32[256,128]{1,0:T(8,128)S(1)}, f32[256,128]{1,0:T(8,128)S(1)}, u32[]{:S(2)}, u32[]{:S(2)}) collective-permute-start(f32[256,128]{1,0:T(8,128)S(1)} %bitcast.165), channel_id=1, source_target_pairs={{0,1},{1,0},{2,3},{3,2},{4,5},{5,4},{6,7},{7,6},{8,9},{9,8},{10,11... | collective-permute-start | bytes 393224 | tf_op jit(solution)/shard_map/ppermute | solution.py:60
  240.0 4.8 %collective-permute-start.43 = (f32[256,128]{1,0:T(8,128)S(1)}, f32[256,128]{1,0:T(8,128)S(1)}, u32[]{:S(2)}, u32[]{:S(2)}) collective-permute-start(f32[256,128]{1,0:T(8,128)S(1)} %bitcast_add_fusion.3), channel_id=1, source_target_pairs={{0,6},{1,7},{2,0},{3,1},{4,2},{5,3},{6,4},{7,5},{8,14},{9,15},{10,... | collective-permute-start | bytes 393224 | tf_op jit(solution)/shard_map/ppermute | solution.py:52
  241.2 8.6 %collective-permute-start.42 = (f32[256,128]{1,0:T(8,128)S(1)}, f32[256,128]{1,0:T(8,128)S(1)}, u32[]{:S(2)}, u32[]{:S(2)}) collective-permute-start(f32[256,128]{1,0:T(8,128)S(1)} %bitcast_add_fusion.3), channel_id=1, source_target_pairs={{0,2},{1,3},{2,4},{3,5},{4,6},{5,7},{6,0},{7,1},{8,10},{9,11},{10,... | collective-permute-start | bytes 393224 | tf_op jit(solution)/shard_map/ppermute | solution.py:52
  241.6 8.2 %collective-permute-start.41 = (f32[256,128]{1,0:T(8,128)S(1)}, f32[256,128]{1,0:T(8,128)S(1)}, u32[]{:S(2)}, u32[]{:S(2)}) collective-permute-start(f32[256,128]{1,0:T(8,128)S(1)} %bitcast_add_fusion.3), channel_id=1, source_target_pairs={{0,4},{1,5},{2,6},{3,7},{4,0},{5,1},{6,2},{7,3},{8,12},{9,13},{10,... | collective-permute-start | bytes 393224 | tf_op jit(solution)/shard_map/ppermute | solution.py:52
  276.8 4.6 %collective-permute-start.44 = (f32[256,128]{1,0:T(8,128)S(1)}, f32[256,128]{1,0:T(8,128)S(1)}, u32[]{:S(2)}, u32[]{:S(2)}) collective-permute-start(f32[256,128]{1,0:T(8,128)S(1)} %dynamic-slice_bitcast_fusion.1), channel_id=1, source_target_pairs={{0,1},{1,0},{2,3},{3,2},{4,5},{5,4},{6,7},{7,6},{8,9},{9,8},{10,11... | collective-permute-start | bytes 393224 | tf_op jit(solution)/shard_map/ppermute | solution.py:66
  281.4 4.8 %collective-permute-start.47 = (f32[256,128]{1,0:T(8,128)S(1)}, f32[256,128]{1,0:T(8,128)S(1)}, u32[]{:S(2)}, u32[]{:S(2)}) collective-permute-start(f32[256,128]{1,0:T(8,128)S(1)} %bitcast_add_fusion.1), channel_id=1, source_target_pairs={{0,6},{1,7},{2,0},{3,1},{4,2},{5,3},{6,4},{7,5},{8,14},{9,15},{10,... | collective-permute-start | bytes 393224 | tf_op jit(solution)/shard_map/ppermute | solution.py:52
  281.5 6.2 %collective-permute-start.46 = (f32[256,128]{1,0:T(8,128)S(1)}, f32[256,128]{1,0:T(8,128)S(1)}, u32[]{:S(2)}, u32[]{:S(2)}) collective-permute-start(f32[256,128]{1,0:T(8,128)S(1)} %bitcast_add_fusion.1), channel_id=1, source_target_pairs={{0,2},{1,3},{2,4},{3,5},{4,6},{5,7},{6,0},{7,1},{8,10},{9,11},{10,... | collective-permute-start | bytes 393224 | tf_op jit(solution)/shard_map/ppermute | solution.py:52
  282.9 6.2 %collective-permute-start.45 = (f32[256,128]{1,0:T(8,128)S(1)}, f32[256,128]{1,0:T(8,128)S(1)}, u32[]{:S(2)}, u32[]{:S(2)}) collective-permute-start(f32[256,128]{1,0:T(8,128)S(1)} %bitcast_add_fusion.1), channel_id=1, source_target_pairs={{0,4},{1,5},{2,6},{3,7},{4,0},{5,1},{6,2},{7,3},{8,12},{9,13},{10,... | collective-permute-start | bytes 393224 | tf_op jit(solution)/shard_map/ppermute | solution.py:52
  289.1 3.5 collective-permute-start.48
  332.0 4.5 %collective-permute-start.49 = (f32[512,128]{1,0:T(8,128)S(1)}, f32[512,128]{1,0:T(8,128)S(1)}, u32[]{:S(2)}, u32[]{:S(2)}) collective-permute-start(f32[512,128]{1,0:T(8,128)S(1)} %dynamic-slice_bitcast_fusion), channel_id=1, source_target_pairs={{0,1},{1,0},{2,3},{3,2},{4,5},{5,4},{6,7},{7,6},{8,9},{9,8},{10,11... | collective-permute-start | bytes 786440 | tf_op jit(solution)/shard_map/ppermute | solution.py:66
  336.6 7.6 %collective-permute-start.52 = (f32[512,128]{1,0:T(8,128)S(1)}, f32[512,128]{1,0:T(8,128)S(1)}, u32[]{:S(2)}, u32[]{:S(2)}) collective-permute-start(f32[512,128]{1,0:T(8,128)S(1)} %bitcast_add_fusion), channel_id=1, source_target_pairs={{0,6},{1,7},{2,0},{3,1},{4,2},{5,3},{6,4},{7,5},{8,14},{9,15},{10,... | collective-permute-start | bytes 786440 | tf_op jit(solution)/shard_map/ppermute | solution.py:52
  337.7 9.0 %collective-permute-start.51 = (f32[512,128]{1,0:T(8,128)S(1)}, f32[512,128]{1,0:T(8,128)S(1)}, u32[]{:S(2)}, u32[]{:S(2)}) collective-permute-start(f32[512,128]{1,0:T(8,128)S(1)} %bitcast_add_fusion), channel_id=1, source_target_pairs={{0,2},{1,3},{2,4},{3,5},{4,6},{5,7},{6,0},{7,1},{8,10},{9,11},{10,... | collective-permute-start | bytes 786440 | tf_op jit(solution)/shard_map/ppermute | solution.py:52
  338.1 13.1 %collective-permute-start.50 = (f32[512,128]{1,0:T(8,128)S(1)}, f32[512,128]{1,0:T(8,128)S(1)}, u32[]{:S(2)}, u32[]{:S(2)}) collective-permute-start(f32[512,128]{1,0:T(8,128)S(1)} %bitcast_add_fusion), channel_id=1, source_target_pairs={{0,4},{1,5},{2,6},{3,7},{4,0},{5,1},{6,2},{7,3},{8,12},{9,13},{10,... | collective-permute-start | bytes 786440 | tf_op jit(solution)/shard_map/ppermute | solution.py:52
  351.2 3.4 collective-permute-start.53
  (34 other events, 431.2 us)
Sparse Core Ops, SparseCore 0:
  34.5 89.1 all-gather.2

commit v5 on v4

--- a/solution.py
+++ b/solution.py
@@ -275,7 +275,7 @@
             near = lax.optimization_barrier((pieces, factor, inverse, rhs))
             pieces = near[0]
             parents = resident(near[1], range(34, 98, 4), range(10, 34, 3))
-            inverses = resident(near[2], range(7, 15), range(3, 7))
+            inverses = resident(near[2], range(7, 15), range(3, 7), range(15, 31))
             order = resident(near[3], range(7, 15))
         part = scatter_rows(pieces)
         if tree_depth == LEV - 1:
@@ -360,7 +360,7 @@
     for tree_depth in range(TOP - 1, LEV):
         if tree_depth >= TOP:
             target = forward_levels[tree_depth] - sum_rows(sum(gathered[tree_depth]))
-            blocks = inverses[0] if tree_depth == TOP else nodes_of(inverse, tree_depth)
+            blocks = inverses[0] if tree_depth == TOP else inverses[2]
             pieces = product(target.astype(bf16), blocks, "nrw,nwc->nrc")
         if tree_depth < LEV - 1:
             solution = sum_columns(pieces)

time: 364 us -> 357 us (0.981)
  other arithmetic: 13.1 us -> 6.31 us
    unnamed x74 -> x72, local copies, waits for them, and re-layouts: 14.8 us -> 13.8 us
  transfers between devices with their start and end apart: 58 -> 58, of which waited for: 40 -> 41; matrix products, arithmetic and copies ran while one was open for 7% -> 5% of each run, Pallas kernels for 2% -> 3%
where the time goes in v5:
time: 357 us; the launch traced here: 355 us
  starting transfers between devices  102 us (29%)
  blocking collectives  98.8 us (28%)
  waiting for transfers between devices  86.7 us (24%)
  matrix products  19 us (5%)
  local copies, waits for them, and re-layouts  16 us (4%)
  between operations  15 us (4%)
  Pallas kernels  11.4 us (3%)
  other arithmetic  6.31 us (2%)
    ppermute x42, waiting for transfers between devices, sum_ring(): across, right, left = [lax.ppermute(values, axis, step) for step in ring]  57.5 us
    all_to_all x3, blocking collectives, scatter_rows(): return lax.all_to_all(chunks, 'prow', 0, 0)  45.7 us
    ppermute x42, starting transfers between devices, sum_ring(): across, right, left = [lax.ppermute(values, axis, step) for step in ring]  45.4 us
    all_to_all x2, blocking collectives, share_rows(): return lax.all_to_all(copies, 'prow', 0, 0).reshape(shape)  31.9 us
    all_to_all x2, blocking collectives, per_device(): got = lax.all_to_all(sent, 'prow', 0, 0, axis_index_groups=ZGROUPS)  21.2 us
    dot_general x28, matrix products, product(): return jnp.einsum(form, left, right, preferred_element_type=jnp.float32)  19 us
    ppermute x5, starting transfers between devices, sum_columns(): flat = flat + lax.ppermute(flat, 'pcol', TWIN)  17.7 us
    all_to_all x2, waiting for transfers between devices, share_rows(): return lax.all_to_all(copies, 'prow', 0, 0).reshape(shape)  17.7 us
  transfers between devices with their start and end apart: 58, of which 41 were waited for; matrix products, arithmetic and copies ran while one was open for 5% of the time, Pallas kernels for 3%

profile of v5, /device:TPU:1, one launch (start us, length us, event | category | flops | bytes accessed | tf_op | source)
XLA Modules:
  0.0 355.5 jit_solution(18328069540317953752)
XLA Ops:
  7.2 2.9 fusion.10
  10.1 8.6 %all-to-all-start = ((f32[16,64,256]{2,1,0:T(8,128)}), f32[16,64,256]{2,1,0:T(8,128)}, u32[]{:S(2)}, u32[]{:S(2)}) async-start(f32[16,64,256]{2,1,0:T(8,128)} %fusion.10), calls=%async_computation | async-start | bytes 2097152 | tf_op jit(solution)/shard_map/all_to_all | solution.py:85
  19.9 2.8 copy-done.3
  22.8 2.3 shard_map.59
  25.8 2.7 shard_map.60
  32.6 1.6 all-to-all-done.parts
  34.3 2.3 shard_map.62
  36.6 5.0 %all-to-all-start.1 = ((f32[16,64,256]{2,1,0:T(8,128)}), f32[16,64,256]{2,1,0:T(8,128)}, u32[]{:S(2)}, u32[]{:S(2)}) async-start(f32[16,64,256]{2,1,0:T(8,128)} %shard_map.62), calls=%async_computation.1 | async-start | bytes 2097152 | tf_op jit(solution)/shard_map/all_to_all | solution.py:97
  41.8 14.6 %all-to-all-done.1 = f32[16,64,256]{2,1,0:T(8,128)} async-done(((f32[16,64,256]{2,1,0:T(8,128)}), f32[16,64,256]{2,1,0:T(8,128)}, u32[]{:S(2)}, u32[]{:S(2)}) %all-to-all-start.1) | async-done | bytes 1048608 | tf_op jit(solution)/shard_map/all_to_all | solution.py:97
  58.2 3.6 %collective-permute-start = (f32[256,128]{1,0:T(8,128)S(1)}, f32[256,128]{1,0:T(8,128)S(1)}, u32[]{:S(2)}, u32[]{:S(2)}) collective-permute-start(f32[256,128]{1,0:T(8,128)S(1)} %dynamic-slice_bitcast_fusion.2), channel_id=1, source_target_pairs={{0,1},{1,0},{2,3},{3,2},{4,5},{5,4},{6,7},{7,6},{8,9},{9,8},{10,11... | collective-permute-start | bytes 393224 | tf_op jit(solution)/shard_map/ppermute | solution.py:66
  62.8 3.0 collective-permute-start.3
  65.8 1.6 collective-permute-start.1
  68.3 6.2 %collective-permute-done.2 = f32[256,128]{1,0:T(8,128)S(1)} collective-permute-done((f32[256,128]{1,0:T(8,128)S(1)}, f32[256,128]{1,0:T(8,128)S(1)}, u32[]{:S(2)}, u32[]{:S(2)}) %collective-permute-start.2) | collective-permute-done | bytes 131104 | tf_op jit(solution)/shard_map/ppermute | solution.py:52
  77.2 15.1 %all_to_all.50.parts = f32[16,32,256]{2,1,0:T(8,128)S(1)} all-to-all(f32[16,32,256]{2,1,0:T(8,128)S(1)} %bitcast.182), channel_id=1, replica_groups=mesh['prow'=16,'pcol'=8] {'prow'}, dimensions={0} | all-to-all | bytes 1048576 | tf_op jit(solution)/shard_map/all_to_all | solution.py:85
  93.2 5.6 %all-to-all-start.3 = ((f32[16,32,256]{2,1,0:T(8,128)}), f32[16,32,256]{2,1,0:T(8,128)S(1)}, u32[]{:S(2)}, u32[]{:S(2)}) async-start(f32[16,32,256]{2,1,0:T(8,128)} %shard_map.63), calls=%async_computation.3 | async-start | bytes 1048576 | tf_op jit(solution)/shard_map/all_to_all | solution.py:97
  100.4 2.5 fusion.5
  102.9 1.9 bitcast_reduce_fusion.2
  104.7 3.0 all-to-all-done.3
  108.2 3.6 %collective-permute-start.5 = (f32[256,128]{1,0:T(8,128)S(1)}, f32[256,128]{1,0:T(8,128)S(1)}, u32[]{:S(2)}, u32[]{:S(2)}) collective-permute-start(f32[256,128]{1,0:T(8,128)S(1)} %bitcast.199), channel_id=1, source_target_pairs={{0,1},{1,0},{2,3},{3,2},{4,5},{5,4},{6,7},{7,6},{8,9},{9,8},{10,11... | collective-permute-start | bytes 393224 | tf_op jit(solution)/shard_map/ppermute | solution.py:294
  111.7 1.9 bitcast_reduce_fusion
  118.9 3.9 %collective-permute-done.7 = f32[256,128]{1,0:T(8,128)S(1)} collective-permute-done((f32[256,128]{1,0:T(8,128)S(1)}, f32[256,128]{1,0:T(8,128)S(1)}, u32[]{:S(2)}, u32[]{:S(2)}) %collective-permute-start.7) | collective-permute-done | bytes 131104 | tf_op jit(solution)/shard_map/ppermute | solution.py:52
  123.1 8.6 %all_to_all.51.got = f32[4,16,1408]{2,1,0:T(8,128)S(1)} all-to-all(f32[4,16,1408]{2,1,0:T(8,128)S(1)} %shard_map.64), channel_id=1, replica_groups={{0,8,16,24},{32,40,48,56},{64,72,80,88},{96,104,112,120},{1,9,17,25},{3..., dimensions={0} | all-to-all | bytes 720896 | tf_op jit(solution)/shard_map/all_to_all | solution.py:301
  132.3 2.1 collective-permute-start.11
  135.3 2.9 copy-done
  140.0 3.8 %collective-permute-start.12 = (f32[32,512]{1,0:T(8,128)S(1)}, f32[32,512]{1,0:T(8,128)S(1)}, u32[]{:S(2)}, u32[]{:S(2)}) collective-permute-start(f32[32,512]{1,0:T(8,128)S(1)} %bitcast.205), channel_id=1, source_target_pairs={{0,1},{1,0},{2,3},{3,2},{4,5},{5,4},{6,7},{7,6},{8,9},{9,8},{10,11... | collective-permute-start | bytes 196616 | tf_op jit(solution)/shard_map/ppermute | solution.py:60
  146.2 1.6 collective-permute-start.13
  147.9 2.6 collective-permute-done.14
  151.6 2.7 collective-permute-start.18
  154.5 2.9 copy-done.2
  159.4 3.4 collective-permute-start.19
  163.7 2.2 collective-permute-start.22
  167.2 2.6 collective-permute-done.21
  171.8 2.3 collective-permute-start.23
  176.1 3.5 collective-permute-start.26
  180.4 2.9 collective-permute-start.29
  184.6 2.7 collective-permute-done.28
  188.1 2.5 collective-permute-start.32
  191.9 3.0 collective-permute-done.30
  195.0 3.5 collective-permute-start.33
  199.4 3.0 collective-permute-start.36
  203.7 5.0 %collective-permute-done.35 = f32[32,512]{1,0:T(8,128)S(1)} collective-permute-done((f32[32,512]{1,0:T(8,128)S(1)}, f32[32,512]{1,0:T(8,128)S(1)}, u32[]{:S(2)}, u32[]{:S(2)}) %collective-permute-start.35) | collective-permute-done | bytes 65568 | tf_op jit(solution)/shard_map/ppermute | solution.py:52
  209.3 2.7 collective-permute-start.39
  212.0 1.6 collective-permute-done.38
  213.6 3.0 collective-permute-done.37
  216.7 12.7 %all_to_all.52 = f32[4,16,3200]{2,1,0:T(8,128)S(1)} all-to-all(f32[4,16,3200]{2,1,0:T(8,128)S(1)} %shard_map.71), channel_id=1, replica_groups={{0,8,16,24},{32,40,48,56},{64,72,80,88},{96,104,112,120},{1,9,17,25},{3..., dimensions={0} | all-to-all | bytes 1638400 | tf_op jit(solution)/shard_map/all_to_all | solution.py:344
  229.6 3.5 collective-permute-start.40
  236.8 2.1 collective-permute-done.43
  238.9 5.0 %collective-permute-done.42 = f32[256,128]{1,0:T(8,128)S(1)} collective-permute-done((f32[256,128]{1,0:T(8,128)S(1)}, f32[256,128]{1,0:T(8,128)S(1)}, u32[]{:S(2)}, u32[]{:S(2)}) %collective-permute-start.42) | collective-permute-done | bytes 131104 | tf_op jit(solution)/shard_map/ppermute | solution.py:52
  244.2 11.6 %all_to_all.53.parts = f32[16,32,256]{2,1,0:T(8,128)S(1)} all-to-all(f32[16,32,256]{2,1,0:T(8,128)S(1)} %bitcast.183), channel_id=1, replica_groups=mesh['prow'=16,'pcol'=8] {'prow'}, dimensions={0} | all-to-all | bytes 1048576 | tf_op jit(solution)/shard_map/all_to_all | solution.py:85
  255.9 13.5 %all_to_all.54 = f32[16,32,256]{2,1,0:T(8,128)S(1)} all-to-all(f32[16,32,256]{2,1,0:T(8,128)S(1)} %shard_map.73), channel_id=1, replica_groups=mesh['prow'=16,'pcol'=8] {'prow'}, dimensions={0} | all-to-all | bytes 1048576 | tf_op jit(solution)/shard_map/all_to_all | solution.py:97
  269.8 3.6 %collective-permute-start.44 = (f32[256,128]{1,0:T(8,128)S(1)}, f32[256,128]{1,0:T(8,128)S(1)}, u32[]{:S(2)}, u32[]{:S(2)}) collective-permute-start(f32[256,128]{1,0:T(8,128)S(1)} %dynamic-slice_bitcast_fusion.1), channel_id=1, source_target_pairs={{0,1},{1,0},{2,3},{3,2},{4,5},{5,4},{6,7},{7,6},{8,9},{9,8},{10,11... | collective-permute-start | bytes 393224 | tf_op jit(solution)/shard_map/ppermute | solution.py:66
  276.7 2.4 collective-permute-done.47
  279.2 1.5 collective-permute-done.46
  282.1 2.5 collective-permute-start.48
  286.0 18.9 %all_to_all.55.parts = f32[16,64,256]{2,1,0:T(8,128)S(1)} all-to-all(f32[16,64,256]{2,1,0:T(8,128)S(1)} %fusion), channel_id=1, replica_groups=mesh['prow'=16,'pcol'=8] {'prow'}, dimensions={0} | all-to-all | bytes 2097152 | tf_op jit(solution)/shard_map/all_to_all | solution.py:85
  305.1 18.3 %all_to_all.56 = f32[16,64,256]{2,1,0:T(8,128)S(1)} all-to-all(f32[16,64,256]{2,1,0:T(8,128)S(1)} %shard_map.74), channel_id=1, replica_groups=mesh['prow'=16,'pcol'=8] {'prow'}, dimensions={0} | all-to-all | bytes 2097152 | tf_op jit(solution)/shard_map/all_to_all | solution.py:97
  323.4 1.6 fusion.18
  325.0 3.3 collective-permute-start.49
  331.1 1.7 collective-permute-start.50
  332.9 2.7 pad_maximum_fusion
  335.6 1.5 collective-permute-done.52
  337.2 2.6 collective-permute-done.51
  339.8 4.4 %collective-permute-done.50 = f32[512,128]{1,0:T(8,128)S(1)} collective-permute-done((f32[512,128]{1,0:T(8,128)S(1)}, f32[512,128]{1,0:T(8,128)S(1)}, u32[]{:S(2)}, u32[]{:S(2)}) %collective-permute-start.50) | collective-permute-done | bytes 262176 | tf_op jit(solution)/shard_map/ppermute | solution.py:52
  344.2 2.2 collective-permute-start.53
  (250 shorter events, 59.0 us)
Async XLA Ops:
  10.1 24.2 %all-to-all-start = ((f32[16,64,256]{2,1,0:T(8,128)}), f32[16,64,256]{2,1,0:T(8,128)}, u32[]{:S(2)}, u32[]{:S(2)}) async-start(f32[16,64,256]{2,1,0:T(8,128)} %fusion.10), calls=%async_computation | async-start | bytes 2097152 | tf_op jit(solution)/shard_map/all_to_all | solution.py:85
  18.7 113.0 %all-gather.3.cloned.1.call-start = ((), (), s32[]{:S(2)}) async-start(), calls=%async_computation.10 | async-start | bytes 8519680 | tf_op jit(solution)/shard_map/all_gather | solution.py:171
  36.6 19.8 %all-to-all-start.1 = ((f32[16,64,256]{2,1,0:T(8,128)}), f32[16,64,256]{2,1,0:T(8,128)}, u32[]{:S(2)}, u32[]{:S(2)}) async-start(f32[16,64,256]{2,1,0:T(8,128)} %shard_map.62), calls=%async_computation.1 | async-start | bytes 2097152 | tf_op jit(solution)/shard_map/all_to_all | solution.py:97
  57.7 50.1 %copy-start.8 = (bf16[8,128,256]{2,1,0:T(8,128)(2,1)S(1)}, bf16[8,128,256]{2,1,0:T(8,128)(2,1)}, u32[]{:S(2)}) copy-start(bf16[8,128,256]{2,1,0:T(8,128)(2,1)} %copy-done.7) | copy-start | bytes 1572868
  58.2 4.6 %collective-permute-start = (f32[256,128]{1,0:T(8,128)S(1)}, f32[256,128]{1,0:T(8,128)S(1)}, u32[]{:S(2)}, u32[]{:S(2)}) collective-permute-start(f32[256,128]{1,0:T(8,128)S(1)} %dynamic-slice_bitcast_fusion.2), channel_id=1, source_target_pairs={{0,1},{1,0},{2,3},{3,2},{4,5},{5,4},{6,7},{7,6},{8,9},{9,8},{10,11... | collective-permute-start | bytes 393224 | tf_op jit(solution)/shard_map/ppermute | solution.py:66
  62.8 5.5 %collective-permute-start.3 = (f32[256,128]{1,0:T(8,128)S(1)}, f32[256,128]{1,0:T(8,128)S(1)}, u32[]{:S(2)}, u32[]{:S(2)}) collective-permute-start(f32[256,128]{1,0:T(8,128)S(1)} %bitcast_add_fusion.2), channel_id=1, source_target_pairs={{0,6},{1,7},{2,0},{3,1},{4,2},{5,3},{6,4},{7,5},{8,14},{9,15},{10,... | collective-permute-start | bytes 393224 | tf_op jit(solution)/shard_map/ppermute | solution.py:52
  65.8 8.7 %collective-permute-start.2 = (f32[256,128]{1,0:T(8,128)S(1)}, f32[256,128]{1,0:T(8,128)S(1)}, u32[]{:S(2)}, u32[]{:S(2)}) collective-permute-start(f32[256,128]{1,0:T(8,128)S(1)} %bitcast_add_fusion.2), channel_id=1, source_target_pairs={{0,2},{1,3},{2,4},{3,5},{4,6},{5,7},{6,0},{7,1},{8,10},{9,11},{10,... | collective-permute-start | bytes 393224 | tf_op jit(solution)/shard_map/ppermute | solution.py:52
  65.8 8.7 %collective-permute-start.1 = (f32[256,128]{1,0:T(8,128)S(1)}, f32[256,128]{1,0:T(8,128)S(1)}, u32[]{:S(2)}, u32[]{:S(2)}) collective-permute-start(f32[256,128]{1,0:T(8,128)S(1)} %bitcast_add_fusion.2), channel_id=1, source_target_pairs={{0,4},{1,5},{2,6},{3,7},{4,0},{5,1},{6,2},{7,3},{8,12},{9,13},{10,... | collective-permute-start | bytes 393224 | tf_op jit(solution)/shard_map/ppermute | solution.py:52
  74.5 2.3 collective-permute-start.4
  93.2 14.6 %all-to-all-start.3 = ((f32[16,32,256]{2,1,0:T(8,128)}), f32[16,32,256]{2,1,0:T(8,128)S(1)}, u32[]{:S(2)}, u32[]{:S(2)}) async-start(f32[16,32,256]{2,1,0:T(8,128)} %shard_map.63), calls=%async_computation.3 | async-start | bytes 1048576 | tf_op jit(solution)/shard_map/all_to_all | solution.py:97
  108.2 5.4 %collective-permute-start.5 = (f32[256,128]{1,0:T(8,128)S(1)}, f32[256,128]{1,0:T(8,128)S(1)}, u32[]{:S(2)}, u32[]{:S(2)}) collective-permute-start(f32[256,128]{1,0:T(8,128)S(1)} %bitcast.199), channel_id=1, source_target_pairs={{0,1},{1,0},{2,3},{3,2},{4,5},{5,4},{6,7},{7,6},{8,9},{9,8},{10,11... | collective-permute-start | bytes 393224 | tf_op jit(solution)/shard_map/ppermute | solution.py:294
  113.6 5.3 %collective-permute-start.8 = (f32[256,128]{1,0:T(8,128)S(1)}, f32[256,128]{1,0:T(8,128)S(1)}, u32[]{:S(2)}, u32[]{:S(2)}) collective-permute-start(f32[256,128]{1,0:T(8,128)S(1)} %bitcast_add_fusion.6), channel_id=1, source_target_pairs={{0,6},{1,7},{2,0},{3,1},{4,2},{5,3},{6,4},{7,5},{8,14},{9,15},{10,... | collective-permute-start | bytes 393224 | tf_op jit(solution)/shard_map/ppermute | solution.py:52
  113.9 8.9 %collective-permute-start.7 = (f32[256,128]{1,0:T(8,128)S(1)}, f32[256,128]{1,0:T(8,128)S(1)}, u32[]{:S(2)}, u32[]{:S(2)}) collective-permute-start(f32[256,128]{1,0:T(8,128)S(1)} %bitcast_add_fusion.6), channel_id=1, source_target_pairs={{0,2},{1,3},{2,4},{3,5},{4,6},{5,7},{6,0},{7,1},{8,10},{9,11},{10,... | collective-permute-start | bytes 393224 | tf_op jit(solution)/shard_map/ppermute | solution.py:52
  115.2 7.6 %collective-permute-start.6 = (f32[256,128]{1,0:T(8,128)S(1)}, f32[256,128]{1,0:T(8,128)S(1)}, u32[]{:S(2)}, u32[]{:S(2)}) collective-permute-start(f32[256,128]{1,0:T(8,128)S(1)} %bitcast_add_fusion.6), channel_id=1, source_target_pairs={{0,4},{1,5},{2,6},{3,7},{4,0},{5,1},{6,2},{7,3},{8,12},{9,13},{10,... | collective-permute-start | bytes 393224 | tf_op jit(solution)/shard_map/ppermute | solution.py:52
  131.7 7.2 %collective-permute-start.10 = (f32[64,256]{1,0:T(8,128)S(1)}, f32[64,256]{1,0:T(8,128)S(1)}, u32[]{:S(2)}, u32[]{:S(2)}) collective-permute-start(f32[64,256]{1,0:T(8,128)S(1)} %bitcast.170), channel_id=1, source_target_pairs={{0,32},{8,40},{16,48},{24,56},{32,64},{40,72},{48,80},{56,88},{64,... | collective-permute-start | bytes 196616 | tf_op jit(solution)/shard_map/ppermute | solution.py:52
  132.3 6.6 %collective-permute-start.11 = (f32[64,256]{1,0:T(8,128)S(1)}, f32[64,256]{1,0:T(8,128)S(1)}, u32[]{:S(2)}, u32[]{:S(2)}) collective-permute-start(f32[64,256]{1,0:T(8,128)S(1)} %bitcast.171), channel_id=1, source_target_pairs={{0,96},{8,104},{16,112},{24,120},{32,0},{40,8},{48,16},{56,24},{64... | collective-permute-start | bytes 196616 | tf_op jit(solution)/shard_map/ppermute | solution.py:52
  134.4 5.1 %collective-permute-start.9 = (f32[64,256]{1,0:T(8,128)S(1)}, f32[64,256]{1,0:T(8,128)S(1)}, u32[]{:S(2)}, u32[]{:S(2)}) collective-permute-start(f32[64,256]{1,0:T(8,128)S(1)} %bitcast.172), channel_id=1, source_target_pairs={{0,64},{8,72},{16,80},{24,88},{32,96},{40,104},{48,112},{56,120},{... | collective-permute-start | bytes 196616 | tf_op jit(solution)/shard_map/ppermute | solution.py:52
  140.0 4.7 %collective-permute-start.12 = (f32[32,512]{1,0:T(8,128)S(1)}, f32[32,512]{1,0:T(8,128)S(1)}, u32[]{:S(2)}, u32[]{:S(2)}) collective-permute-start(f32[32,512]{1,0:T(8,128)S(1)} %bitcast.205), channel_id=1, source_target_pairs={{0,1},{1,0},{2,3},{3,2},{4,5},{5,4},{6,7},{7,6},{8,9},{9,8},{10,11... | collective-permute-start | bytes 196616 | tf_op jit(solution)/shard_map/ppermute | solution.py:60
  144.7 3.2 collective-permute-start.15
  146.0 4.5 %collective-permute-start.14 = (f32[32,512]{1,0:T(8,128)S(1)}, f32[32,512]{1,0:T(8,128)S(1)}, u32[]{:S(2)}, u32[]{:S(2)}) collective-permute-start(f32[32,512]{1,0:T(8,128)S(1)} %bitcast_add_fusion.5), channel_id=1, source_target_pairs={{0,2},{1,3},{2,4},{3,5},{4,6},{5,7},{6,0},{7,1},{8,10},{9,11},{10,... | collective-permute-start | bytes 196616 | tf_op jit(solution)/shard_map/ppermute | solution.py:52
  146.2 5.1 %collective-permute-start.13 = (f32[32,512]{1,0:T(8,128)S(1)}, f32[32,512]{1,0:T(8,128)S(1)}, u32[]{:S(2)}, u32[]{:S(2)}) collective-permute-start(f32[32,512]{1,0:T(8,128)S(1)} %bitcast_add_fusion.5), channel_id=1, source_target_pairs={{0,4},{1,5},{2,6},{3,7},{4,0},{5,1},{6,2},{7,3},{8,12},{9,13},{10,... | collective-permute-start | bytes 196616 | tf_op jit(solution)/shard_map/ppermute | solution.py:52
  151.6 7.2 %collective-permute-start.17 = (f32[32,256]{1,0:T(8,128)S(1)}, f32[32,256]{1,0:T(8,128)S(1)}, u32[]{:S(2)}, u32[]{:S(2)}) collective-permute-start(f32[32,256]{1,0:T(8,128)S(1)} %bitcast.212), channel_id=1, source_target_pairs={{0,32},{8,40},{16,48},{24,56},{32,64},{40,72},{48,80},{56,88},{64,... | collective-permute-start | bytes 98312 | tf_op jit(solution)/shard_map/ppermute | solution.py:52
  151.6 7.2 %collective-permute-start.18 = (f32[32,256]{1,0:T(8,128)S(1)}, f32[32,256]{1,0:T(8,128)S(1)}, u32[]{:S(2)}, u32[]{:S(2)}) collective-permute-start(f32[32,256]{1,0:T(8,128)S(1)} %bitcast.213), channel_id=1, source_target_pairs={{0,96},{8,104},{16,112},{24,120},{32,0},{40,8},{48,16},{56,24},{64... | collective-permute-start | bytes 98312 | tf_op jit(solution)/shard_map/ppermute | solution.py:52
  154.3 4.5 %collective-permute-start.16 = (f32[32,256]{1,0:T(8,128)S(1)}, f32[32,256]{1,0:T(8,128)S(1)}, u32[]{:S(2)}, u32[]{:S(2)}) collective-permute-start(f32[32,256]{1,0:T(8,128)S(1)} %bitcast.214), channel_id=1, source_target_pairs={{0,64},{8,72},{16,80},{24,88},{32,96},{40,104},{48,112},{56,120},{... | collective-permute-start | bytes 98312 | tf_op jit(solution)/shard_map/ppermute | solution.py:52
  159.4 4.2 %collective-permute-start.19 = (f32[16,512]{1,0:T(8,128)S(1)}, f32[16,512]{1,0:T(8,128)S(1)}, u32[]{:S(2)}, u32[]{:S(2)}) collective-permute-start(f32[16,512]{1,0:T(8,128)S(1)} %fusion.9), channel_id=1, source_target_pairs={{0,1},{1,0},{2,3},{3,2},{4,5},{5,4},{6,7},{7,6},{8,9},{9,8},{10,11... | collective-permute-start | bytes 98312 | tf_op jit(solution)/shard_map/ppermute | solution.py:60
  163.7 65.7 %copy-start.17 = (bf16[4,256,128]{2,1,0:T(8,128)(2,1)S(1)}, bf16[4,256,128]{2,1,0:T(8,128)(2,1)}, u32[]{:S(2)}) copy-start(bf16[4,256,128]{2,1,0:T(8,128)(2,1)} %copy-done.15) | copy-start | bytes 786436
  163.7 3.5 collective-permute-start.22
  165.8 4.0 %collective-permute-start.21 = (f32[16,512]{1,0:T(8,128)S(1)}, f32[16,512]{1,0:T(8,128)S(1)}, u32[]{:S(2)}, u32[]{:S(2)}) collective-permute-start(f32[16,512]{1,0:T(8,128)S(1)} %add.249), channel_id=1, source_target_pairs={{0,2},{1,3},{2,4},{3,5},{4,6},{5,7},{6,0},{7,1},{8,10},{9,11},{10,... | collective-permute-start | bytes 98312 | tf_op jit(solution)/shard_map/ppermute | solution.py:52
  165.9 4.3 %collective-permute-start.20 = (f32[16,512]{1,0:T(8,128)S(1)}, f32[16,512]{1,0:T(8,128)S(1)}, u32[]{:S(2)}, u32[]{:S(2)}) collective-permute-start(f32[16,512]{1,0:T(8,128)S(1)} %add.249), channel_id=1, source_target_pairs={{0,4},{1,5},{2,6},{3,7},{4,0},{5,1},{6,2},{7,3},{8,12},{9,13},{10,... | collective-permute-start | bytes 98312 | tf_op jit(solution)/shard_map/ppermute | solution.py:52
  167.1 66.0 %slice-start.4 = ((s8[6422528]{0:T(1024)(128)(4,1)}), s8[2228224]{0:T(1024)(128)(4,1)S(1)}, s32[]{:S(2)}) async-start(s8[6422528]{0:T(1024)(128)(4,1)} %bitcast.155), calls=%async_computation.15 | async-start | bytes 4456448
  167.2 65.9 %copy-start.28 = (f32[8]{0:T(128)S(1)}, f32[8]{0:T(128)}, u32[]{:S(2)}) copy-start(f32[8]{0:T(128)} %copy-done.27) | copy-start | bytes 100
  170.3 3.8 %collective-permute-start.25 = (f32[16,256]{1,0:T(8,128)S(1)}, f32[16,256]{1,0:T(8,128)S(1)}, u32[]{:S(2)}, u32[]{:S(2)}) collective-permute-start(f32[16,256]{1,0:T(8,128)S(1)} %fusion.27), channel_id=1, source_target_pairs={{0,96},{8,104},{16,112},{24,120},{32,0},{40,8},{48,16},{56,24},{64... | collective-permute-start | bytes 49160 | tf_op jit(solution)/shard_map/ppermute | solution.py:52
  170.8 3.8 %collective-permute-start.24 = (f32[16,256]{1,0:T(8,128)S(1)}, f32[16,256]{1,0:T(8,128)S(1)}, u32[]{:S(2)}, u32[]{:S(2)}) collective-permute-start(f32[16,256]{1,0:T(8,128)S(1)} %fusion.27), channel_id=1, source_target_pairs={{0,32},{8,40},{16,48},{24,56},{32,64},{40,72},{48,80},{56,88},{64,... | collective-permute-start | bytes 49160 | tf_op jit(solution)/shard_map/ppermute | solution.py:52
  171.8 4.1 %collective-permute-start.23 = (f32[16,256]{1,0:T(8,128)S(1)}, f32[16,256]{1,0:T(8,128)S(1)}, u32[]{:S(2)}, u32[]{:S(2)}) collective-permute-start(f32[16,256]{1,0:T(8,128)S(1)} %fusion.27), channel_id=1, source_target_pairs={{0,64},{8,72},{16,80},{24,88},{32,96},{40,104},{48,112},{56,120},{... | collective-permute-start | bytes 49160 | tf_op jit(solution)/shard_map/ppermute | solution.py:52
  176.1 4.4 %collective-permute-start.26 = (f32[16,512]{1,0:T(8,128)S(1)}, f32[16,512]{1,0:T(8,128)S(1)}, u32[]{:S(2)}, u32[]{:S(2)}) collective-permute-start(f32[16,512]{1,0:T(8,128)S(1)} %fusion.25), channel_id=1, source_target_pairs={{0,1},{1,0},{2,3},{3,2},{4,5},{5,4},{6,7},{7,6},{8,9},{9,8},{10,11... | collective-permute-start | bytes 98312 | tf_op jit(solution)/shard_map/ppermute | solution.py:60
  180.4 4.2 %collective-permute-start.29 = (f32[16,512]{1,0:T(8,128)S(1)}, f32[16,512]{1,0:T(8,128)S(1)}, u32[]{:S(2)}, u32[]{:S(2)}) collective-permute-start(f32[16,512]{1,0:T(8,128)S(1)} %add.256), channel_id=1, source_target_pairs={{0,6},{1,7},{2,0},{3,1},{4,2},{5,3},{6,4},{7,5},{8,14},{9,15},{10,... | collective-permute-start | bytes 98312 | tf_op jit(solution)/shard_map/ppermute | solution.py:52
  183.3 4.0 %collective-permute-start.28 = (f32[16,512]{1,0:T(8,128)S(1)}, f32[16,512]{1,0:T(8,128)S(1)}, u32[]{:S(2)}, u32[]{:S(2)}) collective-permute-start(f32[16,512]{1,0:T(8,128)S(1)} %add.256), channel_id=1, source_target_pairs={{0,2},{1,3},{2,4},{3,5},{4,6},{5,7},{6,0},{7,1},{8,10},{9,11},{10,... | collective-permute-start | bytes 98312 | tf_op jit(solution)/shard_map/ppermute | solution.py:52
  183.3 4.3 %collective-permute-start.27 = (f32[16,512]{1,0:T(8,128)S(1)}, f32[16,512]{1,0:T(8,128)S(1)}, u32[]{:S(2)}, u32[]{:S(2)}) collective-permute-start(f32[16,512]{1,0:T(8,128)S(1)} %add.256), channel_id=1, source_target_pairs={{0,4},{1,5},{2,6},{3,7},{4,0},{5,1},{6,2},{7,3},{8,12},{9,13},{10,... | collective-permute-start | bytes 98312 | tf_op jit(solution)/shard_map/ppermute | solution.py:52
  187.9 56.1 %copy-start.9 = (bf16[8,128,256]{2,1,0:T(8,128)(2,1)S(1)}, bf16[8,128,256]{2,1,0:T(8,128)(2,1)}, u32[]{:S(2)}) copy-start(bf16[8,128,256]{2,1,0:T(8,128)(2,1)} %copy-done.7) | copy-start | bytes 1572868
  187.9 4.0 %collective-permute-start.31 = (f32[32,256]{1,0:T(8,128)S(1)}, f32[32,256]{1,0:T(8,128)S(1)}, u32[]{:S(2)}, u32[]{:S(2)}) collective-permute-start(f32[32,256]{1,0:T(8,128)S(1)} %bitcast.215), channel_id=1, source_target_pairs={{0,32},{8,40},{16,48},{24,56},{32,64},{40,72},{48,80},{56,88},{64,... | collective-permute-start | bytes 98312 | tf_op jit(solution)/shard_map/ppermute | solution.py:52
  188.1 3.8 %collective-permute-start.32 = (f32[32,256]{1,0:T(8,128)S(1)}, f32[32,256]{1,0:T(8,128)S(1)}, u32[]{:S(2)}, u32[]{:S(2)}) collective-permute-start(f32[32,256]{1,0:T(8,128)S(1)} %bitcast.216), channel_id=1, source_target_pairs={{0,96},{8,104},{16,112},{24,120},{32,0},{40,8},{48,16},{56,24},{64... | collective-permute-start | bytes 98312 | tf_op jit(solution)/shard_map/ppermute | solution.py:52
  190.6 4.3 %collective-permute-start.30 = (f32[32,256]{1,0:T(8,128)S(1)}, f32[32,256]{1,0:T(8,128)S(1)}, u32[]{:S(2)}, u32[]{:S(2)}) collective-permute-start(f32[32,256]{1,0:T(8,128)S(1)} %bitcast.217), channel_id=1, source_target_pairs={{0,64},{8,72},{16,80},{24,88},{32,96},{40,104},{48,112},{56,120},{... | collective-permute-start | bytes 98312 | tf_op jit(solution)/shard_map/ppermute | solution.py:52
  195.0 4.4 %collective-permute-start.33 = (f32[32,512]{1,0:T(8,128)S(1)}, f32[32,512]{1,0:T(8,128)S(1)}, u32[]{:S(2)}, u32[]{:S(2)}) collective-permute-start(f32[32,512]{1,0:T(8,128)S(1)} %bitcast.206), channel_id=1, source_target_pairs={{0,1},{1,0},{2,3},{3,2},{4,5},{5,4},{6,7},{7,6},{8,9},{9,8},{10,11... | collective-permute-start | bytes 196616 | tf_op jit(solution)/shard_map/ppermute | solution.py:60
  199.4 4.3 %collective-permute-start.36 = (f32[32,512]{1,0:T(8,128)S(1)}, f32[32,512]{1,0:T(8,128)S(1)}, u32[]{:S(2)}, u32[]{:S(2)}) collective-permute-start(f32[32,512]{1,0:T(8,128)S(1)} %bitcast_add_fusion.4), channel_id=1, source_target_pairs={{0,6},{1,7},{2,0},{3,1},{4,2},{5,3},{6,4},{7,5},{8,14},{9,15},{10,... | collective-permute-start | bytes 196616 | tf_op jit(solution)/shard_map/ppermute | solution.py:52
  202.4 6.3 %collective-permute-start.35 = (f32[32,512]{1,0:T(8,128)S(1)}, f32[32,512]{1,0:T(8,128)S(1)}, u32[]{:S(2)}, u32[]{:S(2)}) collective-permute-start(f32[32,512]{1,0:T(8,128)S(1)} %bitcast_add_fusion.4), channel_id=1, source_target_pairs={{0,2},{1,3},{2,4},{3,5},{4,6},{5,7},{6,0},{7,1},{8,10},{9,11},{10,... | collective-permute-start | bytes 196616 | tf_op jit(solution)/shard_map/ppermute | solution.py:52
  202.4 6.3 %collective-permute-start.34 = (f32[32,512]{1,0:T(8,128)S(1)}, f32[32,512]{1,0:T(8,128)S(1)}, u32[]{:S(2)}, u32[]{:S(2)}) collective-permute-start(f32[32,512]{1,0:T(8,128)S(1)} %bitcast_add_fusion.4), channel_id=1, source_target_pairs={{0,4},{1,5},{2,6},{3,7},{4,0},{5,1},{6,2},{7,3},{8,12},{9,13},{10,... | collective-permute-start | bytes 196616 | tf_op jit(solution)/shard_map/ppermute | solution.py:52
  209.3 4.3 %collective-permute-start.38 = (f32[64,256]{1,0:T(8,128)S(1)}, f32[64,256]{1,0:T(8,128)S(1)}, u32[]{:S(2)}, u32[]{:S(2)}) collective-permute-start(f32[64,256]{1,0:T(8,128)S(1)} %bitcast.202), channel_id=1, source_target_pairs={{0,32},{8,40},{16,48},{24,56},{32,64},{40,72},{48,80},{56,88},{64,... | collective-permute-start | bytes 196616 | tf_op jit(solution)/shard_map/ppermute | solution.py:52
  209.3 4.3 %collective-permute-start.39 = (f32[64,256]{1,0:T(8,128)S(1)}, f32[64,256]{1,0:T(8,128)S(1)}, u32[]{:S(2)}, u32[]{:S(2)}) collective-permute-start(f32[64,256]{1,0:T(8,128)S(1)} %bitcast.203), channel_id=1, source_target_pairs={{0,96},{8,104},{16,112},{24,120},{32,0},{40,8},{48,16},{56,24},{64... | collective-permute-start | bytes 196616 | tf_op jit(solution)/shard_map/ppermute | solution.py:52
  212.0 4.6 %collective-permute-start.37 = (f32[64,256]{1,0:T(8,128)S(1)}, f32[64,256]{1,0:T(8,128)S(1)}, u32[]{:S(2)}, u32[]{:S(2)}) collective-permute-start(f32[64,256]{1,0:T(8,128)S(1)} %bitcast.204), channel_id=1, source_target_pairs={{0,64},{8,72},{16,80},{24,88},{32,96},{40,104},{48,112},{56,120},{... | collective-permute-start | bytes 196616 | tf_op jit(solution)/shard_map/ppermute | solution.py:52
  216.6 52.8 %copy-start.19 = (f32[16,32,256]{2,1,0:T(8,128)S(1)}, f32[16,32,256]{2,1,0:T(8,128)}, u32[]{:S(2)}) copy-start(f32[16,32,256]{2,1,0:T(8,128)} %copy-done.18) | copy-start | bytes 1572868
  229.6 4.5 %collective-permute-start.40 = (f32[256,128]{1,0:T(8,128)S(1)}, f32[256,128]{1,0:T(8,128)S(1)}, u32[]{:S(2)}, u32[]{:S(2)}) collective-permute-start(f32[256,128]{1,0:T(8,128)S(1)} %bitcast.168), channel_id=1, source_target_pairs={{0,1},{1,0},{2,3},{3,2},{4,5},{5,4},{6,7},{7,6},{8,9},{9,8},{10,11... | collective-permute-start | bytes 393224 | tf_op jit(solution)/shard_map/ppermute | solution.py:60
  234.1 4.8 %collective-permute-start.43 = (f32[256,128]{1,0:T(8,128)S(1)}, f32[256,128]{1,0:T(8,128)S(1)}, u32[]{:S(2)}, u32[]{:S(2)}) collective-permute-start(f32[256,128]{1,0:T(8,128)S(1)} %bitcast_add_fusion.3), channel_id=1, source_target_pairs={{0,6},{1,7},{2,0},{3,1},{4,2},{5,3},{6,4},{7,5},{8,14},{9,15},{10,... | collective-permute-start | bytes 393224 | tf_op jit(solution)/shard_map/ppermute | solution.py:52
  235.3 8.6 %collective-permute-start.42 = (f32[256,128]{1,0:T(8,128)S(1)}, f32[256,128]{1,0:T(8,128)S(1)}, u32[]{:S(2)}, u32[]{:S(2)}) collective-permute-start(f32[256,128]{1,0:T(8,128)S(1)} %bitcast_add_fusion.3), channel_id=1, source_target_pairs={{0,2},{1,3},{2,4},{3,5},{4,6},{5,7},{6,0},{7,1},{8,10},{9,11},{10,... | collective-permute-start | bytes 393224 | tf_op jit(solution)/shard_map/ppermute | solution.py:52
  235.7 8.2 %collective-permute-start.41 = (f32[256,128]{1,0:T(8,128)S(1)}, f32[256,128]{1,0:T(8,128)S(1)}, u32[]{:S(2)}, u32[]{:S(2)}) collective-permute-start(f32[256,128]{1,0:T(8,128)S(1)} %bitcast_add_fusion.3), channel_id=1, source_target_pairs={{0,4},{1,5},{2,6},{3,7},{4,0},{5,1},{6,2},{7,3},{8,12},{9,13},{10,... | collective-permute-start | bytes 393224 | tf_op jit(solution)/shard_map/ppermute | solution.py:52
  269.8 4.6 %collective-permute-start.44 = (f32[256,128]{1,0:T(8,128)S(1)}, f32[256,128]{1,0:T(8,128)S(1)}, u32[]{:S(2)}, u32[]{:S(2)}) collective-permute-start(f32[256,128]{1,0:T(8,128)S(1)} %dynamic-slice_bitcast_fusion.1), channel_id=1, source_target_pairs={{0,1},{1,0},{2,3},{3,2},{4,5},{5,4},{6,7},{7,6},{8,9},{9,8},{10,11... | collective-permute-start | bytes 393224 | tf_op jit(solution)/shard_map/ppermute | solution.py:66
  274.4 4.8 %collective-permute-start.47 = (f32[256,128]{1,0:T(8,128)S(1)}, f32[256,128]{1,0:T(8,128)S(1)}, u32[]{:S(2)}, u32[]{:S(2)}) collective-permute-start(f32[256,128]{1,0:T(8,128)S(1)} %bitcast_add_fusion.1), channel_id=1, source_target_pairs={{0,6},{1,7},{2,0},{3,1},{4,2},{5,3},{6,4},{7,5},{8,14},{9,15},{10,... | collective-permute-start | bytes 393224 | tf_op jit(solution)/shard_map/ppermute | solution.py:52
  274.5 6.2 %collective-permute-start.46 = (f32[256,128]{1,0:T(8,128)S(1)}, f32[256,128]{1,0:T(8,128)S(1)}, u32[]{:S(2)}, u32[]{:S(2)}) collective-permute-start(f32[256,128]{1,0:T(8,128)S(1)} %bitcast_add_fusion.1), channel_id=1, source_target_pairs={{0,2},{1,3},{2,4},{3,5},{4,6},{5,7},{6,0},{7,1},{8,10},{9,11},{10,... | collective-permute-start | bytes 393224 | tf_op jit(solution)/shard_map/ppermute | solution.py:52
  275.9 6.2 %collective-permute-start.45 = (f32[256,128]{1,0:T(8,128)S(1)}, f32[256,128]{1,0:T(8,128)S(1)}, u32[]{:S(2)}, u32[]{:S(2)}) collective-permute-start(f32[256,128]{1,0:T(8,128)S(1)} %bitcast_add_fusion.1), channel_id=1, source_target_pairs={{0,4},{1,5},{2,6},{3,7},{4,0},{5,1},{6,2},{7,3},{8,12},{9,13},{10,... | collective-permute-start | bytes 393224 | tf_op jit(solution)/shard_map/ppermute | solution.py:52
  282.1 3.4 collective-permute-start.48
  325.0 4.5 %collective-permute-start.49 = (f32[512,128]{1,0:T(8,128)S(1)}, f32[512,128]{1,0:T(8,128)S(1)}, u32[]{:S(2)}, u32[]{:S(2)}) collective-permute-start(f32[512,128]{1,0:T(8,128)S(1)} %dynamic-slice_bitcast_fusion), channel_id=1, source_target_pairs={{0,1},{1,0},{2,3},{3,2},{4,5},{5,4},{6,7},{7,6},{8,9},{9,8},{10,11... | collective-permute-start | bytes 786440 | tf_op jit(solution)/shard_map/ppermute | solution.py:66
  329.6 7.6 %collective-permute-start.52 = (f32[512,128]{1,0:T(8,128)S(1)}, f32[512,128]{1,0:T(8,128)S(1)}, u32[]{:S(2)}, u32[]{:S(2)}) collective-permute-start(f32[512,128]{1,0:T(8,128)S(1)} %bitcast_add_fusion), channel_id=1, source_target_pairs={{0,6},{1,7},{2,0},{3,1},{4,2},{5,3},{6,4},{7,5},{8,14},{9,15},{10,... | collective-permute-start | bytes 786440 | tf_op jit(solution)/shard_map/ppermute | solution.py:52
  330.7 9.0 %collective-permute-start.51 = (f32[512,128]{1,0:T(8,128)S(1)}, f32[512,128]{1,0:T(8,128)S(1)}, u32[]{:S(2)}, u32[]{:S(2)}) collective-permute-start(f32[512,128]{1,0:T(8,128)S(1)} %bitcast_add_fusion), channel_id=1, source_target_pairs={{0,2},{1,3},{2,4},{3,5},{4,6},{5,7},{6,0},{7,1},{8,10},{9,11},{10,... | collective-permute-start | bytes 786440 | tf_op jit(solution)/shard_map/ppermute | solution.py:52
  331.1 13.1 %collective-permute-start.50 = (f32[512,128]{1,0:T(8,128)S(1)}, f32[512,128]{1,0:T(8,128)S(1)}, u32[]{:S(2)}, u32[]{:S(2)}) collective-permute-start(f32[512,128]{1,0:T(8,128)S(1)} %bitcast_add_fusion), channel_id=1, source_target_pairs={{0,4},{1,5},{2,6},{3,7},{4,0},{5,1},{6,2},{7,3},{8,12},{9,13},{10,... | collective-permute-start | bytes 786440 | tf_op jit(solution)/shard_map/ppermute | solution.py:52
  344.2 3.4 collective-permute-start.53
  (33 other events, 531.3 us)
Sparse Core Ops, SparseCore 0:
  34.4 89.9 all-gather.2
